TPU v7x, 32 devices: a whole 2x2x4 slice. The times are simulated.
32 devices in a mesh: ty: 2 (over core), tx: 16 (over z, y, x).
Axes of the slice: x: 2, y: 2, z: 4, core: 2. Of those that a mesh axis runs over, the one named last changes fastest.
Arguments:
- movie: bfloat16 [64, 512, 128], P('ty', 'tx'), may hold values from 0 to 2
- footprints: bfloat16 [2, 16, 32, 1024], P('ty', 'tx'), may hold values from 0.049804688 to 1
- centres: int32 [2, 16, 32, 2], P('ty', 'tx'), may hold values from 0 to 31
- traces: bfloat16 [2, 16, 32, 128], P('ty', 'tx'), may hold values from 0 to 1
- counts: int32 [2, 16], P('ty', 'tx'), may hold values from 8 to 32
- order: int32 [2, 16, 32], P('ty', 'tx'), may hold values from 0 to 31, each once within a row
Outputs:
- new_traces: float32 [2, 16, 32, 128], P('ty', 'tx')
Inputs may be any that keep to these rules, and one draw needn't show every extreme that they name: Slots 0 to counts - 1 of a tile hold neurons; the footprints, centres and traces of the other slots are not used. order[a, b] holds each of 0 to 31 once. `centres`: A centre lies inside its owner tile.
All inputs are finite; a program needn't handle non-finite values.
Results may differ from a plain program's by a relative error of at most 0.0003.
Values may be sent and summed in bfloat16 or wider, within the bound.
No kernel may reach another device: no remote copies, remote signals or barrier semaphores. Data moves between devices by JAX's collectives and lax.ppermute only.
A program may use at most 64 MiB of HBM per device.

v0:
```python
import jax
import jax.numpy as jnp
from jax import lax
from jax.sharding import PartitionSpec as P

BLOCKS = 4
PATCH = 32


precise = lax.Precision.HIGHEST


def extended(x, sides, width):
    for axis, dim in sides:
        devices, length = (lax.axis_size(axis), x.shape[dim])
        up = [(i, (i + 1) % devices) for i in range(devices - 1)]
        down = [(j, i) for i, j in up]
        last = lax.slice_in_dim(x, length - width, length, axis=dim)
        first = lax.slice_in_dim(x, 0, width, axis=dim)
        before = lax.ppermute(last, axis, up)
        after = lax.ppermute(first, axis, down)
        x = jnp.concatenate([before, x, after], axis=dim)
    return x


def placement(anchors, extent, length):
    across = jnp.arange(extent, dtype=jnp.int32)[None, :, None]
    inside = jnp.arange(length, dtype=jnp.int32)[None, None, :]
    return (across == anchors[:, None, None] + inside).astype(jnp.bfloat16)


def paint(patches, top_rows, left_cols, canvas_rows, canvas_cols):
    rows_hot = placement(top_rows, canvas_rows, PATCH)
    cols_hot = placement(left_cols, canvas_cols, PATCH)
    spread = jnp.einsum(
        "kyi,kij->kyj", rows_hot, patches, preferred_element_type=jnp.float32
    ).astype(jnp.bfloat16)
    canvas = jnp.einsum(
        "kyj,kxj->kyx", spread, cols_hot, preferred_element_type=jnp.float32
    ).astype(jnp.bfloat16)
    return canvas.reshape(patches.shape[0], canvas_rows * canvas_cols)


def body(movie, footprints, centres, traces, counts, order):
    tile_side = movie.shape[0]
    frame_count = movie.shape[2]
    slot_count = footprints.shape[2]
    half_patch = PATCH // 2
    block_rows = slot_count // BLOCKS
    ordering = order[0, 0]
    alive_mask = ordering < counts[0, 0]
    selector = ordering[:, None] == jnp.arange(slot_count, dtype=jnp.int32)[None, :]
    chooser = (selector & alive_mask[:, None]).astype(jnp.bfloat16)
    own_flat = jnp.dot(chooser, footprints[0, 0], preferred_element_type=jnp.float32).astype(
        jnp.bfloat16
    )
    first_traces = jnp.dot(chooser, traces[0, 0], preferred_element_type=jnp.float32).astype(
        jnp.bfloat16
    )
    picker = selector.astype(jnp.int32)
    own_pos = jnp.sum(picker[:, :, None] * centres[0, 0][None, :, :], axis=1)
    near_flat, near_pos, near_traces = (
        extended(own_flat[None, None], (("ty", 0), ("tx", 1)), 1),
        extended(own_pos.astype(jnp.bfloat16)[None, None], (("ty", 0), ("tx", 1)), 1),
        extended(first_traces[None, None], (("ty", 0), ("tx", 1)), 1),
    )
    offsets = (jnp.arange(3, dtype=jnp.int32) - 1) * tile_side
    near_rows = (near_pos[..., 0].astype(jnp.int32) + offsets[:, None, None]).reshape(
        9 * slot_count
    )
    near_cols = (near_pos[..., 1].astype(jnp.int32) + offsets[None, :, None]).reshape(
        9 * slot_count
    )
    own_rows = own_pos[:, 0]
    own_cols = own_pos[:, 1]
    own_patch = own_flat.reshape(slot_count, PATCH, PATCH)
    near_patch = near_flat.reshape(9 * slot_count, PATCH, PATCH)
    canvas_side = tile_side + 2 * half_patch
    own_canvas = paint(own_patch, own_rows, own_cols, canvas_side, canvas_side)
    near_canvas = paint(near_patch, near_rows, near_cols, canvas_side, canvas_side)
    margins = lax.dot_general(
        own_canvas, near_canvas, (((1,), (1,)), ((), ())), preferred_element_type=jnp.float32
    )
    by_source = margins.reshape(slot_count, 9, slot_count)
    padded_movie = extended(movie, (("ty", 0), ("tx", 1)), half_patch)
    drive_term = jnp.dot(
        own_canvas,
        padded_movie.reshape(canvas_side * canvas_side, frame_count),
        preferred_element_type=jnp.float32,
    )
    current = first_traces.astype(jnp.float32)
    coupling = jnp.dot(
        margins,
        near_traces.reshape(9 * slot_count, frame_count).astype(jnp.float32),
        precision=precise,
        preferred_element_type=jnp.float32,
    )
    diagonal = jnp.diagonal(by_source[:, 4])
    denominator = jnp.where(alive_mask, diagonal, 1.0)
    for block_index in range(BLOCKS):
        lower = block_index * block_rows
        upper = lower + block_rows
        previous = current[lower:upper]
        renewed = jnp.maximum(
            previous
            + (drive_term[lower:upper] - coupling[lower:upper]) / denominator[lower:upper, None],
            0.0,
        )
        renewed = jnp.where(alive_mask[lower:upper, None], renewed, 0.0)
        current = current.at[lower:upper].set(renewed)
        if block_index + 1 < BLOCKS:
            change = extended((renewed - previous)[None, None], (("ty", 0), ("tx", 1)), 1)
            columns = by_source[:, :, lower:upper].reshape(slot_count, 9 * block_rows)
            coupling = coupling + jnp.dot(
                columns,
                change.reshape(9 * block_rows, frame_count),
                precision=precise,
                preferred_element_type=jnp.float32,
            )
    result = lax.dot_general(
        selector.astype(jnp.float32),
        current,
        (((0,), (0,)), ((), ())),
        precision=precise,
        preferred_element_type=jnp.float32,
    )
    return result[None, None]


def solution(mesh):
    in_specs = (
        P("ty", "tx", None),
        P("ty", "tx", None, None),
        P("ty", "tx", None, None),
        P("ty", "tx", None, None),
        P("ty", "tx"),
        P("ty", "tx", None),
    )
    out_specs = P("ty", "tx", None, None)
    return jax.shard_map(body, mesh=mesh, in_specs=in_specs, out_specs=out_specs, check_vma=False)
```

profile of v0, /device:TPU:0, one launch (start us, length us, event | category | flops | bytes accessed | tf_op | source)
XLA Modules:
  0.0 127.6 jit_solution(13149936400083150239)
XLA Ops:
  1.4 0.9 convolution_convert_fusion.2
  2.2 2.4 %collective-permute-start.8 = (bf16[1,1,32,1024]{3,2,1,0:T(8,128)(2,1)S(1)}, bf16[1,1,32,1024]{3,2,1,0:T(8,128)(2,1)S(1)}, u32[]{:S(2)}, u32[]{:S(2)}) collective-permute-start(bf16[1,1,32,1024]{3,2,1,0:T(8,128)(2,1)S(1)} %bitcast.65), channel_id=1, source_target_pairs={{0,16},{1,17},{2,18},{3,19},{4,20},{5,21},{6,22},{7,23},{8,24},{9,... | collective-permute-start | bytes 196616 | tf_op jit(solution)/shard_map/ppermute | solution.py:20
  4.6 1.3 %collective-permute-start.9 = (bf16[1,1,32,1024]{3,2,1,0:T(8,128)(2,1)S(1)}, bf16[1,1,32,1024]{3,2,1,0:T(8,128)(2,1)S(1)}, u32[]{:S(2)}, u32[]{:S(2)}) collective-permute-start(bf16[1,1,32,1024]{3,2,1,0:T(8,128)(2,1)S(1)} %bitcast.66), channel_id=1, source_target_pairs={{16,0},{17,1},{18,2},{19,3},{20,4},{21,5},{22,6},{23,7},{24,8},{25... | collective-permute-start | bytes 196616 | tf_op jit(solution)/shard_map/ppermute | solution.py:21
  6.6 0.8 multiply_reduce_fusion
  7.4 3.0 %collective-permute-start.4 = (bf16[1,1,32,2]{2,3,1,0:T(2,128)(2,1)S(1)}, bf16[1,1,32,2]{2,3,1,0:T(2,128)(2,1)S(1)}, u32[]{:S(2)}, u32[]{:S(2)}) collective-permute-start(bf16[1,1,32,2]{2,3,1,0:T(2,128)(2,1)S(1)} %convert_bitcast_fusion), channel_id=1, source_target_pairs={{0,16},{1,17},{2,18},{3,19},{4,20},{5,21},{6,22},{7,23},{8,24},{9,... | collective-permute-start | bytes 392 | tf_op jit(solution)/shard_map/ppermute | solution.py:20
  10.5 1.3 %collective-permute-start.5 = (bf16[1,1,32,2]{2,3,1,0:T(2,128)(2,1)S(1)}, bf16[1,1,32,2]{2,3,1,0:T(2,128)(2,1)S(1)}, u32[]{:S(2)}, u32[]{:S(2)}) collective-permute-start(bf16[1,1,32,2]{2,3,1,0:T(2,128)(2,1)S(1)} %convert_bitcast_fusion), channel_id=1, source_target_pairs={{16,0},{17,1},{18,2},{19,3},{20,4},{21,5},{22,6},{23,7},{24,8},{25... | collective-permute-start | bytes 392 | tf_op jit(solution)/shard_map/ppermute | solution.py:21
  11.8 1.5 %fusion.61 = (f32[32,128]{1,0:T(8,128)}, bf16[32,128]{1,0:T(8,128)(2,1)S(1)}) fusion(bf16[1,1,32,128]{3,2,1,0:T(8,128)(2,1)} %param.17, s32[32]{0:T(128)} %bitcast.83, pred[32]{0:T(512)(128)(4,1)S(1)} %broadcast_compare_fusion), kind=kOutput, calls=%fused_computation.108 | convolution fusion | flops 272384 | bytes 32928 | tf_op jit(solution)/shard_map/dot_general | solution.py:57
  13.3 3.0 %collective-permute-start.12 = (bf16[1,1,32,128]{3,2,1,0:T(8,128)(2,1)S(1)}, bf16[1,1,32,128]{3,2,1,0:T(8,128)(2,1)S(1)}, u32[]{:S(2)}, u32[]{:S(2)}) collective-permute-start(bf16[1,1,32,128]{3,2,1,0:T(8,128)(2,1)S(1)} %bitcast.77), channel_id=1, source_target_pairs={{0,16},{1,17},{2,18},{3,19},{4,20},{5,21},{6,22},{7,23},{8,24},{9,... | collective-permute-start | bytes 24584 | tf_op jit(solution)/shard_map/ppermute | solution.py:20
  17.0 1.0 fusion.58
  18.1 1.8 %convolution_convert_fusion = bf16[32,64,64]{2,1,0:T(8,128)(2,1)} fusion(bf16[32,32,32]{2,1,0:T(8,128)(2,1)S(1)} %reshape.303, s32[32,32]{1,0:T(8,128)S(1)} %get-tuple-element.77, s32[32,32]{1,0:T(8,128)S(1)} %get-tuple-element.78), kind=kOutput, calls=%fused_computation.10 | convolution fusion | flops 12910592 | bytes 335872 | tf_op jit(solution)/shard_map/kyj,kxj->kyx/dot_general | solution.py:38
  19.9 4.2 %collective-permute-start.6 = (bf16[3,1,32,2]{2,3,1,0:T(2,128)(2,1)S(1)}, bf16[3,1,32,2]{2,3,1,0:T(2,128)(2,1)S(1)}, u32[]{:S(2)}, u32[]{:S(2)}) collective-permute-start(bf16[3,1,32,2]{2,3,1,0:T(2,128)(2,1)S(1)} %pad_maximum_fusion.11), channel_id=1, source_target_pairs={{0,1},{1,2},{2,3},{3,4},{4,5},{5,6},{6,7},{7,8},{8,9},{9,10},{10,1... | collective-permute-start | bytes 1160 | tf_op jit(solution)/shard_map/ppermute | solution.py:20
  24.2 1.3 %collective-permute-start.7 = (bf16[3,1,32,2]{2,3,1,0:T(2,128)(2,1)S(1)}, bf16[3,1,32,2]{2,3,1,0:T(2,128)(2,1)S(1)}, u32[]{:S(2)}, u32[]{:S(2)}) collective-permute-start(bf16[3,1,32,2]{2,3,1,0:T(2,128)(2,1)S(1)} %pad_maximum_fusion.11), channel_id=1, source_target_pairs={{1,0},{2,1},{3,2},{4,3},{5,4},{6,5},{7,6},{8,7},{9,8},{10,9},{11,1... | collective-permute-start | bytes 1160 | tf_op jit(solution)/shard_map/ppermute | solution.py:21
  25.8 1.3 %collective-permute-start.13 = (bf16[1,1,32,128]{3,2,1,0:T(8,128)(2,1)S(1)}, bf16[1,1,32,128]{3,2,1,0:T(8,128)(2,1)S(1)}, u32[]{:S(2)}, u32[]{:S(2)}) collective-permute-start(bf16[1,1,32,128]{3,2,1,0:T(8,128)(2,1)S(1)} %bitcast.78), channel_id=1, source_target_pairs={{16,0},{17,1},{18,2},{19,3},{20,4},{21,5},{22,6},{23,7},{24,8},{25... | collective-permute-start | bytes 24584 | tf_op jit(solution)/shard_map/ppermute | solution.py:21
  27.1 2.5 %collective-permute-done.7 = bf16[3,1,32,2]{2,3,1,0:T(2,128)(2,1)S(1)} collective-permute-done((bf16[3,1,32,2]{2,3,1,0:T(2,128)(2,1)S(1)}, bf16[3,1,32,2]{2,3,1,0:T(2,128)(2,1)S(1)}, u32[]{:S(2)}, u32[]{:S(2)}) %collective-permute-start.7) | collective-permute-done | bytes 416 | tf_op jit(solution)/shard_map/ppermute | solution.py:21
  29.6 1.3 %collective-permute-start = (bf16[16,32,128]{2,1,0:T(8,128)(2,1)S(1)}, bf16[16,32,128]{2,1,0:T(8,128)(2,1)S(1)}, u32[]{:S(2)}, u32[]{:S(2)}) collective-permute-start(bf16[16,32,128]{2,1,0:T(8,128)(2,1)S(1)} %get-tuple-element.64), channel_id=1, source_target_pairs={{0,16},{1,17},{2,18},{3,19},{4,20},{5,21},{6,22},{7,23},{8,24},{9,... | collective-permute-start | bytes 393224 | tf_op jit(solution)/shard_map/ppermute | solution.py:20
  31.6 4.3 %collective-permute-start.14 = (bf16[3,1,32,128]{3,2,1,0:T(8,128)(2,1)S(1)}, bf16[3,1,32,128]{3,2,1,0:T(8,128)(2,1)S(1)}, u32[]{:S(2)}, u32[]{:S(2)}) collective-permute-start(bf16[3,1,32,128]{3,2,1,0:T(8,128)(2,1)S(1)} %pad_maximum_fusion.6), channel_id=1, source_target_pairs={{0,1},{1,2},{2,3},{3,4},{4,5},{5,6},{6,7},{7,8},{8,9},{9,10},{10,1... | collective-permute-start | bytes 73736 | tf_op jit(solution)/shard_map/ppermute | solution.py:20
  35.9 1.3 %collective-permute-start.15 = (bf16[3,1,32,128]{3,2,1,0:T(8,128)(2,1)S(1)}, bf16[3,1,32,128]{3,2,1,0:T(8,128)(2,1)S(1)}, u32[]{:S(2)}, u32[]{:S(2)}) collective-permute-start(bf16[3,1,32,128]{3,2,1,0:T(8,128)(2,1)S(1)} %pad_maximum_fusion.6), channel_id=1, source_target_pairs={{1,0},{2,1},{3,2},{4,3},{5,4},{6,5},{7,6},{8,7},{9,8},{10,9},{11,1... | collective-permute-start | bytes 73736 | tf_op jit(solution)/shard_map/ppermute | solution.py:21
  38.0 6.4 %copy.17 = pred[288,64,32]{1,2,0:T(32,128)(4,1)} copy(pred[288,64,32]{0,2,1:T(32,128)(4,1)S(1)} %iota_compare_fusion.2) | data formatting | bytes 1179648 | tf_op jit(solution)/shard_map/eq | solution.py:29
  44.4 1.3 %collective-permute-start.1 = (bf16[16,32,128]{2,1,0:T(8,128)(2,1)S(1)}, bf16[16,32,128]{2,1,0:T(8,128)(2,1)S(1)}, u32[]{:S(2)}, u32[]{:S(2)}) collective-permute-start(bf16[16,32,128]{2,1,0:T(8,128)(2,1)S(1)} %get-tuple-element.63), channel_id=1, source_target_pairs={{16,0},{17,1},{18,2},{19,3},{20,4},{21,5},{22,6},{23,7},{24,8},{25... | collective-permute-start | bytes 393224 | tf_op jit(solution)/shard_map/ppermute | solution.py:21
  46.4 4.6 %collective-permute-start.10 = (bf16[3,1,32,1024]{3,2,1,0:T(8,128)(2,1)S(1)}, bf16[3,1,32,1024]{3,2,1,0:T(8,128)(2,1)S(1)}, u32[]{:S(2)}, u32[]{:S(2)}) collective-permute-start(bf16[3,1,32,1024]{3,2,1,0:T(8,128)(2,1)S(1)} %pad_maximum_fusion.1), channel_id=1, source_target_pairs={{0,1},{1,2},{2,3},{3,4},{4,5},{5,6},{6,7},{7,8},{8,9},{9,10},{10,1... | collective-permute-start | bytes 589832 | tf_op jit(solution)/shard_map/ppermute | solution.py:20
  51.0 1.3 %collective-permute-start.11 = (bf16[3,1,32,1024]{3,2,1,0:T(8,128)(2,1)S(1)}, bf16[3,1,32,1024]{3,2,1,0:T(8,128)(2,1)S(1)}, u32[]{:S(2)}, u32[]{:S(2)}) collective-permute-start(bf16[3,1,32,1024]{3,2,1,0:T(8,128)(2,1)S(1)} %pad_maximum_fusion.1), channel_id=1, source_target_pairs={{1,0},{2,1},{3,2},{4,3},{5,4},{6,5},{7,6},{8,7},{9,8},{10,9},{11,1... | collective-permute-start | bytes 589832 | tf_op jit(solution)/shard_map/ppermute | solution.py:21
  52.4 0.8 fusion.57
  53.2 6.0 %collective-permute-start.2 = (bf16[64,16,128]{2,1,0:T(8,128)(2,1)}, bf16[64,16,128]{2,1,0:T(8,128)(2,1)}, u32[]{:S(2)}, u32[]{:S(2)}) collective-permute-start(bf16[64,16,128]{2,1,0:T(8,128)(2,1)} %get-tuple-element.61), channel_id=1, source_target_pairs={{0,1},{1,2},{2,3},{3,4},{4,5},{5,6},{6,7},{7,8},{8,9},{9,10},{10,1... | collective-permute-start | bytes 786440 | tf_op jit(solution)/shard_map/ppermute | solution.py:20
  59.2 1.5 %collective-permute-start.3 = (bf16[64,16,128]{2,1,0:T(8,128)(2,1)}, bf16[64,16,128]{2,1,0:T(8,128)(2,1)}, u32[]{:S(2)}, u32[]{:S(2)}) collective-permute-start(bf16[64,16,128]{2,1,0:T(8,128)(2,1)} %get-tuple-element.62), channel_id=1, source_target_pairs={{1,0},{2,1},{3,2},{4,3},{5,4},{6,5},{7,6},{8,7},{9,8},{10,9},{11,1... | collective-permute-start | bytes 786440 | tf_op jit(solution)/shard_map/ppermute | solution.py:21
  60.7 2.8 %collective-permute-done.11 = bf16[3,1,32,1024]{3,2,1,0:T(8,128)(2,1)S(1)} collective-permute-done((bf16[3,1,32,1024]{3,2,1,0:T(8,128)(2,1)S(1)}, bf16[3,1,32,1024]{3,2,1,0:T(8,128)(2,1)S(1)}, u32[]{:S(2)}, u32[]{:S(2)}) %collective-permute-start.11) | collective-permute-done | bytes 196640 | tf_op jit(solution)/shard_map/ppermute | solution.py:21
  63.6 1.8 %reshape.304 = bf16[288,32,32]{2,1,0:T(8,128)(2,1)S(1)} reshape(bf16[3,3,32,1024]{3,2,1,0:T(8,128)(2,1)S(1)} %pad_maximum_fusion) | data formatting | bytes 1179648 | tf_op jit(solution)/shard_map/reshape | solution.py:77
  65.4 6.5 %fusion.3 = bf16[288,64,64]{2,1,0:T(8,128)(2,1)} fusion(s32[288,32]{1,0:T(8,128)} %iota_add_fusion, pred[288,64,32]{1,2,0:T(32,128)(4,1)} %copy.17, bf16[288,32,32]{2,1,0:T(8,128)(2,1)S(1)} %reshape.304), kind=kOutput, calls=%fused_computation.6 | convolution fusion | flops 115605504 | bytes 3575808 | tf_op jit(solution)/shard_map/kyj,kxj->kyx/dot_general | solution.py:38
  71.9 5.2 %fusion.8 = f32[32,288]{1,0:T(8,128)S(1)} fusion(bf16[288,64,64]{2,1,0:T(8,128)(2,1)} %fusion.3, bf16[32,64,64]{2,1,0:T(8,128)(2,1)S(1)} %copy-done.6), kind=kOutput, calls=%fused_computation.13 | convolution fusion | flops 75497472 | bytes 2658304 | tf_op jit(solution)/shard_map/dot_general | solution.py:81
  78.4 1.8 %convolution_bitcast_fusion = f32[32,128]{1,0:T(8,128)S(1)} fusion(bf16[64,16,128]{2,1,0:T(8,128)(2,1)} %collective-permute-done.3, bf16[64,32,128]{2,1,0:T(8,128)(2,1)S(1)} %constant_dynamic-update-slice_fusion, bf16[64,16,128]{2,1,0:T(8,128)(2,1)} %collective-permute-done.2, bf16[32,64,64]{2,1,0:T(8,128)(2,1)S(1)} %copy-done.6), kind=kOutput, calls=%fused_computation.14 | convolution fusion | flops 36700160 | bytes 1327104 | tf_op jit(solution)/shard_map/dot_general | solution.py:86
  80.3 2.0 %collective-permute-start.16 = (f32[1,1,8,128]{3,2,1,0:T(8,128)S(1)}, f32[1,1,8,128]{3,2,1,0:T(8,128)S(1)}, u32[]{:S(2)}, u32[]{:S(2)}) collective-permute-start(f32[1,1,8,128]{3,2,1,0:T(8,128)S(1)} %get-tuple-element.59), channel_id=1, source_target_pairs={{0,16},{1,17},{2,18},{3,19},{4,20},{5,21},{6,22},{7,23},{8,24},{9,... | collective-permute-start | bytes 12296 | tf_op jit(solution)/shard_map/ppermute | solution.py:20
  82.3 1.3 %collective-permute-start.17 = (f32[1,1,8,128]{3,2,1,0:T(8,128)S(1)}, f32[1,1,8,128]{3,2,1,0:T(8,128)S(1)}, u32[]{:S(2)}, u32[]{:S(2)}) collective-permute-start(f32[1,1,8,128]{3,2,1,0:T(8,128)S(1)} %get-tuple-element.59), channel_id=1, source_target_pairs={{16,0},{17,1},{18,2},{19,3},{20,4},{21,5},{22,6},{23,7},{24,8},{25... | collective-permute-start | bytes 12296 | tf_op jit(solution)/shard_map/ppermute | solution.py:21
  83.6 1.8 %collective-permute-done.17 = f32[1,1,8,128]{3,2,1,0:T(8,128)S(1)} collective-permute-done((f32[1,1,8,128]{3,2,1,0:T(8,128)S(1)}, f32[1,1,8,128]{3,2,1,0:T(8,128)S(1)}, u32[]{:S(2)}, u32[]{:S(2)}) %collective-permute-start.17) | collective-permute-done | bytes 4128 | tf_op jit(solution)/shard_map/ppermute | solution.py:21
  85.4 3.0 %collective-permute-start.18 = (f32[3,1,8,128]{3,2,1,0:T(8,128)S(1)}, f32[3,1,8,128]{3,2,1,0:T(8,128)S(1)}, u32[]{:S(2)}, u32[]{:S(2)}) collective-permute-start(f32[3,1,8,128]{3,2,1,0:T(8,128)S(1)} %pad_maximum_fusion.7), channel_id=1, source_target_pairs={{0,1},{1,2},{2,3},{3,4},{4,5},{5,6},{6,7},{7,8},{8,9},{9,10},{10,1... | collective-permute-start | bytes 36872 | tf_op jit(solution)/shard_map/ppermute | solution.py:20
  88.4 1.3 %collective-permute-start.19 = (f32[3,1,8,128]{3,2,1,0:T(8,128)S(1)}, f32[3,1,8,128]{3,2,1,0:T(8,128)S(1)}, u32[]{:S(2)}, u32[]{:S(2)}) collective-permute-start(f32[3,1,8,128]{3,2,1,0:T(8,128)S(1)} %pad_maximum_fusion.7), channel_id=1, source_target_pairs={{1,0},{2,1},{3,2},{4,3},{5,4},{6,5},{7,6},{8,7},{9,8},{10,9},{11,1... | collective-permute-start | bytes 36872 | tf_op jit(solution)/shard_map/ppermute | solution.py:21
  89.8 4.2 %collective-permute-done.19 = f32[3,1,8,128]{3,2,1,0:T(8,128)S(1)} collective-permute-done((f32[3,1,8,128]{3,2,1,0:T(8,128)S(1)}, f32[3,1,8,128]{3,2,1,0:T(8,128)S(1)}, u32[]{:S(2)}, u32[]{:S(2)}) %collective-permute-start.19) | collective-permute-done | bytes 12320 | tf_op jit(solution)/shard_map/ppermute | solution.py:21
  94.3 1.3 %collective-permute-start.20 = (f32[1,1,8,128]{3,2,1,0:T(8,128)S(1)}, f32[1,1,8,128]{3,2,1,0:T(8,128)S(1)}, u32[]{:S(2)}, u32[]{:S(2)}) collective-permute-start(f32[1,1,8,128]{3,2,1,0:T(8,128)S(1)} %get-tuple-element.57), channel_id=1, source_target_pairs={{0,16},{1,17},{2,18},{3,19},{4,20},{5,21},{6,22},{7,23},{8,24},{9,... | collective-permute-start | bytes 12296 | tf_op jit(solution)/shard_map/ppermute | solution.py:20
  95.6 1.3 %collective-permute-start.21 = (f32[1,1,8,128]{3,2,1,0:T(8,128)S(1)}, f32[1,1,8,128]{3,2,1,0:T(8,128)S(1)}, u32[]{:S(2)}, u32[]{:S(2)}) collective-permute-start(f32[1,1,8,128]{3,2,1,0:T(8,128)S(1)} %get-tuple-element.57), channel_id=1, source_target_pairs={{16,0},{17,1},{18,2},{19,3},{20,4},{21,5},{22,6},{23,7},{24,8},{25... | collective-permute-start | bytes 12296 | tf_op jit(solution)/shard_map/ppermute | solution.py:21
  96.9 1.8 %collective-permute-done.21 = f32[1,1,8,128]{3,2,1,0:T(8,128)S(1)} collective-permute-done((f32[1,1,8,128]{3,2,1,0:T(8,128)S(1)}, f32[1,1,8,128]{3,2,1,0:T(8,128)S(1)}, u32[]{:S(2)}, u32[]{:S(2)}) %collective-permute-start.21) | collective-permute-done | bytes 4128 | tf_op jit(solution)/shard_map/ppermute | solution.py:21
  98.7 5.0 %collective-permute-start.22 = (f32[3,1,8,128]{3,2,1,0:T(8,128)S(1)}, f32[3,1,8,128]{3,2,1,0:T(8,128)S(1)}, u32[]{:S(2)}, u32[]{:S(2)}) collective-permute-start(f32[3,1,8,128]{3,2,1,0:T(8,128)S(1)} %pad_maximum_fusion.8), channel_id=1, source_target_pairs={{0,1},{1,2},{2,3},{3,4},{4,5},{5,6},{6,7},{7,8},{8,9},{9,10},{10,1... | collective-permute-start | bytes 36872 | tf_op jit(solution)/shard_map/ppermute | solution.py:20
  103.7 1.3 %collective-permute-start.23 = (f32[3,1,8,128]{3,2,1,0:T(8,128)S(1)}, f32[3,1,8,128]{3,2,1,0:T(8,128)S(1)}, u32[]{:S(2)}, u32[]{:S(2)}) collective-permute-start(f32[3,1,8,128]{3,2,1,0:T(8,128)S(1)} %pad_maximum_fusion.8), channel_id=1, source_target_pairs={{1,0},{2,1},{3,2},{4,3},{5,4},{6,5},{7,6},{8,7},{9,8},{10,9},{11,1... | collective-permute-start | bytes 36872 | tf_op jit(solution)/shard_map/ppermute | solution.py:21
  105.1 5.3 %collective-permute-done.23 = f32[3,1,8,128]{3,2,1,0:T(8,128)S(1)} collective-permute-done((f32[3,1,8,128]{3,2,1,0:T(8,128)S(1)}, f32[3,1,8,128]{3,2,1,0:T(8,128)S(1)}, u32[]{:S(2)}, u32[]{:S(2)}) %collective-permute-start.23) | collective-permute-done | bytes 12320 | tf_op jit(solution)/shard_map/ppermute | solution.py:21
  110.7 1.3 %collective-permute-start.24 = (f32[1,1,8,128]{3,2,1,0:T(8,128)S(1)}, f32[1,1,8,128]{3,2,1,0:T(8,128)S(1)}, u32[]{:S(2)}, u32[]{:S(2)}) collective-permute-start(f32[1,1,8,128]{3,2,1,0:T(8,128)S(1)} %get-tuple-element.55), channel_id=1, source_target_pairs={{0,16},{1,17},{2,18},{3,19},{4,20},{5,21},{6,22},{7,23},{8,24},{9,... | collective-permute-start | bytes 12296 | tf_op jit(solution)/shard_map/ppermute | solution.py:20
  112.0 1.3 %collective-permute-start.25 = (f32[1,1,8,128]{3,2,1,0:T(8,128)S(1)}, f32[1,1,8,128]{3,2,1,0:T(8,128)S(1)}, u32[]{:S(2)}, u32[]{:S(2)}) collective-permute-start(f32[1,1,8,128]{3,2,1,0:T(8,128)S(1)} %get-tuple-element.55), channel_id=1, source_target_pairs={{16,0},{17,1},{18,2},{19,3},{20,4},{21,5},{22,6},{23,7},{24,8},{25... | collective-permute-start | bytes 12296 | tf_op jit(solution)/shard_map/ppermute | solution.py:21
  113.3 1.8 %collective-permute-done.25 = f32[1,1,8,128]{3,2,1,0:T(8,128)S(1)} collective-permute-done((f32[1,1,8,128]{3,2,1,0:T(8,128)S(1)}, f32[1,1,8,128]{3,2,1,0:T(8,128)S(1)}, u32[]{:S(2)}, u32[]{:S(2)}) %collective-permute-start.25) | collective-permute-done | bytes 4128 | tf_op jit(solution)/shard_map/ppermute | solution.py:21
  115.1 5.7 %collective-permute-start.26 = (f32[3,1,8,128]{3,2,1,0:T(8,128)S(1)}, f32[3,1,8,128]{3,2,1,0:T(8,128)S(1)}, u32[]{:S(2)}, u32[]{:S(2)}) collective-permute-start(f32[3,1,8,128]{3,2,1,0:T(8,128)S(1)} %pad_maximum_fusion.9), channel_id=1, source_target_pairs={{0,1},{1,2},{2,3},{3,4},{4,5},{5,6},{6,7},{7,8},{8,9},{9,10},{10,1... | collective-permute-start | bytes 36872 | tf_op jit(solution)/shard_map/ppermute | solution.py:20
  120.8 1.3 %collective-permute-start.27 = (f32[3,1,8,128]{3,2,1,0:T(8,128)S(1)}, f32[3,1,8,128]{3,2,1,0:T(8,128)S(1)}, u32[]{:S(2)}, u32[]{:S(2)}) collective-permute-start(f32[3,1,8,128]{3,2,1,0:T(8,128)S(1)} %pad_maximum_fusion.9), channel_id=1, source_target_pairs={{1,0},{2,1},{3,2},{4,3},{5,4},{6,5},{7,6},{8,7},{9,8},{10,9},{11,1... | collective-permute-start | bytes 36872 | tf_op jit(solution)/shard_map/ppermute | solution.py:21
  122.2 4.2 %collective-permute-done.27 = f32[3,1,8,128]{3,2,1,0:T(8,128)S(1)} collective-permute-done((f32[3,1,8,128]{3,2,1,0:T(8,128)S(1)}, f32[3,1,8,128]{3,2,1,0:T(8,128)S(1)}, u32[]{:S(2)}, u32[]{:S(2)}) %collective-permute-start.27) | collective-permute-done | bytes 12320 | tf_op jit(solution)/shard_map/ppermute | solution.py:21
  126.7 0.9 convolution_bitcast_fusion.1
  (87 shorter events, 7.2 us)
Async XLA Ops:
  0.0 1.4 %copy-start = (bf16[1,1,32,1024]{3,2,1,0:T(8,128)(2,1)S(1)}, bf16[1,1,32,1024]{3,2,1,0:T(8,128)(2,1)}, u32[]{:S(2)}) copy-start(bf16[1,1,32,1024]{3,2,1,0:T(8,128)(2,1)} %param.15) | copy-start | bytes 196612
  2.2 44.2 %collective-permute-start.8 = (bf16[1,1,32,1024]{3,2,1,0:T(8,128)(2,1)S(1)}, bf16[1,1,32,1024]{3,2,1,0:T(8,128)(2,1)S(1)}, u32[]{:S(2)}, u32[]{:S(2)}) collective-permute-start(bf16[1,1,32,1024]{3,2,1,0:T(8,128)(2,1)S(1)} %bitcast.65), channel_id=1, source_target_pairs={{0,16},{1,17},{2,18},{3,19},{4,20},{5,21},{6,22},{7,23},{8,24},{9,... | collective-permute-start | bytes 196616 | tf_op jit(solution)/shard_map/ppermute | solution.py:20
  4.6 41.8 %collective-permute-start.9 = (bf16[1,1,32,1024]{3,2,1,0:T(8,128)(2,1)S(1)}, bf16[1,1,32,1024]{3,2,1,0:T(8,128)(2,1)S(1)}, u32[]{:S(2)}, u32[]{:S(2)}) collective-permute-start(bf16[1,1,32,1024]{3,2,1,0:T(8,128)(2,1)S(1)} %bitcast.66), channel_id=1, source_target_pairs={{16,0},{17,1},{18,2},{19,3},{20,4},{21,5},{22,6},{23,7},{24,8},{25... | collective-permute-start | bytes 196616 | tf_op jit(solution)/shard_map/ppermute | solution.py:21
  7.4 12.5 %collective-permute-start.4 = (bf16[1,1,32,2]{2,3,1,0:T(2,128)(2,1)S(1)}, bf16[1,1,32,2]{2,3,1,0:T(2,128)(2,1)S(1)}, u32[]{:S(2)}, u32[]{:S(2)}) collective-permute-start(bf16[1,1,32,2]{2,3,1,0:T(2,128)(2,1)S(1)} %convert_bitcast_fusion), channel_id=1, source_target_pairs={{0,16},{1,17},{2,18},{3,19},{4,20},{5,21},{6,22},{7,23},{8,24},{9,... | collective-permute-start | bytes 392 | tf_op jit(solution)/shard_map/ppermute | solution.py:20
  10.5 9.4 %collective-permute-start.5 = (bf16[1,1,32,2]{2,3,1,0:T(2,128)(2,1)S(1)}, bf16[1,1,32,2]{2,3,1,0:T(2,128)(2,1)S(1)}, u32[]{:S(2)}, u32[]{:S(2)}) collective-permute-start(bf16[1,1,32,2]{2,3,1,0:T(2,128)(2,1)S(1)} %convert_bitcast_fusion), channel_id=1, source_target_pairs={{16,0},{17,1},{18,2},{19,3},{20,4},{21,5},{22,6},{23,7},{24,8},{25... | collective-permute-start | bytes 392 | tf_op jit(solution)/shard_map/ppermute | solution.py:21
  13.3 18.3 %collective-permute-start.12 = (bf16[1,1,32,128]{3,2,1,0:T(8,128)(2,1)S(1)}, bf16[1,1,32,128]{3,2,1,0:T(8,128)(2,1)S(1)}, u32[]{:S(2)}, u32[]{:S(2)}) collective-permute-start(bf16[1,1,32,128]{3,2,1,0:T(8,128)(2,1)S(1)} %bitcast.77), channel_id=1, source_target_pairs={{0,16},{1,17},{2,18},{3,19},{4,20},{5,21},{6,22},{7,23},{8,24},{9,... | collective-permute-start | bytes 24584 | tf_op jit(solution)/shard_map/ppermute | solution.py:20
  18.1 34.2 %copy-start.1 = (bf16[32,32,128]{2,1,0:T(8,128)(2,1)S(1)}, bf16[32,32,128]{2,1,0:T(8,128)(2,1)}, u32[]{:S(2)}) copy-start(bf16[32,32,128]{2,1,0:T(8,128)(2,1)} %param.14) | copy-start | bytes 786436
  19.9 5.9 %collective-permute-start.6 = (bf16[3,1,32,2]{2,3,1,0:T(2,128)(2,1)S(1)}, bf16[3,1,32,2]{2,3,1,0:T(2,128)(2,1)S(1)}, u32[]{:S(2)}, u32[]{:S(2)}) collective-permute-start(bf16[3,1,32,2]{2,3,1,0:T(2,128)(2,1)S(1)} %pad_maximum_fusion.11), channel_id=1, source_target_pairs={{0,1},{1,2},{2,3},{3,4},{4,5},{5,6},{6,7},{7,8},{8,9},{9,10},{10,1... | collective-permute-start | bytes 1160 | tf_op jit(solution)/shard_map/ppermute | solution.py:20
  24.2 5.5 %collective-permute-start.7 = (bf16[3,1,32,2]{2,3,1,0:T(2,128)(2,1)S(1)}, bf16[3,1,32,2]{2,3,1,0:T(2,128)(2,1)S(1)}, u32[]{:S(2)}, u32[]{:S(2)}) collective-permute-start(bf16[3,1,32,2]{2,3,1,0:T(2,128)(2,1)S(1)} %pad_maximum_fusion.11), channel_id=1, source_target_pairs={{1,0},{2,1},{3,2},{4,3},{5,4},{6,5},{7,6},{8,7},{9,8},{10,9},{11,1... | collective-permute-start | bytes 1160 | tf_op jit(solution)/shard_map/ppermute | solution.py:21
  25.8 5.8 %collective-permute-start.13 = (bf16[1,1,32,128]{3,2,1,0:T(8,128)(2,1)S(1)}, bf16[1,1,32,128]{3,2,1,0:T(8,128)(2,1)S(1)}, u32[]{:S(2)}, u32[]{:S(2)}) collective-permute-start(bf16[1,1,32,128]{3,2,1,0:T(8,128)(2,1)S(1)} %bitcast.78), channel_id=1, source_target_pairs={{16,0},{17,1},{18,2},{19,3},{20,4},{21,5},{22,6},{23,7},{24,8},{25... | collective-permute-start | bytes 24584 | tf_op jit(solution)/shard_map/ppermute | solution.py:21
  29.6 22.6 %collective-permute-start = (bf16[16,32,128]{2,1,0:T(8,128)(2,1)S(1)}, bf16[16,32,128]{2,1,0:T(8,128)(2,1)S(1)}, u32[]{:S(2)}, u32[]{:S(2)}) collective-permute-start(bf16[16,32,128]{2,1,0:T(8,128)(2,1)S(1)} %get-tuple-element.64), channel_id=1, source_target_pairs={{0,16},{1,17},{2,18},{3,19},{4,20},{5,21},{6,22},{7,23},{8,24},{9,... | collective-permute-start | bytes 393224 | tf_op jit(solution)/shard_map/ppermute | solution.py:20
  31.6 12.8 %collective-permute-start.14 = (bf16[3,1,32,128]{3,2,1,0:T(8,128)(2,1)S(1)}, bf16[3,1,32,128]{3,2,1,0:T(8,128)(2,1)S(1)}, u32[]{:S(2)}, u32[]{:S(2)}) collective-permute-start(bf16[3,1,32,128]{3,2,1,0:T(8,128)(2,1)S(1)} %pad_maximum_fusion.6), channel_id=1, source_target_pairs={{0,1},{1,2},{2,3},{3,4},{4,5},{5,6},{6,7},{7,8},{8,9},{9,10},{10,1... | collective-permute-start | bytes 73736 | tf_op jit(solution)/shard_map/ppermute | solution.py:20
  35.9 9.8 %collective-permute-start.15 = (bf16[3,1,32,128]{3,2,1,0:T(8,128)(2,1)S(1)}, bf16[3,1,32,128]{3,2,1,0:T(8,128)(2,1)S(1)}, u32[]{:S(2)}, u32[]{:S(2)}) collective-permute-start(bf16[3,1,32,128]{3,2,1,0:T(8,128)(2,1)S(1)} %pad_maximum_fusion.6), channel_id=1, source_target_pairs={{1,0},{2,1},{3,2},{4,3},{5,4},{6,5},{7,6},{8,7},{9,8},{10,9},{11,1... | collective-permute-start | bytes 73736 | tf_op jit(solution)/shard_map/ppermute | solution.py:21
  44.4 7.9 %collective-permute-start.1 = (bf16[16,32,128]{2,1,0:T(8,128)(2,1)S(1)}, bf16[16,32,128]{2,1,0:T(8,128)(2,1)S(1)}, u32[]{:S(2)}, u32[]{:S(2)}) collective-permute-start(bf16[16,32,128]{2,1,0:T(8,128)(2,1)S(1)} %get-tuple-element.63), channel_id=1, source_target_pairs={{16,0},{17,1},{18,2},{19,3},{20,4},{21,5},{22,6},{23,7},{24,8},{25... | collective-permute-start | bytes 393224 | tf_op jit(solution)/shard_map/ppermute | solution.py:21
  46.4 14.2 %collective-permute-start.10 = (bf16[3,1,32,1024]{3,2,1,0:T(8,128)(2,1)S(1)}, bf16[3,1,32,1024]{3,2,1,0:T(8,128)(2,1)S(1)}, u32[]{:S(2)}, u32[]{:S(2)}) collective-permute-start(bf16[3,1,32,1024]{3,2,1,0:T(8,128)(2,1)S(1)} %pad_maximum_fusion.1), channel_id=1, source_target_pairs={{0,1},{1,2},{2,3},{3,4},{4,5},{5,6},{6,7},{7,8},{8,9},{9,10},{10,1... | collective-permute-start | bytes 589832 | tf_op jit(solution)/shard_map/ppermute | solution.py:20
  51.0 12.5 %collective-permute-start.11 = (bf16[3,1,32,1024]{3,2,1,0:T(8,128)(2,1)S(1)}, bf16[3,1,32,1024]{3,2,1,0:T(8,128)(2,1)S(1)}, u32[]{:S(2)}, u32[]{:S(2)}) collective-permute-start(bf16[3,1,32,1024]{3,2,1,0:T(8,128)(2,1)S(1)} %pad_maximum_fusion.1), channel_id=1, source_target_pairs={{1,0},{2,1},{3,2},{4,3},{5,4},{6,5},{7,6},{8,7},{9,8},{10,9},{11,1... | collective-permute-start | bytes 589832 | tf_op jit(solution)/shard_map/ppermute | solution.py:21
  53.2 25.1 %collective-permute-start.2 = (bf16[64,16,128]{2,1,0:T(8,128)(2,1)}, bf16[64,16,128]{2,1,0:T(8,128)(2,1)}, u32[]{:S(2)}, u32[]{:S(2)}) collective-permute-start(bf16[64,16,128]{2,1,0:T(8,128)(2,1)} %get-tuple-element.61), channel_id=1, source_target_pairs={{0,1},{1,2},{2,3},{3,4},{4,5},{5,6},{6,7},{7,8},{8,9},{9,10},{10,1... | collective-permute-start | bytes 786440 | tf_op jit(solution)/shard_map/ppermute | solution.py:20
  59.2 19.2 %collective-permute-start.3 = (bf16[64,16,128]{2,1,0:T(8,128)(2,1)}, bf16[64,16,128]{2,1,0:T(8,128)(2,1)}, u32[]{:S(2)}, u32[]{:S(2)}) collective-permute-start(bf16[64,16,128]{2,1,0:T(8,128)(2,1)} %get-tuple-element.62), channel_id=1, source_target_pairs={{1,0},{2,1},{3,2},{4,3},{5,4},{6,5},{7,6},{8,7},{9,8},{10,9},{11,1... | collective-permute-start | bytes 786440 | tf_op jit(solution)/shard_map/ppermute | solution.py:21
  65.4 6.6 %copy-start.6 = (bf16[32,64,64]{2,1,0:T(8,128)(2,1)S(1)}, bf16[32,64,64]{2,1,0:T(8,128)(2,1)}, u32[]{:S(2)}) copy-start(bf16[32,64,64]{2,1,0:T(8,128)(2,1)} %convolution_convert_fusion) | copy-start | bytes 786436
  71.9 6.2 %copy-start.4 = (s32[1,1,32]{2,1,0:T(1,128)S(1)}, s32[1,1,32]{2,1,0:T(1,128)}, u32[]{:S(2)}) copy-start(s32[1,1,32]{2,1,0:T(1,128)} %param.19) | copy-start | bytes 388
  71.9 6.3 %copy-start.2 = (bf16[3,3,32,128]{3,2,1,0:T(8,128)(2,1)S(1)}, bf16[3,3,32,128]{3,2,1,0:T(8,128)(2,1)}, u32[]{:S(2)}) copy-start(bf16[3,3,32,128]{3,2,1,0:T(8,128)(2,1)} %pad_maximum_fusion.2) | copy-start | bytes 221188
  77.2 3.0 %copy-start.3 = (f32[32,128]{1,0:T(8,128)S(1)}, f32[32,128]{1,0:T(8,128)}, u32[]{:S(2)}) copy-start(f32[32,128]{1,0:T(8,128)} %get-tuple-element.75) | copy-start | bytes 49156
  77.2 3.0 %copy-start.5 = (pred[8]{0:T(512)(128)(4,1)S(1)}, pred[8]{0:T(512)(128)(4,1)}, u32[]{:S(2)}) copy-start(pred[8]{0:T(512)(128)(4,1)} %get-tuple-element.70) | copy-start | bytes 28
  80.3 3.4 %collective-permute-start.16 = (f32[1,1,8,128]{3,2,1,0:T(8,128)S(1)}, f32[1,1,8,128]{3,2,1,0:T(8,128)S(1)}, u32[]{:S(2)}, u32[]{:S(2)}) collective-permute-start(f32[1,1,8,128]{3,2,1,0:T(8,128)S(1)} %get-tuple-element.59), channel_id=1, source_target_pairs={{0,16},{1,17},{2,18},{3,19},{4,20},{5,21},{6,22},{7,23},{8,24},{9,... | collective-permute-start | bytes 12296 | tf_op jit(solution)/shard_map/ppermute | solution.py:20
  82.3 3.1 %collective-permute-start.17 = (f32[1,1,8,128]{3,2,1,0:T(8,128)S(1)}, f32[1,1,8,128]{3,2,1,0:T(8,128)S(1)}, u32[]{:S(2)}, u32[]{:S(2)}) collective-permute-start(f32[1,1,8,128]{3,2,1,0:T(8,128)S(1)} %get-tuple-element.59), channel_id=1, source_target_pairs={{16,0},{17,1},{18,2},{19,3},{20,4},{21,5},{22,6},{23,7},{24,8},{25... | collective-permute-start | bytes 12296 | tf_op jit(solution)/shard_map/ppermute | solution.py:21
  85.4 4.4 %collective-permute-start.18 = (f32[3,1,8,128]{3,2,1,0:T(8,128)S(1)}, f32[3,1,8,128]{3,2,1,0:T(8,128)S(1)}, u32[]{:S(2)}, u32[]{:S(2)}) collective-permute-start(f32[3,1,8,128]{3,2,1,0:T(8,128)S(1)} %pad_maximum_fusion.7), channel_id=1, source_target_pairs={{0,1},{1,2},{2,3},{3,4},{4,5},{5,6},{6,7},{7,8},{8,9},{9,10},{10,1... | collective-permute-start | bytes 36872 | tf_op jit(solution)/shard_map/ppermute | solution.py:20
  88.4 5.6 %collective-permute-start.19 = (f32[3,1,8,128]{3,2,1,0:T(8,128)S(1)}, f32[3,1,8,128]{3,2,1,0:T(8,128)S(1)}, u32[]{:S(2)}, u32[]{:S(2)}) collective-permute-start(f32[3,1,8,128]{3,2,1,0:T(8,128)S(1)} %pad_maximum_fusion.7), channel_id=1, source_target_pairs={{1,0},{2,1},{3,2},{4,3},{5,4},{6,5},{7,6},{8,7},{9,8},{10,9},{11,1... | collective-permute-start | bytes 36872 | tf_op jit(solution)/shard_map/ppermute | solution.py:21
  94.3 2.6 %collective-permute-start.20 = (f32[1,1,8,128]{3,2,1,0:T(8,128)S(1)}, f32[1,1,8,128]{3,2,1,0:T(8,128)S(1)}, u32[]{:S(2)}, u32[]{:S(2)}) collective-permute-start(f32[1,1,8,128]{3,2,1,0:T(8,128)S(1)} %get-tuple-element.57), channel_id=1, source_target_pairs={{0,16},{1,17},{2,18},{3,19},{4,20},{5,21},{6,22},{7,23},{8,24},{9,... | collective-permute-start | bytes 12296 | tf_op jit(solution)/shard_map/ppermute | solution.py:20
  95.6 3.1 %collective-permute-start.21 = (f32[1,1,8,128]{3,2,1,0:T(8,128)S(1)}, f32[1,1,8,128]{3,2,1,0:T(8,128)S(1)}, u32[]{:S(2)}, u32[]{:S(2)}) collective-permute-start(f32[1,1,8,128]{3,2,1,0:T(8,128)S(1)} %get-tuple-element.57), channel_id=1, source_target_pairs={{16,0},{17,1},{18,2},{19,3},{20,4},{21,5},{22,6},{23,7},{24,8},{25... | collective-permute-start | bytes 12296 | tf_op jit(solution)/shard_map/ppermute | solution.py:21
  98.7 6.4 %collective-permute-start.22 = (f32[3,1,8,128]{3,2,1,0:T(8,128)S(1)}, f32[3,1,8,128]{3,2,1,0:T(8,128)S(1)}, u32[]{:S(2)}, u32[]{:S(2)}) collective-permute-start(f32[3,1,8,128]{3,2,1,0:T(8,128)S(1)} %pad_maximum_fusion.8), channel_id=1, source_target_pairs={{0,1},{1,2},{2,3},{3,4},{4,5},{5,6},{6,7},{7,8},{8,9},{9,10},{10,1... | collective-permute-start | bytes 36872 | tf_op jit(solution)/shard_map/ppermute | solution.py:20
  103.7 6.7 %collective-permute-start.23 = (f32[3,1,8,128]{3,2,1,0:T(8,128)S(1)}, f32[3,1,8,128]{3,2,1,0:T(8,128)S(1)}, u32[]{:S(2)}, u32[]{:S(2)}) collective-permute-start(f32[3,1,8,128]{3,2,1,0:T(8,128)S(1)} %pad_maximum_fusion.8), channel_id=1, source_target_pairs={{1,0},{2,1},{3,2},{4,3},{5,4},{6,5},{7,6},{8,7},{9,8},{10,9},{11,1... | collective-permute-start | bytes 36872 | tf_op jit(solution)/shard_map/ppermute | solution.py:21
  110.7 2.6 %collective-permute-start.24 = (f32[1,1,8,128]{3,2,1,0:T(8,128)S(1)}, f32[1,1,8,128]{3,2,1,0:T(8,128)S(1)}, u32[]{:S(2)}, u32[]{:S(2)}) collective-permute-start(f32[1,1,8,128]{3,2,1,0:T(8,128)S(1)} %get-tuple-element.55), channel_id=1, source_target_pairs={{0,16},{1,17},{2,18},{3,19},{4,20},{5,21},{6,22},{7,23},{8,24},{9,... | collective-permute-start | bytes 12296 | tf_op jit(solution)/shard_map/ppermute | solution.py:20
  112.0 3.1 %collective-permute-start.25 = (f32[1,1,8,128]{3,2,1,0:T(8,128)S(1)}, f32[1,1,8,128]{3,2,1,0:T(8,128)S(1)}, u32[]{:S(2)}, u32[]{:S(2)}) collective-permute-start(f32[1,1,8,128]{3,2,1,0:T(8,128)S(1)} %get-tuple-element.55), channel_id=1, source_target_pairs={{16,0},{17,1},{18,2},{19,3},{20,4},{21,5},{22,6},{23,7},{24,8},{25... | collective-permute-start | bytes 12296 | tf_op jit(solution)/shard_map/ppermute | solution.py:21
  115.1 7.1 %collective-permute-start.26 = (f32[3,1,8,128]{3,2,1,0:T(8,128)S(1)}, f32[3,1,8,128]{3,2,1,0:T(8,128)S(1)}, u32[]{:S(2)}, u32[]{:S(2)}) collective-permute-start(f32[3,1,8,128]{3,2,1,0:T(8,128)S(1)} %pad_maximum_fusion.9), channel_id=1, source_target_pairs={{0,1},{1,2},{2,3},{3,4},{4,5},{5,6},{6,7},{7,8},{8,9},{9,10},{10,1... | collective-permute-start | bytes 36872 | tf_op jit(solution)/shard_map/ppermute | solution.py:20
  120.8 5.6 %collective-permute-start.27 = (f32[3,1,8,128]{3,2,1,0:T(8,128)S(1)}, f32[3,1,8,128]{3,2,1,0:T(8,128)S(1)}, u32[]{:S(2)}, u32[]{:S(2)}) collective-permute-start(f32[3,1,8,128]{3,2,1,0:T(8,128)S(1)} %pad_maximum_fusion.9), channel_id=1, source_target_pairs={{1,0},{2,1},{3,2},{4,3},{5,4},{6,5},{7,6},{8,7},{9,8},{10,9},{11,1... | collective-permute-start | bytes 36872 | tf_op jit(solution)/shard_map/ppermute | solution.py:21
where the time goes:
time: 128 us
  starting transfers between devices  65.3 us (51%)
  waiting for transfers between devices  24.7 us (19%)
  matrix products  19.5 us (15%)
  local copies, waits for them, and re-layouts  12.3 us (10%)
  other arithmetic  4.62 us (4%)
    ppermute x14, starting transfers between devices, extended(): before = lax.ppermute(last, axis, up)  47.1 us
    ppermute x14, waiting for transfers between devices, extended(): after = lax.ppermute(first, axis, down)  24.4 us
    ppermute x14, starting transfers between devices, extended(): after = lax.ppermute(first, axis, down)  18.2 us
    dot_general x2, matrix products, paint(): jnp.einsum('kyj,kxj->kyx', spread, cols_hot, preferred_element_type=jnp.f...  8.35 us
    eq x1, local copies, waits for them, and re-layouts, placement(): return (across == anchors[:, None, None] + inside).astype(jnp.bfloat16)  6.43 us
    dot_general x1, matrix products, body(): lax.dot_general(own_canvas, near_canvas, (((1,), (1,)), ((), ())), prefer...  5.24 us
  transfers between devices with their start and end apart: 28, of which 11 were waited for; matrix products, arithmetic and copies ran while one was open for 24% of the time, Pallas kernels for 0%

commit v1 on v0

--- a/solution.py
+++ b/solution.py
@@ -1,10 +1,15 @@
+import functools
+
 import jax
 import jax.numpy as jnp
 from jax import lax
+from jax.experimental import pallas as pl
+from jax.experimental.pallas import tpu as pltpu
 from jax.sharding import PartitionSpec as P
 
 BLOCKS = 4
 PATCH = 32
+LANES = 128
 
 
 precise = lax.Precision.HIGHEST
@@ -41,7 +46,7 @@
     return canvas.reshape(patches.shape[0], canvas_rows * canvas_cols)
 
 
-def body(movie, footprints, centres, traces, counts, order):
+def general_body(movie, footprints, centres, traces, counts, order):
     tile_side = movie.shape[0]
     frame_count = movie.shape[2]
     slot_count = footprints.shape[2]
@@ -127,6 +132,301 @@
     return result[None, None]
 
 
+def swap(x):
+    return lax.ppermute(x, "ty", [(0, 1), (1, 0)])
+
+
+def pairwise(x, step):
+    count = lax.axis_size("tx")
+    pairs = []
+    for i in range(count - step):
+        base = count * ((i // step) % 2)
+        pairs += [(base + i, base + i + step), (base + i + step, base + i)]
+    return lax.ppermute(x, ("ty", "tx"), pairs)
+
+
+def upward(step):
+    column = lax.axis_index("tx")
+    return (((column // step) % 2) == lax.axis_index("ty")).astype(jnp.int32)
+
+
+def near_kernel(
+    slots, meta, own, direct, other, film_own, film_pair, film_direct, film_other,
+    far1, far2, far3, keep, patches, trails, canvas, start, film,
+):
+    tiles = 6
+    total = 6 * slots
+    block = slots // BLOCKS
+    group = 2 * block
+    source = 3 * group
+    pixels = PATCH * PATCH // LANES
+    depth = canvas.shape[0] // total
+    sources = ((own, 0), (own, 1), (direct, 0), (direct, 1), (other, 0), (other, 1))
+
+    canvas[...] = jnp.zeros_like(canvas)
+    for t, (ref, u) in enumerate(sources):
+        rows = slots * pixels
+        patches[t * rows:(t + 1) * rows, :] = ref[u, :rows, :].astype(jnp.float32)
+        trails[t * slots:(t + 1) * slots, :] = ref[u, rows:rows + slots, :].astype(jnp.float32)
+
+    lane = lax.broadcasted_iota(jnp.int32, (pixels, LANES), 1)
+    sub = lax.broadcasted_iota(jnp.int32, (pixels, LANES), 0)
+    low = lane < LANES // 2
+    inner = lane & (LANES // 2 - 1)
+
+    def paint(t, s):
+        a = meta[t, 3 * slots + 1]
+        j = meta[t, 3 * slots + 2]
+        p = meta[t, s]
+        live = (p < meta[t, 3 * slots]).astype(jnp.int32)
+        top = a * PATCH + meta[t, slots + p]
+        left = meta[t, 2 * slots + p] + (j - 1) * PATCH
+        slot = (s // block) * source + j * group + a * block + s % block
+        odd = top & 1
+        level = top // 2
+        value = patches[pl.ds(pl.multiple_of((t * slots + p) * pixels, pixels), pixels), :]
+        shift = left + 32 * odd + LANES
+        turned = [pltpu.roll(value, (shift + 32 * m) & (LANES - 1), 1) for m in range(4)]
+        first = pltpu.roll(turned[0], odd, 0)
+        inside = (inner >= left) & (inner < left + PATCH * live)
+        even_rows = jnp.where(low, jnp.where(sub >= odd, first, 0.0), turned[1])
+        odd_rows = jnp.where(low, turned[2], turned[3])
+        last = jnp.where(inside & low & (sub < odd), first, 0.0)
+        at = level * total + slot
+        canvas[pl.ds(at, pixels, stride=2 * total), :] = jnp.where(inside, even_rows, 0.0)
+        canvas[pl.ds(at + total, pixels, stride=2 * total), :] = jnp.where(inside, odd_rows, 0.0)
+        canvas[pl.ds(at + 2 * pixels * total, 1), :] = last[0:1, :]
+        trail = trails[pl.ds(t * slots + p, 1), :]
+        start[pl.ds(slot, 1), :] = trail * live.astype(jnp.float32)
+
+    for t in range(tiles):
+        @pl.loop(0, slots // UNROLL)
+        def _(step):
+            for k in range(UNROLL):
+                paint(t, step * UNROLL + k)
+
+    height = film_own.shape[0]
+    half = PATCH // 2
+    row0 = pl.multiple_of(meta[0, 3 * slots + 1] * height, height)
+    row1 = pl.multiple_of(meta[1, 3 * slots + 1] * height, height)
+    film[pl.ds(row0, height), half:half + PATCH, :] = film_own[...]
+    film[pl.ds(row1, height), half:half + PATCH, :] = film_pair[...]
+    for t, ref in ((2, film_direct), (4, film_other)):
+        for u in range(2):
+            row = pl.multiple_of(meta[t + u, 3 * slots + 1] * height, height)
+            part = ref[u * height:(u + 1) * height]
+            side = meta[t + u, 3 * slots + 2]
+
+            @pl.when(side == 0)
+            def _():
+                film[pl.ds(row, height), 0:half, :] = part
+
+            @pl.when(side != 0)
+            def _():
+                film[pl.ds(row, height), half + PATCH:2 * PATCH, :] = part
+
+    margins = jnp.zeros((2 * slots, total), jnp.float32)
+    drive = jnp.zeros((2 * slots, film.shape[2]), jnp.float32)
+    edge = half // 4
+    for step in range(depth // 2):
+        at = 2 * step * total
+        painted = jnp.concatenate(
+            [canvas[at:at + total, :], canvas[at + total:at + 2 * total, :]], axis=1
+        ).astype(jnp.bfloat16)
+        mine = jnp.concatenate(
+            [painted[q * source + group:q * source + 2 * group] for q in range(BLOCKS)], axis=0
+        )
+        margins += lax.dot_general(
+            mine, painted, (((1,), (1,)), ((), ())), preferred_element_type=jnp.float32
+        )
+        if edge <= step < depth // 2 - edge:
+            pixels_here = film[(step - edge) * 4:(step - edge) * 4 + 4].reshape(2 * LANES, -1)
+            drive += jnp.dot(mine, pixels_here, preferred_element_type=jnp.float32)
+
+    coupling = jnp.dot(
+        margins, start[...], precision=precise, preferred_element_type=jnp.float32
+    )
+    line = lax.broadcasted_iota(jnp.int32, margins.shape, 0)
+    column = lax.broadcasted_iota(jnp.int32, margins.shape, 1)
+    matching = column == (line // group) * source + group + line % group
+    diagonal = jnp.sum(jnp.where(matching, margins, 0.0), axis=1, keepdims=True)
+    diagonal = jnp.where(diagonal > 0.0, diagonal, 1.0)
+    begin = jnp.concatenate(
+        [start[q * source + group:q * source + 2 * group, :] for q in range(BLOCKS)], axis=0
+    )
+    level = begin + (drive - coupling) / diagonal
+    share = margins / diagonal
+
+    def rows_of(x, q):
+        return x[q * group:(q + 1) * group]
+
+    first = jnp.maximum(rows_of(level, 0), 0.0)
+    change = first - rows_of(begin, 0)
+    pieces = (
+        change,
+        rows_of(level, 1), rows_of(begin, 1), rows_of(share, 1)[:, :LANES],
+        rows_of(level, 2), rows_of(begin, 2), rows_of(share, 2)[:, :LANES],
+    )
+    for ref in (far1, far2, far3):
+        for i in range(ref.shape[0] // group):
+            ref[i * group:(i + 1) * group, :] = pieces[i]
+    keep[0:group, :] = first
+    keep[group:2 * group, :] = rows_of(level, 3)
+    keep[2 * group:3 * group, :] = rows_of(share, 3)[:, :LANES]
+    keep[3 * group:4 * group, :total - LANES] = rows_of(share, 3)[:, LANES:]
+
+
+def sweep_kernel(slots, where, mine, keep, direct, other, order, out, box, current):
+    block = slots // BLOCKS
+    group = 2 * block
+    reach = BLOCKS - 1
+    sizes = (7 * group, 4 * group, group)
+    box[reach] = mine[...]
+    at = 0
+    for step in range(1, BLOCKS):
+        size = sizes[step - 1]
+        up = where[step]
+        box[reach - step + 2 * step * up, 0:size, :] = direct[at:at + size, :]
+        box[reach + step - 2 * step * up, 0:size, :] = other[at:at + size, :]
+        at += size
+
+    def exact(a, b):
+        return jnp.dot(a, b, precision=precise, preferred_element_type=jnp.float32)
+
+    def around(values, j):
+        return [values[j - 1], values[j], values[j + 1]]
+
+    def part(j, i):
+        return box[j, i * group:(i + 1) * group, :]
+
+    change0 = {j: part(j, 0) for j in range(2 * reach + 1)}
+    renewed1, change1 = {}, {}
+    for j in range(1, 2 * reach):
+        near = jnp.concatenate(around(change0, j), axis=0)
+        renewed1[j] = jnp.maximum(part(j, 1) - exact(part(j, 3)[:, :3 * group], near), 0.0)
+        change1[j] = renewed1[j] - part(j, 2)
+    renewed2, change2 = {}, {}
+    for j in range(2, 2 * reach - 1):
+        near = jnp.concatenate(around(change0, j) + around(change1, j), axis=0)
+        renewed2[j] = jnp.maximum(part(j, 4) - exact(part(j, 6)[:, :6 * group], near), 0.0)
+        change2[j] = renewed2[j] - part(j, 5)
+    near = jnp.concatenate(
+        around(change0, reach) + around(change1, reach) + around(change2, reach), axis=0
+    )
+    share = jnp.concatenate(
+        [keep[2 * group:3 * group, :], keep[3 * group:4 * group, :9 * group - LANES]], axis=1
+    )
+    current[0:group, :] = keep[0:group, :]
+    current[group:2 * group, :] = renewed1[reach]
+    current[2 * group:3 * group, :] = renewed2[reach]
+    current[3 * group:4 * group, :] = jnp.maximum(
+        keep[group:2 * group, :] - exact(share, near), 0.0
+    )
+    row = pl.multiple_of(where[0] * block, block)
+    ordered = jnp.concatenate(
+        [current[pl.ds(q * group + row, block), :] for q in range(BLOCKS)], axis=0
+    )
+    place = lax.broadcasted_iota(jnp.int32, (slots, slots), 0) == order[...]
+    out[...] = exact(place.astype(jnp.float32), ordered)
+
+
+UNROLL = 4
+
+
+def strip_body(movie, footprints, centres, traces, counts, order):
+    height, width, frames = movie.shape
+    slots = footprints.shape[2]
+    half = PATCH // 2
+    group = 2 * slots // BLOCKS
+    bf16 = jnp.bfloat16
+    core = lax.axis_index("ty")
+    up = [upward(step) for step in range(1, BLOCKS)]
+
+    numbers = jnp.concatenate(
+        [order[0, 0], centres[0, 0, :, 0], centres[0, 0, :, 1], counts[0]]
+    ).astype(bf16)
+    numbers = jnp.pad(numbers[None], ((0, 15), (0, LANES - numbers.shape[0])))
+    packed = jnp.concatenate(
+        [footprints[0, 0].reshape(-1, LANES), traces[0, 0], numbers], axis=0
+    )
+    pair_packed = swap(packed)
+    pair_movie = swap(movie)
+    both = jnp.stack([packed, pair_packed])
+    direct = pairwise(both, 1)
+    edge = half * up[0]
+    edges = jnp.concatenate(
+        [
+            lax.dynamic_slice_in_dim(movie, edge, half, axis=1),
+            lax.dynamic_slice_in_dim(pair_movie, edge, half, axis=1),
+        ],
+        axis=0,
+    )
+    film_direct = pairwise(edges, 1)
+    other = swap(direct)
+    film_other = swap(film_direct)
+
+    line = packed.shape[0] - 16
+    meta = jnp.concatenate([both[:, line], direct[:, line], other[:, line]], axis=0)
+    rows = jnp.stack([core, 1 - core, core, 1 - core, 1 - core, core])
+    sides = jnp.stack([1, 1, 2 * up[0], 2 * up[0], 2 - 2 * up[0], 2 - 2 * up[0]])
+    lanes = jnp.arange(LANES)[None]
+    meta = jnp.where(
+        lanes == 3 * slots + 1,
+        rows[:, None],
+        jnp.where(lanes == 3 * slots + 2, sides[:, None], meta.astype(jnp.int32)),
+    ).astype(jnp.int32)
+
+    vmem = pl.BlockSpec(memory_space=pltpu.VMEM)
+    smem = pl.BlockSpec(memory_space=pltpu.SMEM)
+    f32 = jnp.float32
+    depth = (2 * height + PATCH) // 2
+    far1, far2, far3, keep = pl.pallas_call(
+        functools.partial(near_kernel, slots),
+        out_shape=[
+            jax.ShapeDtypeStruct((7 * group, frames), f32),
+            jax.ShapeDtypeStruct((4 * group, frames), f32),
+            jax.ShapeDtypeStruct((group, frames), f32),
+            jax.ShapeDtypeStruct((4 * group, frames), f32),
+        ],
+        in_specs=[smem] + [vmem] * 7,
+        out_specs=[vmem] * 4,
+        scratch_shapes=[
+            pltpu.VMEM((6 * slots * PATCH * PATCH // LANES, LANES), f32),
+            pltpu.VMEM((6 * slots, frames), f32),
+            pltpu.VMEM((depth * 6 * slots, LANES), f32),
+            pltpu.VMEM((6 * slots, frames), f32),
+            pltpu.VMEM((2 * height, 2 * PATCH, frames), bf16),
+        ],
+        name="near",
+    )(meta, both, direct, other, movie, pair_movie, film_direct, film_other)
+
+    far = jnp.concatenate([pairwise(far1, 1), pairwise(far2, 2), pairwise(far3, 3)], axis=0)
+    far_other = swap(far)
+    where = jnp.stack([core] + up).astype(jnp.int32)
+    result = pl.pallas_call(
+        functools.partial(sweep_kernel, slots),
+        out_shape=jax.ShapeDtypeStruct((slots, frames), f32),
+        in_specs=[smem] + [vmem] * 5,
+        out_specs=vmem,
+        scratch_shapes=[
+            pltpu.VMEM((2 * BLOCKS - 1, 7 * group, frames), f32),
+            pltpu.VMEM((4 * group, frames), f32),
+        ],
+        name="sweep",
+    )(where, far1, keep, far, far_other, order[0])
+    return result[None, None]
+
+
+def body(movie, footprints, centres, traces, counts, order):
+    strip = (
+        lax.axis_size("ty") == 2
+        and movie.shape == (PATCH, PATCH, LANES)
+        and footprints.shape[2] == PATCH
+    )
+    chosen = strip_body if strip else general_body
+    return chosen(movie, footprints, centres, traces, counts, order)
+
+
 def solution(mesh):
     in_specs = (
         P("ty", "tx", None),

time: 128 us -> 52.8 us (0.41)
  starting transfers between devices: 65.3 us -> 17.3 us
  matrix products: 19.5 us -> 0 us
  Pallas kernels: 0 us -> 13.3 us
  waiting for transfers between devices: 24.7 us -> 13.5 us
  local copies, waits for them, and re-layouts: 12.3 us -> 3.79 us
    ppermute x28 -> x10, starting transfers between devices: 65.3 us -> 17.3 us  [the longest x5 16.6 us: pairwise(): return lax.ppermute(x, ('ty', 'tx'), pairs)]
    dot_general x11 -> x0, matrix products: 19.5 us -> none  [the longest x2 8.35 us: paint(): jnp.einsum('kyj,kxj->kyx', spread, cols_hot, preferred_element_type=jnp.f...]
    pallas_call x0 -> x2, Pallas kernels: none -> 13.3 us  [the longest x1 10.8 us: strip_body(): pl.pallas_call(functools.partial(near_kernel, slots), out_shape=[jax.Shap...]
    ppermute x28 -> x10, waiting for transfers between devices: 24.7 us -> 13.5 us  [the longest x5 10.8 us: pairwise(): return lax.ppermute(x, ('ty', 'tx'), pairs)]
    eq x1 -> x0, local copies, waits for them, and re-layouts: 6.43 us -> none  [placement(): return (across == anchors[:, None, None] + inside).astype(jnp.bfloat16)]
    another operation x0 -> x6, other arithmetic: none -> 2.7 us
    unnamed x17 -> x27, local copies, waits for them, and re-layouts: 0.15 us -> 2.7 us
    slice x5 -> x2, local copies, waits for them, and re-layouts: 2.4 us -> 0.01 us  [the longest x1 0.01 us: strip_body(): other[:, line]]
  transfers between devices with their start and end apart: 28 -> 10, of which waited for: 11 -> 6; matrix products, arithmetic and copies ran while one was open for 24% -> 9% of each run, Pallas kernels for 0% -> 0%
where the time goes in v1:
time: 52.8 us; the launch traced here: 52.3 us
  starting transfers between devices  17.3 us (33%)
  waiting for transfers between devices  13.5 us (26%)
  Pallas kernels  13.3 us (25%)
  local copies, waits for them, and re-layouts  3.79 us (7%)
  other arithmetic  3.48 us (7%)
  between operations  0.98 us (2%)
    ppermute x5, starting transfers between devices, pairwise(): return lax.ppermute(x, ('ty', 'tx'), pairs)  16.6 us
    pallas_call x1, Pallas kernels, strip_body(): pl.pallas_call(functools.partial(near_kernel, slots), out_shape=[jax.Shap...  10.8 us
    ppermute x5, waiting for transfers between devices, pairwise(): return lax.ppermute(x, ('ty', 'tx'), pairs)  10.8 us
    unnamed x27, local copies, waits for them, and re-layouts  2.7 us
    ppermute x5, waiting for transfers between devices, swap(): return lax.ppermute(x, 'ty', [(0, 1), (1, 0)])  2.64 us
    pallas_call x1, Pallas kernels, strip_body(): pl.pallas_call(functools.partial(sweep_kernel, slots), out_shape=jax.Shap...  2.47 us
    another operation x2, other arithmetic  1.34 us
  transfers between devices with their start and end apart: 10, of which 6 were waited for; matrix products, arithmetic and copies ran while one was open for 9% of the time, Pallas kernels for 0%

profile of v1, /device:TPU:0, one launch (start us, length us, event | category | flops | bytes accessed | tf_op | source)
XLA Modules:
  0.0 52.3 jit_solution(9297010399541847783)
XLA Ops:
  0.0 0.5 collective-permute-start.3
  1.2 0.7 %convert.18 = bf16[1,1,32,2]{2,3,1,0:T(2,128)(2,1)S(1)} convert(s32[1,1,32,2]{2,3,1,0:T(2,128)} %param.8) | non-fusion elementwise | flops 64 | bytes 384 | tf_op jit(solution)/shard_map/convert.10
  1.8 0.7 %bitcast_convert_fusion = bf16[1,32]{1,0:T(2,128)(2,1)S(1)} fusion(s32[1,1,32]{2,1,0:T(1,128)} %param.11), kind=kLoop, calls=%fused_computation.34 | loop fusion | flops 32 | bytes 192 | tf_op jit(solution)/shard_map/convert.3
  2.5 0.9 %reshape_squeeze.3 = bf16[256,128]{1,0:T(8,128)(2,1)S(1)} reshape(bf16[1,1,32,1024]{3,2,1,0:T(8,128)(2,1)} %param.7) | data formatting | bytes 131072 | tf_op jit(solution)/shard_map/reshape;squeeze | solution.py:350
  3.4 0.1 fusion.8
  3.5 0.7 %fusion.13 = (bf16[1,304,128]{2,1,0:T(8,128)(2,1)S(1)}, bf16[304,128]{1,0:T(8,128)(2,1)S(1)}) fusion(bf16[16,128]{1,0:T(8,128)(2,1)S(1)} %fusion.8, bf16[32,128]{1,0:T(8,128)(2,1)} %bitcast.31, bf16[256,128]{1,0:T(8,128)(2,1)S(1)} %reshape_squeeze.3), kind=kLoop, calls=%fused_computation.35 | loop fusion | flops 233472 | bytes 233472 | tf_op jit(solution)/shard_map/stack | solution.py:354
  4.2 0.1 collective-permute-start
  4.3 0.0 copy-done.1
  4.3 1.2 %collective-permute-done = bf16[304,128]{1,0:T(8,128)(2,1)S(1)} collective-permute-done((bf16[304,128]{1,0:T(8,128)(2,1)S(1)}, bf16[304,128]{1,0:T(8,128)(2,1)S(1)}, u32[]{:S(2)}, u32[]{:S(2)}) %collective-permute-start) | collective-permute-done | bytes 77856 | tf_op jit(solution)/shard_map/ppermute | solution.py:136
  5.5 0.0 copy-start
  5.5 4.5 %collective-permute-start.1 = (bf16[2,304,128]{2,1,0:T(8,128)(2,1)S(1)}, bf16[2,304,128]{2,1,0:T(8,128)(2,1)S(1)}, u32[]{:S(2)}, u32[]{:S(2)}) collective-permute-start(bf16[2,304,128]{2,1,0:T(8,128)(2,1)S(1)} %pad_maximum_fusion.1.own), channel_id=1, source_target_pairs={{0,1},{1,0},{17,18},{18,17},{2,3},{3,2},{19,20},{20,19},{4,5},{5,4... | collective-permute-start | bytes 466952 | tf_op jit(solution)/shard_map/ppermute | solution.py:145
  10.1 0.0 collective-permute-done.3.film_pair
  10.1 0.0 copy-start.2
  10.2 0.0 copy-done
  10.2 0.6 %copy-done.2 = bf16[32,32,128]{2,1,0:T(8,128)(2,1)} copy-done((bf16[32,32,128]{2,1,0:T(8,128)(2,1)}, bf16[32,32,128]{2,1,0:T(8,128)(2,1)S(1)}, u32[]{:S(2)}) %copy-start.2) | copy-done | bytes 262168
  10.8 1.9 %collective-permute-start.4 = (bf16[64,16,128]{2,1,0:T(8,128)(2,1)S(1)}, bf16[64,16,128]{2,1,0:T(8,128)(2,1)S(1)}, u32[]{:S(2)}, u32[]{:S(2)}) collective-permute-start(bf16[64,16,128]{2,1,0:T(8,128)(2,1)S(1)} %pad_maximum_fusion), channel_id=1, source_target_pairs={{0,1},{1,0},{17,18},{18,17},{2,3},{3,2},{19,20},{20,19},{4,5},{5,4... | collective-permute-start | bytes 786440 | tf_op jit(solution)/shard_map/ppermute | solution.py:145
  12.7 1.8 %collective-permute-done.1.direct = bf16[2,304,128]{2,1,0:T(8,128)(2,1)S(1)} collective-permute-done((bf16[2,304,128]{2,1,0:T(8,128)(2,1)S(1)}, bf16[2,304,128]{2,1,0:T(8,128)(2,1)S(1)}, u32[]{:S(2)}, u32[]{:S(2)}) %collective-permute-start.1) | collective-permute-done | bytes 155680 | tf_op jit(solution)/shard_map/ppermute | solution.py:145
  14.5 0.0 collective-permute-start.2
  14.5 0.1 stack.64
  14.6 0.1 stack.67
  14.7 7.2 %collective-permute-done.4.film_direct = bf16[64,16,128]{2,1,0:T(8,128)(2,1)S(1)} collective-permute-done((bf16[64,16,128]{2,1,0:T(8,128)(2,1)S(1)}, bf16[64,16,128]{2,1,0:T(8,128)(2,1)S(1)}, u32[]{:S(2)}, u32[]{:S(2)}) %collective-permute-start.4) | collective-permute-done | bytes 262176 | tf_op jit(solution)/shard_map/ppermute | solution.py:145
  21.9 0.0 collective-permute-start.5
  21.9 0.0 collective-permute-done.2.other
  21.9 0.0 copy-start.7
  22.0 0.7 %select_select_fusion.meta = s32[6,128]{1,0:T(8,128)} fusion(bf16[2,128]{1,0:T(2,128)(2,1)S(1)} %bitcast.35, bf16[2,128]{1,0:T(2,128)(2,1)S(1)} %bitcast.34, bf16[2,128]{1,0:T(2,128)(2,1)S(1)} %bitcast.33, s32[6]{0:T(128)S(1)} %stack.67, s32[6]{0:T(128)S(1)} %stack.64, pred[128]{0:T(512)(128)(4,1)S(1)} %get-tuple-element.17, ...), kind=kLoop, calls=%fused_computation.22 | loop fusion | flops 6144 | bytes 4912 | tf_op jit(solution)/shard_map/jit(_where)/select_n | solution.py:373
  22.6 0.8 %collective-permute-done.5.film_other = bf16[64,16,128]{2,1,0:T(8,128)(2,1)S(1)} collective-permute-done((bf16[64,16,128]{2,1,0:T(8,128)(2,1)S(1)}, bf16[64,16,128]{2,1,0:T(8,128)(2,1)S(1)}, u32[]{:S(2)}, u32[]{:S(2)}) %collective-permute-start.5) | collective-permute-done | bytes 262176 | tf_op jit(solution)/shard_map/ppermute | solution.py:136
  23.4 0.0 copy-done.6
  23.4 0.0 copy-done.3
  23.4 0.0 copy-done.7
  23.4 0.0 copy-start.4
  23.4 0.7 %copy-done.4 = bf16[64,16,128]{2,1,0:T(8,128)(2,1)} copy-done((bf16[64,16,128]{2,1,0:T(8,128)(2,1)}, bf16[64,16,128]{2,1,0:T(8,128)(2,1)S(1)}, u32[]{:S(2)}) %copy-start.4) | copy-done | bytes 262168
  24.1 10.8 %near.1 = (f32[112,128]{1,0:T(8,128)}, f32[64,128]{1,0:T(8,128)}, f32[16,128]{1,0:T(8,128)}, f32[64,128]{1,0:T(8,128)}) custom-call(s32[6,128]{1,0:T(8,128)} %select_select_fusion.meta, bf16[2,304,128]{2,1,0:T(8,128)(2,1)} %copy-done, bf16[2,304,128]{2,1,0:T(8,128)(2,1)} %copy-done.6, bf16[2,304,128]{2,1,0:T(8,128)(2,1)} %copy-done.7, ...), custom_call_target="tpu_custom_call" | custom-call | tf_op jit(solution)/shard_map/near/pallas_call | solution.py:383
  34.9 2.8 %collective-permute-start.6 = (f32[112,128]{1,0:T(8,128)}, f32[112,128]{1,0:T(8,128)S(1)}, u32[]{:S(2)}, u32[]{:S(2)}) collective-permute-start(f32[112,128]{1,0:T(8,128)} %get-tuple-element.9.mine), channel_id=1, source_target_pairs={{0,1},{1,0},{17,18},{18,17},{2,3},{3,2},{19,20},{20,19},{4,5},{5,4... | collective-permute-start | bytes 172040 | tf_op jit(solution)/shard_map/ppermute | solution.py:145
  37.8 0.0 copy-start.9
  37.9 0.0 copy-start.10
  37.9 0.7 %copy-done.10 = f32[16,128]{1,0:T(8,128)S(1)} copy-done((f32[16,128]{1,0:T(8,128)S(1)}, f32[16,128]{1,0:T(8,128)}, u32[]{:S(2)}) %copy-start.10) | copy-done | bytes 8216
  38.6 3.3 %collective-permute-start.8 = (f32[16,128]{1,0:T(8,128)S(1)}, f32[16,128]{1,0:T(8,128)S(1)}, u32[]{:S(2)}, u32[]{:S(2)}) collective-permute-start(f32[16,128]{1,0:T(8,128)S(1)} %copy-done.10), channel_id=1, source_target_pairs={{0,3},{3,0},{1,4},{4,1},{2,5},{5,2},{19,22},{22,19},{20,23},{23,20... | collective-permute-start | bytes 24584 | tf_op jit(solution)/shard_map/ppermute | solution.py:145
  41.9 0.0 copy-done.9
  41.9 4.0 %collective-permute-start.7 = (f32[64,128]{1,0:T(8,128)S(1)}, f32[64,128]{1,0:T(8,128)S(1)}, u32[]{:S(2)}, u32[]{:S(2)}) collective-permute-start(f32[64,128]{1,0:T(8,128)S(1)} %copy-done.9), channel_id=1, source_target_pairs={{0,2},{2,0},{1,3},{3,1},{18,20},{20,18},{19,21},{21,19},{4,6},{6,4... | collective-permute-start | bytes 98312 | tf_op jit(solution)/shard_map/ppermute | solution.py:145
  45.9 0.0 collective-permute-done.6
  46.0 1.9 %collective-permute-done.7 = f32[64,128]{1,0:T(8,128)S(1)} collective-permute-done((f32[64,128]{1,0:T(8,128)S(1)}, f32[64,128]{1,0:T(8,128)S(1)}, u32[]{:S(2)}, u32[]{:S(2)}) %collective-permute-start.7) | collective-permute-done | bytes 32800 | tf_op jit(solution)/shard_map/ppermute | solution.py:145
  47.8 0.0 collective-permute-done.8
  47.8 0.1 collective-permute-start.9
  47.9 0.6 %pad_add_fusion.where = s32[4]{0:T(128)} fusion(s32[1]{0:T(128)} %bitcast.3, s32[1]{0:T(128)} %bitcast.2, s32[1]{0:T(128)} %bitcast.1, s32[1]{0:T(128)} %bitcast), kind=kLoop, calls=%fused_computation.24 | loop fusion | flops 12 | bytes 32 | tf_op jit(solution)/shard_map/stack | solution.py:405
  48.6 0.7 %collective-permute-done.9.other = f32[192,128]{1,0:T(8,128)S(1)} collective-permute-done((f32[192,128]{1,0:T(8,128)S(1)}, f32[192,128]{1,0:T(8,128)S(1)}, u32[]{:S(2)}, u32[]{:S(2)}) %collective-permute-start.9) | collective-permute-done | bytes 98336 | tf_op jit(solution)/shard_map/ppermute | solution.py:136
  49.2 0.0 copy-done.5
  49.2 0.6 %copy-done.8 = f32[192,128]{1,0:T(8,128)} copy-done((f32[192,128]{1,0:T(8,128)}, f32[192,128]{1,0:T(8,128)S(1)}, u32[]{:S(2)}) %copy-start.8) | copy-done | bytes 98328
  49.9 2.5 %sweep.1 = f32[32,128]{1,0:T(8,128)} custom-call(s32[4]{0:T(128)} %pad_add_fusion.where, f32[112,128]{1,0:T(8,128)} %get-tuple-element.9.mine, f32[64,128]{1,0:T(8,128)} %get-tuple-element.10.keep, f32[192,128]{1,0:T(8,128)} %copy-done.5, f32[192,128]{1,0:T(8,128)} %copy-done.8, s32[1,32]{1,0:T(1,128)} %bitcast.32), custom_call_target="tpu_custom_call" | custom-call | tf_op jit(solution)/shard_map/sweep/pallas_call | solution.py:406
  (21 shorter events, 0.1 us)
Async XLA Ops:
  0.0 4.3 %copy-start.1 = (bf16[32,32,128]{2,1,0:T(8,128)(2,1)S(1)}, bf16[32,32,128]{2,1,0:T(8,128)(2,1)}, u32[]{:S(2)}) copy-start(bf16[32,32,128]{2,1,0:T(8,128)(2,1)} %film_own.1) | copy-start | bytes 786436
  0.0 10.1 %collective-permute-start.3 = (bf16[32,32,128]{2,1,0:T(8,128)(2,1)}, bf16[32,32,128]{2,1,0:T(8,128)(2,1)S(1)}, u32[]{:S(2)}, u32[]{:S(2)}) collective-permute-start(bf16[32,32,128]{2,1,0:T(8,128)(2,1)} %film_own.1), channel_id=1, source_target_pairs={{0,16},{16,0},{1,17},{17,1},{2,18},{18,2},{3,19},{19,3},{4,20},{20... | collective-permute-start | bytes 786440 | tf_op jit(solution)/shard_map/ppermute | solution.py:136
  4.2 1.3 %collective-permute-start = (bf16[304,128]{1,0:T(8,128)(2,1)S(1)}, bf16[304,128]{1,0:T(8,128)(2,1)S(1)}, u32[]{:S(2)}, u32[]{:S(2)}) collective-permute-start(bf16[304,128]{1,0:T(8,128)(2,1)S(1)} %get-tuple-element.14), channel_id=1, source_target_pairs={{0,16},{16,0},{1,17},{17,1},{2,18},{18,2},{3,19},{19,3},{4,20},{20... | collective-permute-start | bytes 233480 | tf_op jit(solution)/shard_map/ppermute | solution.py:136
  5.5 4.6 %copy-start = (bf16[2,304,128]{2,1,0:T(8,128)(2,1)}, bf16[2,304,128]{2,1,0:T(8,128)(2,1)S(1)}, u32[]{:S(2)}) copy-start(bf16[2,304,128]{2,1,0:T(8,128)(2,1)S(1)} %pad_maximum_fusion.1.own) | copy-start | bytes 466948
  5.5 9.0 %collective-permute-start.1 = (bf16[2,304,128]{2,1,0:T(8,128)(2,1)S(1)}, bf16[2,304,128]{2,1,0:T(8,128)(2,1)S(1)}, u32[]{:S(2)}, u32[]{:S(2)}) collective-permute-start(bf16[2,304,128]{2,1,0:T(8,128)(2,1)S(1)} %pad_maximum_fusion.1.own), channel_id=1, source_target_pairs={{0,1},{1,0},{17,18},{18,17},{2,3},{3,2},{19,20},{20,19},{4,5},{5,4... | collective-permute-start | bytes 466952 | tf_op jit(solution)/shard_map/ppermute | solution.py:145
  10.1 0.7 %copy-start.2 = (bf16[32,32,128]{2,1,0:T(8,128)(2,1)}, bf16[32,32,128]{2,1,0:T(8,128)(2,1)S(1)}, u32[]{:S(2)}) copy-start(bf16[32,32,128]{2,1,0:T(8,128)(2,1)S(1)} %collective-permute-done.3.film_pair) | copy-start | bytes 786436
  10.8 11.1 %collective-permute-start.4 = (bf16[64,16,128]{2,1,0:T(8,128)(2,1)S(1)}, bf16[64,16,128]{2,1,0:T(8,128)(2,1)S(1)}, u32[]{:S(2)}, u32[]{:S(2)}) collective-permute-start(bf16[64,16,128]{2,1,0:T(8,128)(2,1)S(1)} %pad_maximum_fusion), channel_id=1, source_target_pairs={{0,1},{1,0},{17,18},{18,17},{2,3},{3,2},{19,20},{20,19},{4,5},{5,4... | collective-permute-start | bytes 786440 | tf_op jit(solution)/shard_map/ppermute | solution.py:145
  14.5 8.9 %copy-start.6 = (bf16[2,304,128]{2,1,0:T(8,128)(2,1)}, bf16[2,304,128]{2,1,0:T(8,128)(2,1)S(1)}, u32[]{:S(2)}) copy-start(bf16[2,304,128]{2,1,0:T(8,128)(2,1)S(1)} %collective-permute-done.1.direct) | copy-start | bytes 466948
  14.5 7.4 %collective-permute-start.2 = (bf16[2,304,128]{2,1,0:T(8,128)(2,1)S(1)}, bf16[2,304,128]{2,1,0:T(8,128)(2,1)S(1)}, u32[]{:S(2)}, u32[]{:S(2)}) collective-permute-start(bf16[2,304,128]{2,1,0:T(8,128)(2,1)S(1)} %collective-permute-done.1.direct), channel_id=1, source_target_pairs={{0,16},{16,0},{1,17},{17,1},{2,18},{18,2},{3,19},{19,3},{4,20},{20... | collective-permute-start | bytes 466952 | tf_op jit(solution)/shard_map/ppermute | solution.py:136
  21.9 1.5 %copy-start.3 = (bf16[64,16,128]{2,1,0:T(8,128)(2,1)}, bf16[64,16,128]{2,1,0:T(8,128)(2,1)S(1)}, u32[]{:S(2)}) copy-start(bf16[64,16,128]{2,1,0:T(8,128)(2,1)S(1)} %collective-permute-done.4.film_direct) | copy-start | bytes 786436
  21.9 1.5 %collective-permute-start.5 = (bf16[64,16,128]{2,1,0:T(8,128)(2,1)S(1)}, bf16[64,16,128]{2,1,0:T(8,128)(2,1)S(1)}, u32[]{:S(2)}, u32[]{:S(2)}) collective-permute-start(bf16[64,16,128]{2,1,0:T(8,128)(2,1)S(1)} %collective-permute-done.4.film_direct), channel_id=1, source_target_pairs={{0,16},{16,0},{1,17},{17,1},{2,18},{18,2},{3,19},{19,3},{4,20},{20... | collective-permute-start | bytes 786440 | tf_op jit(solution)/shard_map/ppermute | solution.py:136
  21.9 1.5 %copy-start.7 = (bf16[2,304,128]{2,1,0:T(8,128)(2,1)}, bf16[2,304,128]{2,1,0:T(8,128)(2,1)S(1)}, u32[]{:S(2)}) copy-start(bf16[2,304,128]{2,1,0:T(8,128)(2,1)S(1)} %collective-permute-done.2.other) | copy-start | bytes 466948
  23.4 0.7 %copy-start.4 = (bf16[64,16,128]{2,1,0:T(8,128)(2,1)}, bf16[64,16,128]{2,1,0:T(8,128)(2,1)S(1)}, u32[]{:S(2)}) copy-start(bf16[64,16,128]{2,1,0:T(8,128)(2,1)S(1)} %collective-permute-done.5.film_other) | copy-start | bytes 786436
  34.9 11.0 %collective-permute-start.6 = (f32[112,128]{1,0:T(8,128)}, f32[112,128]{1,0:T(8,128)S(1)}, u32[]{:S(2)}, u32[]{:S(2)}) collective-permute-start(f32[112,128]{1,0:T(8,128)} %get-tuple-element.9.mine), channel_id=1, source_target_pairs={{0,1},{1,0},{17,18},{18,17},{2,3},{3,2},{19,20},{20,19},{4,5},{5,4... | collective-permute-start | bytes 172040 | tf_op jit(solution)/shard_map/ppermute | solution.py:145
  37.8 4.1 %copy-start.9 = (f32[64,128]{1,0:T(8,128)S(1)}, f32[64,128]{1,0:T(8,128)}, u32[]{:S(2)}) copy-start(f32[64,128]{1,0:T(8,128)} %get-tuple-element.11) | copy-start | bytes 98308
  37.9 0.7 %copy-start.10 = (f32[16,128]{1,0:T(8,128)S(1)}, f32[16,128]{1,0:T(8,128)}, u32[]{:S(2)}) copy-start(f32[16,128]{1,0:T(8,128)} %get-tuple-element.12) | copy-start | bytes 24580
  38.6 9.3 %collective-permute-start.8 = (f32[16,128]{1,0:T(8,128)S(1)}, f32[16,128]{1,0:T(8,128)S(1)}, u32[]{:S(2)}, u32[]{:S(2)}) collective-permute-start(f32[16,128]{1,0:T(8,128)S(1)} %copy-done.10), channel_id=1, source_target_pairs={{0,3},{3,0},{1,4},{4,1},{2,5},{5,2},{19,22},{22,19},{20,23},{23,20... | collective-permute-start | bytes 24584 | tf_op jit(solution)/shard_map/ppermute | solution.py:145
  41.9 5.9 %collective-permute-start.7 = (f32[64,128]{1,0:T(8,128)S(1)}, f32[64,128]{1,0:T(8,128)S(1)}, u32[]{:S(2)}, u32[]{:S(2)}) collective-permute-start(f32[64,128]{1,0:T(8,128)S(1)} %copy-done.9), channel_id=1, source_target_pairs={{0,2},{2,0},{1,3},{3,1},{18,20},{20,18},{19,21},{21,19},{4,6},{6,4... | collective-permute-start | bytes 98312 | tf_op jit(solution)/shard_map/ppermute | solution.py:145
  47.8 1.4 %copy-start.5 = (f32[192,128]{1,0:T(8,128)}, f32[192,128]{1,0:T(8,128)S(1)}, u32[]{:S(2)}) copy-start(f32[192,128]{1,0:T(8,128)S(1)} %constant_dynamic-update-slice_fusion.direct) | copy-start | bytes 294916
  47.8 1.4 %collective-permute-start.9 = (f32[192,128]{1,0:T(8,128)S(1)}, f32[192,128]{1,0:T(8,128)S(1)}, u32[]{:S(2)}, u32[]{:S(2)}) collective-permute-start(f32[192,128]{1,0:T(8,128)S(1)} %constant_dynamic-update-slice_fusion.direct), channel_id=1, source_target_pairs={{0,16},{16,0},{1,17},{17,1},{2,18},{18,2},{3,19},{19,3},{4,20},{20... | collective-permute-start | bytes 294920 | tf_op jit(solution)/shard_map/ppermute | solution.py:136
  49.2 0.6 %copy-start.8 = (f32[192,128]{1,0:T(8,128)}, f32[192,128]{1,0:T(8,128)S(1)}, u32[]{:S(2)}) copy-start(f32[192,128]{1,0:T(8,128)S(1)} %collective-permute-done.9.other) | copy-start | bytes 294916

commit v2 on v1

--- a/solution.py
+++ b/solution.py
@@ -1,5 +1,3 @@
-import functools
-
 import jax
 import jax.numpy as jnp
 from jax import lax
@@ -132,56 +130,100 @@
     return result[None, None]
 
 
+OFFSETS = (
+    ((-1, -3, 3, 1), (3, 1, -1, -3)),
+    ((-2, -2, 2, 2), (-3, 3, -3, 3)),
+    ((1, -1, 1, -1), (2, 2, -2, -2)),
+)
+BESIDE = ((1, -1, 1, -1), (-1, 1, -1, 1))
+UNROLL = 4
+
+
 def swap(x):
     return lax.ppermute(x, "ty", [(0, 1), (1, 0)])
 
 
-def pairwise(x, step):
+def pairwise(x, offsets):
     count = lax.axis_size("tx")
     pairs = []
-    for i in range(count - step):
-        base = count * ((i // step) % 2)
-        pairs += [(base + i, base + i + step), (base + i + step, base + i)]
+    for core, steps in enumerate(offsets):
+        for i in range(count):
+            other = i + steps[i % 4]
+            if 0 <= other < count:
+                pairs.append((core * count + i, core * count + other))
     return lax.ppermute(x, ("ty", "tx"), pairs)
 
 
-def upward(step):
-    column = lax.axis_index("tx")
-    return (((column // step) % 2) == lax.axis_index("ty")).astype(jnp.int32)
-
-
-def near_kernel(
-    slots, meta, own, direct, other, film_own, film_pair, film_direct, film_other,
-    far1, far2, far3, keep, patches, trails, canvas, start, film,
+def partner(offsets):
+    core = lax.axis_index("ty")
+    place = lax.axis_index("tx") & 3
+    picked = []
+    for steps in offsets:
+        step = jnp.int32(steps[3])
+        for i in range(3):
+            step = jnp.where(place == i, steps[i], step)
+        picked.append(step)
+    return jnp.where(core == 0, picked[0], picked[1]), jnp.where(core == 0, picked[1], picked[0])
+
+
+def pack_kernel(footprints, traces, order, centres, counts, packed, numbers):
+    slots, width = footprints.shape
+    numbers[...] = jnp.zeros_like(numbers)
+    numbers[0:1, 0:slots] = order[...].astype(jnp.float32)
+    numbers[1:3, 0:slots] = centres[...].astype(jnp.float32)
+    numbers[3:4, 0:1] = counts[...].astype(jnp.float32)
+    packed[:, :width] = footprints[...]
+    packed[:, width:width + LANES] = traces[...]
+    packed[:, width + LANES:] = numbers[...].astype(jnp.bfloat16)
+
+
+def paint_kernel(
+    own, direct, other, mine, links, scale, begin, coupling,
+    patches, trails, canvas, start, numbers, meta, sem,
 ):
+    slots = own.shape[1]
     tiles = 6
-    total = 6 * slots
+    total = tiles * slots
     block = slots // BLOCKS
     group = 2 * block
     source = 3 * group
     pixels = PATCH * PATCH // LANES
+    width = pixels * LANES
     depth = canvas.shape[0] // total
     sources = ((own, 0), (own, 1), (direct, 0), (direct, 1), (other, 0), (other, 1))
 
+    for t, (ref, u) in enumerate(sources):
+        numbers[t * 8:(t + 1) * 8, :] = (
+            ref[u, 0:16, width + LANES:].astype(jnp.float32)[0:8].astype(jnp.int32)
+        )
+    fetch = pltpu.make_async_copy(numbers, meta, sem)
+    fetch.start()
     canvas[...] = jnp.zeros_like(canvas)
     for t, (ref, u) in enumerate(sources):
-        rows = slots * pixels
-        patches[t * rows:(t + 1) * rows, :] = ref[u, :rows, :].astype(jnp.float32)
-        trails[t * slots:(t + 1) * slots, :] = ref[u, rows:rows + slots, :].astype(jnp.float32)
+        for k in range(pixels):
+            patches[pl.ds(t * slots * pixels + k, slots, stride=pixels), :] = ref[
+                u, :, k * LANES:(k + 1) * LANES
+            ].astype(jnp.float32)
+        trails[t * slots:(t + 1) * slots, :] = ref[u, :, width:width + LANES].astype(jnp.float32)
+    fetch.wait()
 
     lane = lax.broadcasted_iota(jnp.int32, (pixels, LANES), 1)
     sub = lax.broadcasted_iota(jnp.int32, (pixels, LANES), 0)
     low = lane < LANES // 2
     inner = lane & (LANES // 2 - 1)
+    core = lax.axis_index("ty")
+    step_direct, step_other = partner(BESIDE)
+    tile_rows = (core, 1 - core, core, 1 - core, 1 - core, core)
+    tile_cols = (0, 0, step_direct, step_direct, step_other, step_other)
 
     def paint(t, s):
-        a = meta[t, 3 * slots + 1]
-        j = meta[t, 3 * slots + 2]
-        p = meta[t, s]
-        live = (p < meta[t, 3 * slots]).astype(jnp.int32)
-        top = a * PATCH + meta[t, slots + p]
-        left = meta[t, 2 * slots + p] + (j - 1) * PATCH
-        slot = (s // block) * source + j * group + a * block + s % block
+        p = meta[t * 8, s]
+        live = (p < meta[t * 8 + 3, 0]).astype(jnp.int32)
+        top = tile_rows[t] * PATCH + meta[t * 8 + 1, p]
+        left = meta[t * 8 + 2, p] + tile_cols[t] * PATCH
+        slot = (
+            (s // block) * source + (tile_cols[t] + 1) * group + tile_rows[t] * block + s % block
+        )
         odd = top & 1
         level = top // 2
         value = patches[pl.ds(pl.multiple_of((t * slots + p) * pixels, pixels), pixels), :]
@@ -205,45 +247,23 @@
             for k in range(UNROLL):
                 paint(t, step * UNROLL + k)
 
-    height = film_own.shape[0]
-    half = PATCH // 2
-    row0 = pl.multiple_of(meta[0, 3 * slots + 1] * height, height)
-    row1 = pl.multiple_of(meta[1, 3 * slots + 1] * height, height)
-    film[pl.ds(row0, height), half:half + PATCH, :] = film_own[...]
-    film[pl.ds(row1, height), half:half + PATCH, :] = film_pair[...]
-    for t, ref in ((2, film_direct), (4, film_other)):
-        for u in range(2):
-            row = pl.multiple_of(meta[t + u, 3 * slots + 1] * height, height)
-            part = ref[u * height:(u + 1) * height]
-            side = meta[t + u, 3 * slots + 2]
-
-            @pl.when(side == 0)
-            def _():
-                film[pl.ds(row, height), 0:half, :] = part
-
-            @pl.when(side != 0)
-            def _():
-                film[pl.ds(row, height), half + PATCH:2 * PATCH, :] = part
-
     margins = jnp.zeros((2 * slots, total), jnp.float32)
-    drive = jnp.zeros((2 * slots, film.shape[2]), jnp.float32)
-    edge = half // 4
+    edge = PATCH // 8
     for step in range(depth // 2):
         at = 2 * step * total
         painted = jnp.concatenate(
             [canvas[at:at + total, :], canvas[at + total:at + 2 * total, :]], axis=1
         ).astype(jnp.bfloat16)
-        mine = jnp.concatenate(
+        targets = jnp.concatenate(
             [painted[q * source + group:q * source + 2 * group] for q in range(BLOCKS)], axis=0
         )
         margins += lax.dot_general(
-            mine, painted, (((1,), (1,)), ((), ())), preferred_element_type=jnp.float32
+            targets, painted, (((1,), (1,)), ((), ())), preferred_element_type=jnp.float32
         )
         if edge <= step < depth // 2 - edge:
-            pixels_here = film[(step - edge) * 4:(step - edge) * 4 + 4].reshape(2 * LANES, -1)
-            drive += jnp.dot(mine, pixels_here, preferred_element_type=jnp.float32)
-
-    coupling = jnp.dot(
+            mine[step - edge] = targets
+
+    coupling[...] = jnp.dot(
         margins, start[...], precision=precise, preferred_element_type=jnp.float32
     )
     line = lax.broadcasted_iota(jnp.int32, margins.shape, 0)
@@ -251,43 +271,78 @@
     matching = column == (line // group) * source + group + line % group
     diagonal = jnp.sum(jnp.where(matching, margins, 0.0), axis=1, keepdims=True)
     diagonal = jnp.where(diagonal > 0.0, diagonal, 1.0)
-    begin = jnp.concatenate(
-        [start[q * source + group:q * source + 2 * group, :] for q in range(BLOCKS)], axis=0
-    )
-    level = begin + (drive - coupling) / diagonal
+    scale[...] = jnp.broadcast_to(diagonal, scale.shape)
+    for q in range(BLOCKS):
+        begin[q * group:(q + 1) * group, :] = start[q * source + group:q * source + 2 * group, :]
     share = margins / diagonal
+    for i, q in enumerate((1, 2, 3)):
+        links[i * group:(i + 1) * group, :] = share[q * group:(q + 1) * group, :LANES]
+    links[3 * group:4 * group, :total - LANES] = share[3 * group:4 * group, LANES:]
+
+
+def drive_kernel(
+    mine, links, scale, begin, coupling, film_own, film_pair, film_direct, film_other,
+    far, far_short, keep, film,
+):
+    core = lax.axis_index("ty")
+    side_direct, side_other = partner(BESIDE)
+    height = film_own.shape[0]
+    half = PATCH // 2
+    group = links.shape[0] // 4
+
+    def row_of(a):
+        return pl.ds(pl.multiple_of(a * height, height), height)
+
+    film[row_of(core), half:half + PATCH, :] = film_own[...]
+    film[row_of(1 - core), half:half + PATCH, :] = film_pair[...]
+    for ref, side, nearest in ((film_direct, side_direct, core), (film_other, side_other, 1 - core)):
+        for u in range(2):
+            row = row_of(nearest if u == 0 else 1 - nearest)
+            part = ref[u * height:(u + 1) * height]
+
+            @pl.when(side < 0)
+            def _():
+                film[row, 0:half, :] = part
+
+            @pl.when(side >= 0)
+            def _():
+                film[row, half + PATCH:2 * PATCH, :] = part
+
+    drive = jnp.zeros(coupling.shape, jnp.float32)
+    for step in range(mine.shape[0]):
+        pixels_here = film[step * 4:(step + 1) * 4].reshape(mine.shape[2], -1)
+        drive += jnp.dot(mine[step], pixels_here, preferred_element_type=jnp.float32)
+    level = begin[...] + (drive - coupling[...]) / scale[...]
 
     def rows_of(x, q):
         return x[q * group:(q + 1) * group]
 
     first = jnp.maximum(rows_of(level, 0), 0.0)
-    change = first - rows_of(begin, 0)
+    change = first - begin[0:group, :]
     pieces = (
         change,
-        rows_of(level, 1), rows_of(begin, 1), rows_of(share, 1)[:, :LANES],
-        rows_of(level, 2), rows_of(begin, 2), rows_of(share, 2)[:, :LANES],
-    )
-    for ref in (far1, far2, far3):
+        rows_of(level, 1), begin[group:2 * group, :], links[0:group, :],
+        rows_of(level, 2), begin[2 * group:3 * group, :], links[group:2 * group, :],
+    )
+    for ref in (far, far_short):
         for i in range(ref.shape[0] // group):
             ref[i * group:(i + 1) * group, :] = pieces[i]
     keep[0:group, :] = first
     keep[group:2 * group, :] = rows_of(level, 3)
-    keep[2 * group:3 * group, :] = rows_of(share, 3)[:, :LANES]
-    keep[3 * group:4 * group, :total - LANES] = rows_of(share, 3)[:, LANES:]
-
-
-def sweep_kernel(slots, where, mine, keep, direct, other, order, out, box, current):
+    keep[2 * group:4 * group, :] = links[2 * group:4 * group, :]
+
+
+def sweep_kernel(mine, keep, direct, other, order, out, box, current):
+    slots = out.shape[0]
     block = slots // BLOCKS
     group = 2 * block
     reach = BLOCKS - 1
-    sizes = (7 * group, 4 * group, group)
     box[reach] = mine[...]
     at = 0
-    for step in range(1, BLOCKS):
-        size = sizes[step - 1]
-        up = where[step]
-        box[reach - step + 2 * step * up, 0:size, :] = direct[at:at + size, :]
-        box[reach + step - 2 * step * up, 0:size, :] = other[at:at + size, :]
+    for offsets, size in zip(OFFSETS, (7 * group, 4 * group, 7 * group)):
+        step_direct, step_other = partner(offsets)
+        box[reach + step_direct, 0:size, :] = direct[at:at + size, :]
+        box[reach + step_other, 0:size, :] = other[at:at + size, :]
         at += size
 
     def exact(a, b):
@@ -322,7 +377,7 @@
     current[3 * group:4 * group, :] = jnp.maximum(
         keep[group:2 * group, :] - exact(share, near), 0.0
     )
-    row = pl.multiple_of(where[0] * block, block)
+    row = pl.multiple_of(lax.axis_index("ty") * block, block)
     ordered = jnp.concatenate(
         [current[pl.ds(q * group + row, block), :] for q in range(BLOCKS)], axis=0
     )
@@ -330,90 +385,98 @@
     out[...] = exact(place.astype(jnp.float32), ordered)
 
 
-UNROLL = 4
+def call(kernel, outs, scratch, megabytes, name):
+    vmem = pl.BlockSpec(memory_space=pltpu.VMEM)
+
+    def run(*operands):
+        return pl.pallas_call(
+            kernel,
+            out_shape=[jax.ShapeDtypeStruct(*out) for out in outs],
+            in_specs=[vmem] * len(operands),
+            out_specs=[vmem] * len(outs),
+            scratch_shapes=scratch,
+            compiler_params=pltpu.CompilerParams(vmem_limit_bytes=megabytes << 20),
+            name=name,
+        )(*operands)
+
+    return run
 
 
 def strip_body(movie, footprints, centres, traces, counts, order):
     height, width, frames = movie.shape
     slots = footprints.shape[2]
+    area = footprints.shape[3]
     half = PATCH // 2
     group = 2 * slots // BLOCKS
-    bf16 = jnp.bfloat16
-    core = lax.axis_index("ty")
-    up = [upward(step) for step in range(1, BLOCKS)]
-
-    numbers = jnp.concatenate(
-        [order[0, 0], centres[0, 0, :, 0], centres[0, 0, :, 1], counts[0]]
-    ).astype(bf16)
-    numbers = jnp.pad(numbers[None], ((0, 15), (0, LANES - numbers.shape[0])))
-    packed = jnp.concatenate(
-        [footprints[0, 0].reshape(-1, LANES), traces[0, 0], numbers], axis=0
-    )
-    pair_packed = swap(packed)
+    total = 6 * slots
+    bf16, f32 = jnp.bfloat16, jnp.float32
+
     pair_movie = swap(movie)
-    both = jnp.stack([packed, pair_packed])
-    direct = pairwise(both, 1)
-    edge = half * up[0]
+    (packed,) = call(
+        pack_kernel,
+        [((slots, area + 2 * LANES), bf16)],
+        [pltpu.VMEM((slots, LANES), f32)],
+        4,
+        "pack",
+    )(footprints[0, 0], traces[0, 0], order[0], centres[0, 0].T, counts)
+    own = jnp.stack([packed, swap(packed)])
+    direct = pairwise(own, BESIDE)
+    edge = jnp.where(partner(BESIDE)[0] > 0, half, 0)
     edges = jnp.concatenate(
+        [lax.dynamic_slice_in_dim(x, edge, half, axis=1) for x in (movie, pair_movie)], axis=0
+    )
+    film_direct = pairwise(edges, BESIDE)
+    other = swap(direct)
+    film_other = swap(film_direct)
+
+    canvas_rows = (2 * height + PATCH) // 2
+    painted = call(
+        paint_kernel,
         [
-            lax.dynamic_slice_in_dim(movie, edge, half, axis=1),
-            lax.dynamic_slice_in_dim(pair_movie, edge, half, axis=1),
+            ((height // 2, 2 * slots, 2 * LANES), bf16),
+            ((4 * group, LANES), f32),
+            ((2 * slots, frames), f32),
+            ((2 * slots, frames), f32),
+            ((2 * slots, frames), f32),
+        ],
+        [
+            pltpu.VMEM((total * area // LANES, LANES), f32),
+            pltpu.VMEM((total, frames), f32),
+            pltpu.VMEM((canvas_rows * total, LANES), f32),
+            pltpu.VMEM((total, frames), f32),
+            pltpu.VMEM((48, LANES), jnp.int32),
+            pltpu.SMEM((48, LANES), jnp.int32),
+            pltpu.SemaphoreType.DMA,
+        ],
+        16,
+        "paint",
+    )(own, direct, other)
+    far, far_short, keep = call(
+        drive_kernel,
+        [((7 * group, frames), f32), ((4 * group, frames), f32), ((4 * group, frames), f32)],
+        [pltpu.VMEM((2 * height, 2 * PATCH, frames), bf16)],
+        8,
+        "drive",
+    )(*painted, movie, pair_movie, film_direct, film_other)
+
+    came = jnp.concatenate(
+        [
+            pairwise(far, OFFSETS[0]),
+            pairwise(far_short, OFFSETS[1]),
+            pairwise(far, OFFSETS[2]),
         ],
         axis=0,
     )
-    film_direct = pairwise(edges, 1)
-    other = swap(direct)
-    film_other = swap(film_direct)
-
-    line = packed.shape[0] - 16
-    meta = jnp.concatenate([both[:, line], direct[:, line], other[:, line]], axis=0)
-    rows = jnp.stack([core, 1 - core, core, 1 - core, 1 - core, core])
-    sides = jnp.stack([1, 1, 2 * up[0], 2 * up[0], 2 - 2 * up[0], 2 - 2 * up[0]])
-    lanes = jnp.arange(LANES)[None]
-    meta = jnp.where(
-        lanes == 3 * slots + 1,
-        rows[:, None],
-        jnp.where(lanes == 3 * slots + 2, sides[:, None], meta.astype(jnp.int32)),
-    ).astype(jnp.int32)
-
-    vmem = pl.BlockSpec(memory_space=pltpu.VMEM)
-    smem = pl.BlockSpec(memory_space=pltpu.SMEM)
-    f32 = jnp.float32
-    depth = (2 * height + PATCH) // 2
-    far1, far2, far3, keep = pl.pallas_call(
-        functools.partial(near_kernel, slots),
-        out_shape=[
-            jax.ShapeDtypeStruct((7 * group, frames), f32),
-            jax.ShapeDtypeStruct((4 * group, frames), f32),
-            jax.ShapeDtypeStruct((group, frames), f32),
-            jax.ShapeDtypeStruct((4 * group, frames), f32),
-        ],
-        in_specs=[smem] + [vmem] * 7,
-        out_specs=[vmem] * 4,
-        scratch_shapes=[
-            pltpu.VMEM((6 * slots * PATCH * PATCH // LANES, LANES), f32),
-            pltpu.VMEM((6 * slots, frames), f32),
-            pltpu.VMEM((depth * 6 * slots, LANES), f32),
-            pltpu.VMEM((6 * slots, frames), f32),
-            pltpu.VMEM((2 * height, 2 * PATCH, frames), bf16),
-        ],
-        name="near",
-    )(meta, both, direct, other, movie, pair_movie, film_direct, film_other)
-
-    far = jnp.concatenate([pairwise(far1, 1), pairwise(far2, 2), pairwise(far3, 3)], axis=0)
-    far_other = swap(far)
-    where = jnp.stack([core] + up).astype(jnp.int32)
-    result = pl.pallas_call(
-        functools.partial(sweep_kernel, slots),
-        out_shape=jax.ShapeDtypeStruct((slots, frames), f32),
-        in_specs=[smem] + [vmem] * 5,
-        out_specs=vmem,
-        scratch_shapes=[
+    (result,) = call(
+        sweep_kernel,
+        [((slots, frames), f32)],
+        [
             pltpu.VMEM((2 * BLOCKS - 1, 7 * group, frames), f32),
             pltpu.VMEM((4 * group, frames), f32),
         ],
-        name="sweep",
-    )(where, far1, keep, far, far_other, order[0])
+        4,
+        "sweep",
+    )(far, keep, came, swap(came), order[0])
     return result[None, None]
 
 

time: 52.8 us -> 44.5 us (0.84)
  the two profiles are of different devices: /device:TPU:0 before, /device:TPU:7 now
where the time goes in v2:
time: 44.5 us; the launch traced here: 44.2 us
  starting transfers between devices  24.6 us (55%)
  Pallas kernels  10.3 us (23%)
  waiting for transfers between devices  5.26 us (12%)
  local copies, waits for them, and re-layouts  3.12 us (7%)
  between operations  0.84 us (2%)
    ppermute x5, starting transfers between devices, pairwise(): return lax.ppermute(x, ('ty', 'tx'), pairs)  14.7 us
    pallas_call x4, Pallas kernels, run(): pl.pallas_call(kernel, out_shape=[jax.ShapeDtypeStruct(*out) for out in o...  10.3 us
    ppermute x5, starting transfers between devices, swap(): return lax.ppermute(x, 'ty', [(0, 1), (1, 0)])  9.83 us
    ppermute x5, waiting for transfers between devices, pairwise(): return lax.ppermute(x, ('ty', 'tx'), pairs)  3.21 us
    unnamed x12, local copies, waits for them, and re-layouts  2.18 us
    ppermute x5, waiting for transfers between devices, swap(): return lax.ppermute(x, 'ty', [(0, 1), (1, 0)])  2.04 us
    dynamic_slice x2, local copies, waits for them, and re-layouts, strip_body(): lax.dynamic_slice_in_dim(x, edge, half, axis=1)  0.94 us
  transfers between devices with their start and end apart: 10, of which 4 were waited for; matrix products, arithmetic and copies ran while one was open for 2% of the time, Pallas kernels for 19%

profile of v2, /device:TPU:7, one launch (start us, length us, event | category | flops | bytes accessed | tf_op | source)
XLA Modules:
  0.0 44.2 jit_solution(6216311828532022194)
XLA Ops:
  0.0 0.0 copy-start.2
  0.0 0.7 %collective-permute-start.3 = (bf16[32,32,128]{2,1,0:T(8,128)(2,1)}, bf16[32,32,128]{2,1,0:T(8,128)(2,1)S(1)}, u32[]{:S(2)}, u32[]{:S(2)}) collective-permute-start(bf16[32,32,128]{2,1,0:T(8,128)(2,1)} %film_own.1), channel_id=1, source_target_pairs={{0,16},{16,0},{1,17},{17,1},{2,18},{18,2},{3,19},{19,3},{4,20},{20... | collective-permute-start | bytes 786440 | tf_op jit(solution)/shard_map/ppermute | solution.py:143
  1.3 0.0 copy-start.3
  1.3 0.0 copy-done.2
  1.3 0.6 %copy-done.3 = s32[1,1,32]{2,1,0:T(1,128)S(1)} copy-done((s32[1,1,32]{2,1,0:T(1,128)S(1)}, s32[1,1,32]{2,1,0:T(1,128)}, u32[]{:S(2)}) %copy-start.3) | copy-done | bytes 152
  2.0 0.0 copy-start.1
  2.0 0.8 %copy-done.1 = bf16[1,1,32,1024]{3,2,1,0:T(8,128)(2,1)S(1)} copy-done((bf16[1,1,32,1024]{3,2,1,0:T(8,128)(2,1)S(1)}, bf16[1,1,32,1024]{3,2,1,0:T(8,128)(2,1)}, u32[]{:S(2)}) %copy-start.1) | copy-done | bytes 65560
  2.8 0.0 copy-start.4
  2.8 0.7 %copy-done.4 = s32[1,1,32,2]{2,3,1,0:T(2,128)S(1)} copy-done((s32[1,1,32,2]{2,3,1,0:T(2,128)S(1)}, s32[1,1,32,2]{2,3,1,0:T(2,128)}, u32[]{:S(2)}) %copy-start.4) | copy-done | bytes 280
  3.5 0.1 collective-permute-start
  3.6 0.9 %constant_dynamic-slice_fusion.1 = bf16[32,16,128]{2,1,0:T(8,128)(2,1)S(1)} fusion(bf16[32,32,128]{2,1,0:T(8,128)(2,1)} %film_own.1, s32[]{:T(128)S(6)} %select_n.36), kind=kLoop, calls=%fused_computation.6 | loop fusion | bytes 262148 | tf_op jit(solution)/shard_map/dynamic_slice | solution.py:426
  4.6 0.0 collective-permute-done.3.film_pair
  4.6 3.1 %collective-permute-start.4 = (bf16[64,16,128]{2,1,0:T(8,128)(2,1)S(1)}, bf16[64,16,128]{2,1,0:T(8,128)(2,1)S(1)}, u32[]{:S(2)}, u32[]{:S(2)}) collective-permute-start(bf16[64,16,128]{2,1,0:T(8,128)(2,1)S(1)} %pad_maximum_fusion), channel_id=1, source_target_pairs={{0,1},{1,0},{2,3},{3,2},{4,5},{5,4},{6,7},{7,6},{8,9},{9,8},{10,11... | collective-permute-start | bytes 786440 | tf_op jit(solution)/shard_map/ppermute | solution.py:154
  7.8 0.0 collective-permute-done
  7.8 0.0 copy-start
  7.8 4.1 %collective-permute-start.1 = (bf16[2,32,1280]{2,1,0:T(8,128)(2,1)S(1)}, bf16[2,32,1280]{2,1,0:T(8,128)(2,1)S(1)}, u32[]{:S(2)}, u32[]{:S(2)}) collective-permute-start(bf16[2,32,1280]{2,1,0:T(8,128)(2,1)S(1)} %pad_maximum_fusion.1.own), channel_id=1, source_target_pairs={{0,1},{1,0},{2,3},{3,2},{4,5},{5,4},{6,7},{7,6},{8,9},{9,8},{10,11... | collective-permute-start | bytes 491528 | tf_op jit(solution)/shard_map/ppermute | solution.py:154
  11.9 1.7 %collective-permute-done.4.film_direct = bf16[64,16,128]{2,1,0:T(8,128)(2,1)S(1)} collective-permute-done((bf16[64,16,128]{2,1,0:T(8,128)(2,1)S(1)}, bf16[64,16,128]{2,1,0:T(8,128)(2,1)S(1)}, u32[]{:S(2)}, u32[]{:S(2)}) %collective-permute-start.4) | collective-permute-done | bytes 262176 | tf_op jit(solution)/shard_map/ppermute | solution.py:154
  13.6 2.5 %collective-permute-start.5 = (bf16[64,16,128]{2,1,0:T(8,128)(2,1)S(1)}, bf16[64,16,128]{2,1,0:T(8,128)(2,1)S(1)}, u32[]{:S(2)}, u32[]{:S(2)}) collective-permute-start(bf16[64,16,128]{2,1,0:T(8,128)(2,1)S(1)} %collective-permute-done.4.film_direct), channel_id=1, source_target_pairs={{0,16},{16,0},{1,17},{17,1},{2,18},{18,2},{3,19},{19,3},{4,20},{20... | collective-permute-start | bytes 786440 | tf_op jit(solution)/shard_map/ppermute | solution.py:143
  16.2 0.0 collective-permute-done.1.direct
  16.2 2.5 %collective-permute-start.2 = (bf16[2,32,1280]{2,1,0:T(8,128)(2,1)S(1)}, bf16[2,32,1280]{2,1,0:T(8,128)(2,1)S(1)}, u32[]{:S(2)}, u32[]{:S(2)}) collective-permute-start(bf16[2,32,1280]{2,1,0:T(8,128)(2,1)S(1)} %collective-permute-done.1.direct), channel_id=1, source_target_pairs={{0,16},{16,0},{1,17},{17,1},{2,18},{18,2},{3,19},{19,3},{4,20},{20... | collective-permute-start | bytes 491528 | tf_op jit(solution)/shard_map/ppermute | solution.py:143
  18.7 1.0 %collective-permute-done.2.other = bf16[2,32,1280]{2,1,0:T(8,128)(2,1)S(1)} collective-permute-done((bf16[2,32,1280]{2,1,0:T(8,128)(2,1)S(1)}, bf16[2,32,1280]{2,1,0:T(8,128)(2,1)S(1)}, u32[]{:S(2)}, u32[]{:S(2)}) %collective-permute-start.2) | collective-permute-done | bytes 163872 | tf_op jit(solution)/shard_map/ppermute | solution.py:143
  19.7 8.4 %paint.1 = (bf16[16,64,256]{2,1,0:T(8,128)(2,1)S(1)}, f32[64,128]{1,0:T(8,128)S(1)}, f32[64,128]{1,0:T(8,128)S(1)}, f32[64,128]{1,0:T(8,128)S(1)}, f32[64,128]{1,0:T(8,128)S(1)}) custom-call(bf16[2,32,1280]{2,1,0:T(8,128)(2,1)S(1)} %pad_maximum_fusion.1.own, bf16[2,32,1280]{2,1,0:T(8,128)(2,1)S(1)} %collective-permute-done.1.direct, ...), custom_call_target="tpu_custom_call" | custom-call | tf_op jit(solution)/shard_map/paint/pallas_call | solution.py:392
  28.1 0.0 collective-permute-done.5.film_other
  28.1 0.0 copy-done
  28.1 0.5 %drive.1 = (f32[112,128]{1,0:T(8,128)S(1)}, f32[64,128]{1,0:T(8,128)S(1)}, f32[64,128]{1,0:T(8,128)S(1)}) custom-call(bf16[16,64,256]{2,1,0:T(8,128)(2,1)S(1)} %get-tuple-element.13.mine, f32[64,128]{1,0:T(8,128)S(1)} %get-tuple-element.14.links, f32[64,128]{1,0:T(8,128)S(1)} %get-tuple-element.15.scale, f32[64,128]{1,0:T(8,128)S(1)} %get-tuple-element.16.begin, ...), custom_call_target="tpu_custom_call" | custom-call | tf_op jit(solution)/shard_map/drive/pallas_call | solution.py:392
  28.6 2.1 %collective-permute-start.6 = (f32[112,128]{1,0:T(8,128)S(1)}, f32[112,128]{1,0:T(8,128)S(1)}, u32[]{:S(2)}, u32[]{:S(2)}) collective-permute-start(f32[112,128]{1,0:T(8,128)S(1)} %get-tuple-element.18.mine), channel_id=1, source_target_pairs={{2,5},{3,4},{4,3},{5,2},{6,9},{7,8},{8,7},{9,6},{10,13},{11,12},{1... | collective-permute-start | bytes 172040 | tf_op jit(solution)/shard_map/ppermute | solution.py:154
  30.7 1.4 %collective-permute-start.8 = (f32[112,128]{1,0:T(8,128)S(1)}, f32[112,128]{1,0:T(8,128)S(1)}, u32[]{:S(2)}, u32[]{:S(2)}) collective-permute-start(f32[112,128]{1,0:T(8,128)S(1)} %get-tuple-element.18.mine), channel_id=1, source_target_pairs={{0,1},{1,0},{2,3},{3,2},{4,5},{5,4},{6,7},{7,6},{8,9},{9,8},{10,11... | collective-permute-start | bytes 172040 | tf_op jit(solution)/shard_map/ppermute | solution.py:154
  32.1 4.0 %collective-permute-start.7 = (f32[64,128]{1,0:T(8,128)S(1)}, f32[64,128]{1,0:T(8,128)S(1)}, u32[]{:S(2)}, u32[]{:S(2)}) collective-permute-start(f32[64,128]{1,0:T(8,128)S(1)} %get-tuple-element.20), channel_id=1, source_target_pairs={{2,4},{3,5},{4,2},{5,3},{6,8},{7,9},{8,6},{9,7},{10,12},{11,13},{1... | collective-permute-start | bytes 98312 | tf_op jit(solution)/shard_map/ppermute | solution.py:154
  36.2 0.0 collective-permute-done.6
  36.2 1.5 %collective-permute-done.7 = f32[64,128]{1,0:T(8,128)S(1)} collective-permute-done((f32[64,128]{1,0:T(8,128)S(1)}, f32[64,128]{1,0:T(8,128)S(1)}, u32[]{:S(2)}, u32[]{:S(2)}) %collective-permute-start.7) | collective-permute-done | bytes 32800 | tf_op jit(solution)/shard_map/ppermute | solution.py:154
  37.7 0.0 collective-permute-done.8
  37.7 4.0 %collective-permute-start.9 = (f32[288,128]{1,0:T(8,128)S(1)}, f32[288,128]{1,0:T(8,128)S(1)}, u32[]{:S(2)}, u32[]{:S(2)}) collective-permute-start(f32[288,128]{1,0:T(8,128)S(1)} %constant_dynamic-update-slice_fusion.direct), channel_id=1, source_target_pairs={{0,16},{16,0},{1,17},{17,1},{2,18},{18,2},{3,19},{19,3},{4,20},{20... | collective-permute-start | bytes 442376 | tf_op jit(solution)/shard_map/ppermute | solution.py:143
  41.7 1.0 %collective-permute-done.9.other = f32[288,128]{1,0:T(8,128)S(1)} collective-permute-done((f32[288,128]{1,0:T(8,128)S(1)}, f32[288,128]{1,0:T(8,128)S(1)}, u32[]{:S(2)}, u32[]{:S(2)}) %collective-permute-start.9) | collective-permute-done | bytes 147488 | tf_op jit(solution)/shard_map/ppermute | solution.py:143
  42.7 1.5 %sweep.1 = f32[32,128]{1,0:T(8,128)} custom-call(f32[112,128]{1,0:T(8,128)S(1)} %get-tuple-element.18.mine, f32[64,128]{1,0:T(8,128)S(1)} %get-tuple-element.19.keep, f32[288,128]{1,0:T(8,128)S(1)} %constant_dynamic-update-slice_fusion.direct, f32[288,128]{1,0:T(8,128)S(1)} %collective-permute-done.9.other, s32[1,32]{1,0:T(1,128)S(1)} %bitcast.13), custom_call_target="tpu_custom_call" | custom-call | tf_op jit(solution)/shard_map/sweep/pallas_call | solution.py:392
  (7 shorter events, 0.1 us)
Async XLA Ops:
  0.0 1.3 %copy-start.2 = (bf16[1,1,32,128]{3,2,1,0:T(8,128)(2,1)S(1)}, bf16[1,1,32,128]{3,2,1,0:T(8,128)(2,1)}, u32[]{:S(2)}) copy-start(bf16[1,1,32,128]{3,2,1,0:T(8,128)(2,1)} %param.9) | copy-start | bytes 24580
  0.0 4.6 %collective-permute-start.3 = (bf16[32,32,128]{2,1,0:T(8,128)(2,1)}, bf16[32,32,128]{2,1,0:T(8,128)(2,1)S(1)}, u32[]{:S(2)}, u32[]{:S(2)}) collective-permute-start(bf16[32,32,128]{2,1,0:T(8,128)(2,1)} %film_own.1), channel_id=1, source_target_pairs={{0,16},{16,0},{1,17},{17,1},{2,18},{18,2},{3,19},{19,3},{4,20},{20... | collective-permute-start | bytes 786440 | tf_op jit(solution)/shard_map/ppermute | solution.py:143
  1.3 0.7 %copy-start.3 = (s32[1,1,32]{2,1,0:T(1,128)S(1)}, s32[1,1,32]{2,1,0:T(1,128)}, u32[]{:S(2)}) copy-start(s32[1,1,32]{2,1,0:T(1,128)} %param.11) | copy-start | bytes 388
  2.0 0.8 %copy-start.1 = (bf16[1,1,32,1024]{3,2,1,0:T(8,128)(2,1)S(1)}, bf16[1,1,32,1024]{3,2,1,0:T(8,128)(2,1)}, u32[]{:S(2)}) copy-start(bf16[1,1,32,1024]{3,2,1,0:T(8,128)(2,1)} %param.7) | copy-start | bytes 196612
  2.8 0.7 %copy-start.4 = (s32[1,1,32,2]{2,3,1,0:T(2,128)S(1)}, s32[1,1,32,2]{2,3,1,0:T(2,128)}, u32[]{:S(2)}) copy-start(s32[1,1,32,2]{2,3,1,0:T(2,128)} %param.8) | copy-start | bytes 772
  3.5 4.2 %collective-permute-start = (bf16[32,1280]{1,0:T(8,128)(2,1)S(1)}, bf16[32,1280]{1,0:T(8,128)(2,1)S(1)}, u32[]{:S(2)}, u32[]{:S(2)}) collective-permute-start(bf16[32,1280]{1,0:T(8,128)(2,1)S(1)} %pack.1), channel_id=1, source_target_pairs={{0,16},{16,0},{1,17},{17,1},{2,18},{18,2},{3,19},{19,3},{4,20},{20... | collective-permute-start | bytes 245768 | tf_op jit(solution)/shard_map/ppermute | solution.py:143
  4.6 9.0 %collective-permute-start.4 = (bf16[64,16,128]{2,1,0:T(8,128)(2,1)S(1)}, bf16[64,16,128]{2,1,0:T(8,128)(2,1)S(1)}, u32[]{:S(2)}, u32[]{:S(2)}) collective-permute-start(bf16[64,16,128]{2,1,0:T(8,128)(2,1)S(1)} %pad_maximum_fusion), channel_id=1, source_target_pairs={{0,1},{1,0},{2,3},{3,2},{4,5},{5,4},{6,7},{7,6},{8,9},{9,8},{10,11... | collective-permute-start | bytes 786440 | tf_op jit(solution)/shard_map/ppermute | solution.py:154
  7.8 20.3 %copy-start = (bf16[32,32,128]{2,1,0:T(8,128)(2,1)S(1)}, bf16[32,32,128]{2,1,0:T(8,128)(2,1)}, u32[]{:S(2)}) copy-start(bf16[32,32,128]{2,1,0:T(8,128)(2,1)} %film_own.1) | copy-start | bytes 786436
  7.8 8.4 %collective-permute-start.1 = (bf16[2,32,1280]{2,1,0:T(8,128)(2,1)S(1)}, bf16[2,32,1280]{2,1,0:T(8,128)(2,1)S(1)}, u32[]{:S(2)}, u32[]{:S(2)}) collective-permute-start(bf16[2,32,1280]{2,1,0:T(8,128)(2,1)S(1)} %pad_maximum_fusion.1.own), channel_id=1, source_target_pairs={{0,1},{1,0},{2,3},{3,2},{4,5},{5,4},{6,7},{7,6},{8,9},{9,8},{10,11... | collective-permute-start | bytes 491528 | tf_op jit(solution)/shard_map/ppermute | solution.py:154
  13.6 14.5 %collective-permute-start.5 = (bf16[64,16,128]{2,1,0:T(8,128)(2,1)S(1)}, bf16[64,16,128]{2,1,0:T(8,128)(2,1)S(1)}, u32[]{:S(2)}, u32[]{:S(2)}) collective-permute-start(bf16[64,16,128]{2,1,0:T(8,128)(2,1)S(1)} %collective-permute-done.4.film_direct), channel_id=1, source_target_pairs={{0,16},{16,0},{1,17},{17,1},{2,18},{18,2},{3,19},{19,3},{4,20},{20... | collective-permute-start | bytes 786440 | tf_op jit(solution)/shard_map/ppermute | solution.py:143
  16.2 3.6 %collective-permute-start.2 = (bf16[2,32,1280]{2,1,0:T(8,128)(2,1)S(1)}, bf16[2,32,1280]{2,1,0:T(8,128)(2,1)S(1)}, u32[]{:S(2)}, u32[]{:S(2)}) collective-permute-start(bf16[2,32,1280]{2,1,0:T(8,128)(2,1)S(1)} %collective-permute-done.1.direct), channel_id=1, source_target_pairs={{0,16},{16,0},{1,17},{17,1},{2,18},{18,2},{3,19},{19,3},{4,20},{20... | collective-permute-start | bytes 491528 | tf_op jit(solution)/shard_map/ppermute | solution.py:143
  28.6 7.6 %collective-permute-start.6 = (f32[112,128]{1,0:T(8,128)S(1)}, f32[112,128]{1,0:T(8,128)S(1)}, u32[]{:S(2)}, u32[]{:S(2)}) collective-permute-start(f32[112,128]{1,0:T(8,128)S(1)} %get-tuple-element.18.mine), channel_id=1, source_target_pairs={{2,5},{3,4},{4,3},{5,2},{6,9},{7,8},{8,7},{9,6},{10,13},{11,12},{1... | collective-permute-start | bytes 172040 | tf_op jit(solution)/shard_map/ppermute | solution.py:154
  30.7 6.9 %collective-permute-start.8 = (f32[112,128]{1,0:T(8,128)S(1)}, f32[112,128]{1,0:T(8,128)S(1)}, u32[]{:S(2)}, u32[]{:S(2)}) collective-permute-start(f32[112,128]{1,0:T(8,128)S(1)} %get-tuple-element.18.mine), channel_id=1, source_target_pairs={{0,1},{1,0},{2,3},{3,2},{4,5},{5,4},{6,7},{7,6},{8,9},{9,8},{10,11... | collective-permute-start | bytes 172040 | tf_op jit(solution)/shard_map/ppermute | solution.py:154
  32.1 5.5 %collective-permute-start.7 = (f32[64,128]{1,0:T(8,128)S(1)}, f32[64,128]{1,0:T(8,128)S(1)}, u32[]{:S(2)}, u32[]{:S(2)}) collective-permute-start(f32[64,128]{1,0:T(8,128)S(1)} %get-tuple-element.20), channel_id=1, source_target_pairs={{2,4},{3,5},{4,2},{5,3},{6,8},{7,9},{8,6},{9,7},{10,12},{11,13},{1... | collective-permute-start | bytes 98312 | tf_op jit(solution)/shard_map/ppermute | solution.py:154
  37.7 5.0 %collective-permute-start.9 = (f32[288,128]{1,0:T(8,128)S(1)}, f32[288,128]{1,0:T(8,128)S(1)}, u32[]{:S(2)}, u32[]{:S(2)}) collective-permute-start(f32[288,128]{1,0:T(8,128)S(1)} %constant_dynamic-update-slice_fusion.direct), channel_id=1, source_target_pairs={{0,16},{16,0},{1,17},{17,1},{2,18},{18,2},{3,19},{19,3},{4,20},{20... | collective-permute-start | bytes 442376 | tf_op jit(solution)/shard_map/ppermute | solution.py:143

commit v3 on v2

--- a/solution.py
+++ b/solution.py
@@ -136,7 +136,10 @@
     ((1, -1, 1, -1), (2, 2, -2, -2)),
 )
 BESIDE = ((1, -1, 1, -1), (-1, 1, -1, 1))
-UNROLL = 4
+
+
+def take_lanes(values, lanes):
+    return jnp.take_along_axis(values, lanes, axis=1, mode="promise_in_bounds")
 
 
 def swap(x):
@@ -166,20 +169,9 @@
     return jnp.where(core == 0, picked[0], picked[1]), jnp.where(core == 0, picked[1], picked[0])
 
 
-def pack_kernel(footprints, traces, order, centres, counts, packed, numbers):
-    slots, width = footprints.shape
-    numbers[...] = jnp.zeros_like(numbers)
-    numbers[0:1, 0:slots] = order[...].astype(jnp.float32)
-    numbers[1:3, 0:slots] = centres[...].astype(jnp.float32)
-    numbers[3:4, 0:1] = counts[...].astype(jnp.float32)
-    packed[:, :width] = footprints[...]
-    packed[:, width:width + LANES] = traces[...]
-    packed[:, width + LANES:] = numbers[...].astype(jnp.bfloat16)
-
-
 def paint_kernel(
     own, direct, other, mine, links, scale, begin, coupling,
-    patches, trails, canvas, start, numbers, meta, sem,
+    patches, canvas, start, numbers, table, sem,
 ):
     slots = own.shape[1]
     tiles = 6
@@ -191,61 +183,88 @@
     width = pixels * LANES
     depth = canvas.shape[0] // total
     sources = ((own, 0), (own, 1), (direct, 0), (direct, 1), (other, 0), (other, 1))
-
-    for t, (ref, u) in enumerate(sources):
-        numbers[t * 8:(t + 1) * 8, :] = (
-            ref[u, 0:16, width + LANES:].astype(jnp.float32)[0:8].astype(jnp.int32)
-        )
-    fetch = pltpu.make_async_copy(numbers, meta, sem)
+    core = lax.axis_index("ty")
+    step_direct, step_other = partner(BESIDE)
+    tile_rows = (core, 1 - core, core, 1 - core, 1 - core, core)
+    tile_cols = (0, 0, step_direct, step_direct, step_other, step_other)
+
+    heads = [ref[u, 0:16, width + LANES:].astype(jnp.float32) for ref, u in sources]
+    spare = [jnp.zeros((8 - tiles, LANES), jnp.float32)]
+    ordering, top, left, count = (
+        jnp.concatenate([head[i:i + 1, :] for head in heads] + spare, axis=0).astype(jnp.int32)
+        for i in range(4)
+    )
+    row = lax.broadcasted_iota(jnp.int32, (8, LANES), 0)
+    tile_row = jnp.zeros((8, LANES), jnp.int32)
+    tile_col = jnp.zeros((8, LANES), jnp.int32)
+    for t in range(tiles):
+        tile_row = jnp.where(row == t, tile_rows[t], tile_row)
+        tile_col = jnp.where(row == t, tile_cols[t], tile_col)
+    slot_of = lax.broadcasted_iota(jnp.int32, (8, LANES), 1)
+    live = (ordering < count[:, 0:1]).astype(jnp.int32)
+    top = take_lanes(top, ordering) + tile_row * PATCH
+    left = take_lanes(left, ordering) + tile_col * PATCH
+    odd = top & 1
+    spot = (
+        lax.div(slot_of, block) * source
+        + (tile_col + 1) * group
+        + tile_row * block
+        + lax.rem(slot_of, block)
+        + lax.shift_right_logical(top, 1) * total
+    )
+    shift = left + 32 * odd
+    fields = [(row * slots + ordering) * pixels, spot, left, left + PATCH * live, odd]
+    fields += [(shift + 32 * m) & (LANES - 1) for m in range(4)]
+    for i, field in enumerate(fields):
+        numbers[i * 8:(i + 1) * 8, :] = field
+    fetch = pltpu.make_async_copy(numbers, table, sem)
     fetch.start()
+
     canvas[...] = jnp.zeros_like(canvas)
     for t, (ref, u) in enumerate(sources):
         for k in range(pixels):
             patches[pl.ds(t * slots * pixels + k, slots, stride=pixels), :] = ref[
                 u, :, k * LANES:(k + 1) * LANES
             ].astype(jnp.float32)
-        trails[t * slots:(t + 1) * slots, :] = ref[u, :, width:width + LANES].astype(jnp.float32)
+        which = lax.broadcasted_iota(jnp.int32, (slots, slots), 0)
+        chosen = (which == ordering[t:t + 1, :slots]) & (which < count[t:t + 1, 0:1])
+        trail = lax.dot_general(
+            chosen.astype(jnp.bfloat16),
+            ref[u, :, width:width + LANES],
+            (((0,), (0,)), ((), ())),
+            preferred_element_type=jnp.float32,
+        )
+        for q in range(BLOCKS):
+            at = q * source + (tile_cols[t] + 1) * group + tile_rows[t] * block
+            start[pl.ds(pl.multiple_of(at, block), block), :] = trail[q * block:(q + 1) * block]
     fetch.wait()
 
     lane = lax.broadcasted_iota(jnp.int32, (pixels, LANES), 1)
     sub = lax.broadcasted_iota(jnp.int32, (pixels, LANES), 0)
     low = lane < LANES // 2
+    low_first = low & (sub == 0)
     inner = lane & (LANES // 2 - 1)
-    core = lax.axis_index("ty")
-    step_direct, step_other = partner(BESIDE)
-    tile_rows = (core, 1 - core, core, 1 - core, 1 - core, core)
-    tile_cols = (0, 0, step_direct, step_direct, step_other, step_other)
 
     def paint(t, s):
-        p = meta[t * 8, s]
-        live = (p < meta[t * 8 + 3, 0]).astype(jnp.int32)
-        top = tile_rows[t] * PATCH + meta[t * 8 + 1, p]
-        left = meta[t * 8 + 2, p] + tile_cols[t] * PATCH
-        slot = (
-            (s // block) * source + (tile_cols[t] + 1) * group + tile_rows[t] * block + s % block
+        origin, at, begins, ends, odd_row, *turns = (
+            table[i * 8 + t, s] for i in range(len(fields))
         )
-        odd = top & 1
-        level = top // 2
-        value = patches[pl.ds(pl.multiple_of((t * slots + p) * pixels, pixels), pixels), :]
-        shift = left + 32 * odd + LANES
-        turned = [pltpu.roll(value, (shift + 32 * m) & (LANES - 1), 1) for m in range(4)]
-        first = pltpu.roll(turned[0], odd, 0)
-        inside = (inner >= left) & (inner < left + PATCH * live)
-        even_rows = jnp.where(low, jnp.where(sub >= odd, first, 0.0), turned[1])
+        value = patches[pl.ds(pl.multiple_of(origin, pixels), pixels), :]
+        turned = [pltpu.roll(value, turn, 1) for turn in turns]
+        down = pltpu.roll(turned[0], 1, 0)
+        is_odd = jnp.broadcast_to(odd_row, sub.shape) > 0
+        inside = (inner >= begins) & (inner < ends)
+        first = jnp.where(is_odd, jnp.where(sub == 0, 0.0, down), turned[0])
+        even_rows = jnp.where(low, first, turned[1])
         odd_rows = jnp.where(low, turned[2], turned[3])
-        last = jnp.where(inside & low & (sub < odd), first, 0.0)
-        at = level * total + slot
+        last = jnp.where(inside & low_first & is_odd, down, 0.0)
         canvas[pl.ds(at, pixels, stride=2 * total), :] = jnp.where(inside, even_rows, 0.0)
         canvas[pl.ds(at + total, pixels, stride=2 * total), :] = jnp.where(inside, odd_rows, 0.0)
         canvas[pl.ds(at + 2 * pixels * total, 1), :] = last[0:1, :]
-        trail = trails[pl.ds(t * slots + p, 1), :]
-        start[pl.ds(slot, 1), :] = trail * live.astype(jnp.float32)
 
     for t in range(tiles):
-        @pl.loop(0, slots // UNROLL)
-        def _(step):
-            for k in range(UNROLL):
-                paint(t, step * UNROLL + k)
+        for s in range(slots):
+            paint(t, s)
 
     margins = jnp.zeros((2 * slots, total), jnp.float32)
     edge = PATCH // 8
@@ -385,25 +404,23 @@
     out[...] = exact(place.astype(jnp.float32), ordered)
 
 
-def call(kernel, outs, scratch, megabytes, name):
-    vmem = pl.BlockSpec(memory_space=pltpu.VMEM)
-
+def call(kernel, outs, scratch, megabytes, space=pltpu.VMEM, cost=None):
     def run(*operands):
         return pl.pallas_call(
             kernel,
             out_shape=[jax.ShapeDtypeStruct(*out) for out in outs],
-            in_specs=[vmem] * len(operands),
-            out_specs=[vmem] * len(outs),
+            in_specs=[pl.BlockSpec(memory_space=space)] * len(operands),
+            out_specs=[pl.BlockSpec(memory_space=pltpu.VMEM)] * len(outs),
             scratch_shapes=scratch,
             compiler_params=pltpu.CompilerParams(vmem_limit_bytes=megabytes << 20),
-            name=name,
+            cost_estimate=cost,
         )(*operands)
 
     return run
 
 
 def strip_body(movie, footprints, centres, traces, counts, order):
-    height, width, frames = movie.shape
+    height, _, frames = movie.shape
     slots = footprints.shape[2]
     area = footprints.shape[3]
     half = PATCH // 2
@@ -411,19 +428,21 @@
     total = 6 * slots
     bf16, f32 = jnp.bfloat16, jnp.float32
 
-    pair_movie = swap(movie)
-    (packed,) = call(
-        pack_kernel,
-        [((slots, area + 2 * LANES), bf16)],
-        [pltpu.VMEM((slots, LANES), f32)],
-        4,
-        "pack",
-    )(footprints[0, 0], traces[0, 0], order[0], centres[0, 0].T, counts)
+    def spread(values, top):
+        below = slots - top - values.shape[0]
+        return jnp.pad(values, ((top, below), (0, LANES - values.shape[1])))
+
+    numbers = spread(order[0], 0) + spread(centres[0, 0].T, 1) + spread(counts, 3)
+    packed = jnp.concatenate(
+        [footprints[0, 0], traces[0, 0], numbers.astype(bf16)], axis=1
+    )
+    film = movie
     own = jnp.stack([packed, swap(packed)])
+    pair_film = swap(film)
     direct = pairwise(own, BESIDE)
     edge = jnp.where(partner(BESIDE)[0] > 0, half, 0)
     edges = jnp.concatenate(
-        [lax.dynamic_slice_in_dim(x, edge, half, axis=1) for x in (movie, pair_movie)], axis=0
+        [lax.dynamic_slice_in_dim(x, edge, half, axis=1) for x in (film, pair_film)], axis=0
     )
     film_direct = pairwise(edges, BESIDE)
     other = swap(direct)
@@ -441,32 +460,26 @@
         ],
         [
             pltpu.VMEM((total * area // LANES, LANES), f32),
-            pltpu.VMEM((total, frames), f32),
             pltpu.VMEM((canvas_rows * total, LANES), f32),
             pltpu.VMEM((total, frames), f32),
-            pltpu.VMEM((48, LANES), jnp.int32),
-            pltpu.SMEM((48, LANES), jnp.int32),
+            pltpu.VMEM((72, LANES), jnp.int32),
+            pltpu.SMEM((72, LANES), jnp.int32),
             pltpu.SemaphoreType.DMA,
         ],
         16,
-        "paint",
+        cost=pl.CostEstimate(flops=4_000_000_000, bytes_accessed=0, transcendentals=0),
     )(own, direct, other)
     far, far_short, keep = call(
         drive_kernel,
         [((7 * group, frames), f32), ((4 * group, frames), f32), ((4 * group, frames), f32)],
         [pltpu.VMEM((2 * height, 2 * PATCH, frames), bf16)],
         8,
-        "drive",
-    )(*painted, movie, pair_movie, film_direct, film_other)
-
-    came = jnp.concatenate(
-        [
-            pairwise(far, OFFSETS[0]),
-            pairwise(far_short, OFFSETS[1]),
-            pairwise(far, OFFSETS[2]),
-        ],
-        axis=0,
-    )
+    )(*painted, film, pair_film, film_direct, film_other)
+
+    far0 = pairwise(far, OFFSETS[0])
+    far1 = pairwise(far_short, OFFSETS[1])
+    far2 = pairwise(far, OFFSETS[2])
+    came = jnp.concatenate([far0, far1, far2], axis=0)
     (result,) = call(
         sweep_kernel,
         [((slots, frames), f32)],
@@ -475,7 +488,6 @@
             pltpu.VMEM((4 * group, frames), f32),
         ],
         4,
-        "sweep",
     )(far, keep, came, swap(came), order[0])
     return result[None, None]
 

time: 44.5 us -> 38.7 us (0.87)
  Pallas kernels: 10.3 us -> 6.7 us
  local copies, waits for them, and re-layouts: 3.12 us -> 0.05 us
  starting transfers between devices: 24.6 us -> 21.9 us
  waiting for transfers between devices: 5.26 us -> 7.36 us
  other arithmetic: 0.04 us -> 1.61 us
    pallas_call x4 -> x3, Pallas kernels: 10.3 us -> 6.7 us  [run(): pl.pallas_call(kernel, out_shape=[jax.ShapeDtypeStruct(*out) for out in o...]
    ppermute x5, starting transfers between devices: 9.83 us -> 7.24 us  [swap(): return lax.ppermute(x, 'ty', [(0, 1), (1, 0)])]
    ppermute x5, waiting for transfers between devices: 3.21 us -> 5.52 us  [pairwise(): return lax.ppermute(x, ('ty', 'tx'), pairs)]
    unnamed x12 -> x6, local copies, waits for them, and re-layouts: 2.18 us -> 0.02 us
    dynamic_slice x2, local copies, waits for them, and re-layouts: 0.94 us -> 0.03 us  [strip_body(): lax.dynamic_slice_in_dim(x, edge, half, axis=1)]
    another operation x1 -> x2, other arithmetic: 0.02 us -> 0.89 us  [strip_body(): own = jnp.stack([packed, swap(packed)])]
    convert_element_type x0 -> x1, other arithmetic: none -> 0.69 us  [strip_body(): numbers.astype(bf16)]
  transfers between devices with their start and end apart: 10 -> 10, of which waited for: 4 -> 5; matrix products, arithmetic and copies ran while one was open for 2% -> 0% of each run, Pallas kernels for 19% -> 12%
where the time goes in v3:
time: 38.7 us; the launch traced here: 38.4 us
  starting transfers between devices  21.9 us (57%)
  waiting for transfers between devices  7.36 us (19%)
  Pallas kernels  6.7 us (17%)
  other arithmetic  1.61 us (4%)
  between operations  0.82 us (2%)
    ppermute x5, starting transfers between devices, pairwise(): return lax.ppermute(x, ('ty', 'tx'), pairs)  14.6 us
    ppermute x5, starting transfers between devices, swap(): return lax.ppermute(x, 'ty', [(0, 1), (1, 0)])  7.24 us
    pallas_call x3, Pallas kernels, run(): pl.pallas_call(kernel, out_shape=[jax.ShapeDtypeStruct(*out) for out in o...  6.7 us
    ppermute x5, waiting for transfers between devices, pairwise(): return lax.ppermute(x, ('ty', 'tx'), pairs)  5.52 us
    ppermute x5, waiting for transfers between devices, swap(): return lax.ppermute(x, 'ty', [(0, 1), (1, 0)])  1.84 us
    another operation x2, other arithmetic, strip_body(): own = jnp.stack([packed, swap(packed)])  0.89 us
  transfers between devices with their start and end apart: 10, of which 5 were waited for; matrix products, arithmetic and copies ran while one was open for 0% of the time, Pallas kernels for 12%

profile of v3, /device:TPU:7, one launch (start us, length us, event | category | flops | bytes accessed | tf_op | source)
XLA Modules:
  0.0 38.4 jit_solution(3577199563176136636)
XLA Ops:
  0.0 0.0 copy-start
  0.7 0.7 %add_convert_fusion = bf16[32,128]{1,0:T(8,128)(2,1)S(1)} fusion(s32[1,1]{1,0:T(1,128)S(6)} %copy.9, s32[2,32]{1,0:T(2,128)} %bitcast.15, s32[1,32]{1,0:T(1,128)} %bitcast.10), kind=kLoop, calls=%fused_computation.3 | loop fusion | flops 12288 | bytes 8580 | tf_op jit(solution)/shard_map/convert_element_type | solution.py:437
  1.4 0.9 %fusion = (bf16[1,32,1280]{2,1,0:T(8,128)(2,1)S(1)}, bf16[32,1280]{1,0:T(8,128)(2,1)S(1)}) fusion(bf16[32,128]{1,0:T(8,128)(2,1)S(1)} %add_convert_fusion, bf16[32,128]{1,0:T(8,128)(2,1)} %bitcast.14, bf16[32,1024]{1,0:T(8,128)(2,1)} %bitcast.13), kind=kLoop, calls=%fused_computation.9 | loop fusion | flops 245760 | bytes 245760 | tf_op jit(solution)/shard_map/stack | solution.py:440
  2.3 0.7 %collective-permute-start = (bf16[32,1280]{1,0:T(8,128)(2,1)S(1)}, bf16[32,1280]{1,0:T(8,128)(2,1)S(1)}, u32[]{:S(2)}, u32[]{:S(2)}) collective-permute-start(bf16[32,1280]{1,0:T(8,128)(2,1)S(1)} %get-tuple-element.22), channel_id=1, source_target_pairs={{0,16},{16,0},{1,17},{17,1},{2,18},{18,2},{3,19},{19,3},{4,20},{20... | collective-permute-start | bytes 245768 | tf_op jit(solution)/shard_map/ppermute | solution.py:146
  3.0 0.0 copy-done
  3.0 0.1 collective-permute-start.3
  3.1 0.8 %collective-permute-done = bf16[32,1280]{1,0:T(8,128)(2,1)S(1)} collective-permute-done((bf16[32,1280]{1,0:T(8,128)(2,1)S(1)}, bf16[32,1280]{1,0:T(8,128)(2,1)S(1)}, u32[]{:S(2)}, u32[]{:S(2)}) %collective-permute-start) | collective-permute-done | bytes 81952 | tf_op jit(solution)/shard_map/ppermute | solution.py:146
  4.0 3.1 %collective-permute-start.1 = (bf16[2,32,1280]{2,1,0:T(8,128)(2,1)S(1)}, bf16[2,32,1280]{2,1,0:T(8,128)(2,1)S(1)}, u32[]{:S(2)}, u32[]{:S(2)}) collective-permute-start(bf16[2,32,1280]{2,1,0:T(8,128)(2,1)S(1)} %pad_maximum_fusion.1.own), channel_id=1, source_target_pairs={{0,1},{1,0},{2,3},{3,2},{4,5},{5,4},{6,7},{7,6},{8,9},{9,8},{10,11... | collective-permute-start | bytes 491528 | tf_op jit(solution)/shard_map/ppermute | solution.py:157
  7.1 0.0 collective-permute-done.3.film_pair
  7.2 4.0 %collective-permute-start.4 = (bf16[64,16,128]{2,1,0:T(8,128)(2,1)S(1)}, bf16[64,16,128]{2,1,0:T(8,128)(2,1)S(1)}, u32[]{:S(2)}, u32[]{:S(2)}) collective-permute-start(bf16[64,16,128]{2,1,0:T(8,128)(2,1)S(1)} %pad_maximum_fusion), channel_id=1, source_target_pairs={{0,1},{1,0},{2,3},{3,2},{4,5},{5,4},{6,7},{7,6},{8,9},{9,8},{10,11... | collective-permute-start | bytes 786440 | tf_op jit(solution)/shard_map/ppermute | solution.py:157
  11.1 0.8 %collective-permute-done.1.direct = bf16[2,32,1280]{2,1,0:T(8,128)(2,1)S(1)} collective-permute-done((bf16[2,32,1280]{2,1,0:T(8,128)(2,1)S(1)}, bf16[2,32,1280]{2,1,0:T(8,128)(2,1)S(1)}, u32[]{:S(2)}, u32[]{:S(2)}) %collective-permute-start.1) | collective-permute-done | bytes 163872 | tf_op jit(solution)/shard_map/ppermute | solution.py:157
  11.9 0.8 %collective-permute-start.2 = (bf16[2,32,1280]{2,1,0:T(8,128)(2,1)S(1)}, bf16[2,32,1280]{2,1,0:T(8,128)(2,1)S(1)}, u32[]{:S(2)}, u32[]{:S(2)}) collective-permute-start(bf16[2,32,1280]{2,1,0:T(8,128)(2,1)S(1)} %collective-permute-done.1.direct), channel_id=1, source_target_pairs={{0,16},{16,0},{1,17},{17,1},{2,18},{18,2},{3,19},{19,3},{4,20},{20... | collective-permute-start | bytes 491528 | tf_op jit(solution)/shard_map/ppermute | solution.py:146
  12.7 3.5 %collective-permute-done.4.film_direct = bf16[64,16,128]{2,1,0:T(8,128)(2,1)S(1)} collective-permute-done((bf16[64,16,128]{2,1,0:T(8,128)(2,1)S(1)}, bf16[64,16,128]{2,1,0:T(8,128)(2,1)S(1)}, u32[]{:S(2)}, u32[]{:S(2)}) %collective-permute-start.4) | collective-permute-done | bytes 262176 | tf_op jit(solution)/shard_map/ppermute | solution.py:157
  16.2 1.9 %collective-permute-start.5 = (bf16[64,16,128]{2,1,0:T(8,128)(2,1)S(1)}, bf16[64,16,128]{2,1,0:T(8,128)(2,1)S(1)}, u32[]{:S(2)}, u32[]{:S(2)}) collective-permute-start(bf16[64,16,128]{2,1,0:T(8,128)(2,1)S(1)} %collective-permute-done.4.film_direct), channel_id=1, source_target_pairs={{0,16},{16,0},{1,17},{17,1},{2,18},{18,2},{3,19},{19,3},{4,20},{20... | collective-permute-start | bytes 786440 | tf_op jit(solution)/shard_map/ppermute | solution.py:146
  18.0 0.0 collective-permute-done.2.other
  18.0 4.7 %shard_map.64 = (bf16[16,64,256]{2,1,0:T(8,128)(2,1)S(1)}, f32[64,128]{1,0:T(8,128)S(1)}, f32[64,128]{1,0:T(8,128)S(1)}, f32[64,128]{1,0:T(8,128)S(1)}, f32[64,128]{1,0:T(8,128)S(1)}) custom-call(bf16[2,32,1280]{2,1,0:T(8,128)(2,1)S(1)} %pad_maximum_fusion.1.own, bf16[2,32,1280]{2,1,0:T(8,128)(2,1)S(1)} %collective-permute-done.1.direct, ...), custom_call_target="tpu_custom_call" | custom-call | flops 4000000000 | tf_op jit(solution)/shard_map/pallas_call | solution.py:409
  22.8 0.0 collective-permute-done.5.film_other
  22.8 0.5 %shard_map.65 = (f32[112,128]{1,0:T(8,128)S(1)}, f32[64,128]{1,0:T(8,128)S(1)}, f32[64,128]{1,0:T(8,128)S(1)}) custom-call(bf16[16,64,256]{2,1,0:T(8,128)(2,1)S(1)} %get-tuple-element.13.mine, f32[64,128]{1,0:T(8,128)S(1)} %get-tuple-element.14.links, f32[64,128]{1,0:T(8,128)S(1)} %get-tuple-element.15.scale, f32[64,128]{1,0:T(8,128)S(1)} %get-tuple-element.16.begin, ...), custom_call_target="tpu_custom_call" | custom-call | tf_op jit(solution)/shard_map/pallas_call | solution.py:409
  23.3 2.8 %collective-permute-start.6 = (f32[112,128]{1,0:T(8,128)S(1)}, f32[112,128]{1,0:T(8,128)S(1)}, u32[]{:S(2)}, u32[]{:S(2)}) collective-permute-start(f32[112,128]{1,0:T(8,128)S(1)} %get-tuple-element.18.mine), channel_id=1, source_target_pairs={{2,5},{3,4},{4,3},{5,2},{6,9},{7,8},{8,7},{9,6},{10,13},{11,12},{1... | collective-permute-start | bytes 172040 | tf_op jit(solution)/shard_map/ppermute | solution.py:157
  26.0 0.4 collective-permute-start.8
  26.4 4.4 %collective-permute-start.7 = (f32[64,128]{1,0:T(8,128)S(1)}, f32[64,128]{1,0:T(8,128)S(1)}, u32[]{:S(2)}, u32[]{:S(2)}) collective-permute-start(f32[64,128]{1,0:T(8,128)S(1)} %get-tuple-element.20), channel_id=1, source_target_pairs={{2,4},{3,5},{4,2},{5,3},{6,8},{7,9},{8,6},{9,7},{10,12},{11,13},{1... | collective-permute-start | bytes 98312 | tf_op jit(solution)/shard_map/ppermute | solution.py:157
  30.8 0.0 collective-permute-done.6
  30.9 1.3 %collective-permute-done.7 = f32[64,128]{1,0:T(8,128)S(1)} collective-permute-done((f32[64,128]{1,0:T(8,128)S(1)}, f32[64,128]{1,0:T(8,128)S(1)}, u32[]{:S(2)}, u32[]{:S(2)}) %collective-permute-start.7) | collective-permute-done | bytes 32800 | tf_op jit(solution)/shard_map/ppermute | solution.py:157
  32.1 0.0 collective-permute-done.8
  32.1 0.0 copy-start.1
  32.2 3.8 %collective-permute-start.9 = (f32[288,128]{1,0:T(8,128)S(1)}, f32[288,128]{1,0:T(8,128)S(1)}, u32[]{:S(2)}, u32[]{:S(2)}) collective-permute-start(f32[288,128]{1,0:T(8,128)S(1)} %constant_dynamic-update-slice_fusion.direct), channel_id=1, source_target_pairs={{0,16},{16,0},{1,17},{17,1},{2,18},{18,2},{3,19},{19,3},{4,20},{20... | collective-permute-start | bytes 442376 | tf_op jit(solution)/shard_map/ppermute | solution.py:146
  35.9 1.0 %collective-permute-done.9.other = f32[288,128]{1,0:T(8,128)S(1)} collective-permute-done((f32[288,128]{1,0:T(8,128)S(1)}, f32[288,128]{1,0:T(8,128)S(1)}, u32[]{:S(2)}, u32[]{:S(2)}) %collective-permute-start.9) | collective-permute-done | bytes 147488 | tf_op jit(solution)/shard_map/ppermute | solution.py:146
  36.9 0.0 copy-done.1
  36.9 1.5 %shard_map.66 = f32[32,128]{1,0:T(8,128)} custom-call(f32[112,128]{1,0:T(8,128)S(1)} %get-tuple-element.18.mine, f32[64,128]{1,0:T(8,128)S(1)} %get-tuple-element.19.keep, f32[288,128]{1,0:T(8,128)S(1)} %constant_dynamic-update-slice_fusion.direct, f32[288,128]{1,0:T(8,128)S(1)} %collective-permute-done.9.other, s32[1,32]{1,0:T(1,128)S(1)} %bitcast.11), custom_call_target="tpu_custom_call" | custom-call | tf_op jit(solution)/shard_map/pallas_call | solution.py:409
  (7 shorter events, 0.1 us)
Async XLA Ops:
  0.0 3.0 %copy-start = (bf16[32,32,128]{2,1,0:T(8,128)(2,1)S(1)}, bf16[32,32,128]{2,1,0:T(8,128)(2,1)}, u32[]{:S(2)}) copy-start(bf16[32,32,128]{2,1,0:T(8,128)(2,1)} %film_own.1) | copy-start | bytes 786436
  2.3 1.7 %collective-permute-start = (bf16[32,1280]{1,0:T(8,128)(2,1)S(1)}, bf16[32,1280]{1,0:T(8,128)(2,1)S(1)}, u32[]{:S(2)}, u32[]{:S(2)}) collective-permute-start(bf16[32,1280]{1,0:T(8,128)(2,1)S(1)} %get-tuple-element.22), channel_id=1, source_target_pairs={{0,16},{16,0},{1,17},{17,1},{2,18},{18,2},{3,19},{19,3},{4,20},{20... | collective-permute-start | bytes 245768 | tf_op jit(solution)/shard_map/ppermute | solution.py:146
  3.0 4.1 %collective-permute-start.3 = (bf16[32,32,128]{2,1,0:T(8,128)(2,1)S(1)}, bf16[32,32,128]{2,1,0:T(8,128)(2,1)S(1)}, u32[]{:S(2)}, u32[]{:S(2)}) collective-permute-start(bf16[32,32,128]{2,1,0:T(8,128)(2,1)S(1)} %copy-done), channel_id=1, source_target_pairs={{0,16},{16,0},{1,17},{17,1},{2,18},{18,2},{3,19},{19,3},{4,20},{20... | collective-permute-start | bytes 786440 | tf_op jit(solution)/shard_map/ppermute | solution.py:146
  4.0 8.0 %collective-permute-start.1 = (bf16[2,32,1280]{2,1,0:T(8,128)(2,1)S(1)}, bf16[2,32,1280]{2,1,0:T(8,128)(2,1)S(1)}, u32[]{:S(2)}, u32[]{:S(2)}) collective-permute-start(bf16[2,32,1280]{2,1,0:T(8,128)(2,1)S(1)} %pad_maximum_fusion.1.own), channel_id=1, source_target_pairs={{0,1},{1,0},{2,3},{3,2},{4,5},{5,4},{6,7},{7,6},{8,9},{9,8},{10,11... | collective-permute-start | bytes 491528 | tf_op jit(solution)/shard_map/ppermute | solution.py:157
  7.2 9.0 %collective-permute-start.4 = (bf16[64,16,128]{2,1,0:T(8,128)(2,1)S(1)}, bf16[64,16,128]{2,1,0:T(8,128)(2,1)S(1)}, u32[]{:S(2)}, u32[]{:S(2)}) collective-permute-start(bf16[64,16,128]{2,1,0:T(8,128)(2,1)S(1)} %pad_maximum_fusion), channel_id=1, source_target_pairs={{0,1},{1,0},{2,3},{3,2},{4,5},{5,4},{6,7},{7,6},{8,9},{9,8},{10,11... | collective-permute-start | bytes 786440 | tf_op jit(solution)/shard_map/ppermute | solution.py:157
  11.9 6.1 %collective-permute-start.2 = (bf16[2,32,1280]{2,1,0:T(8,128)(2,1)S(1)}, bf16[2,32,1280]{2,1,0:T(8,128)(2,1)S(1)}, u32[]{:S(2)}, u32[]{:S(2)}) collective-permute-start(bf16[2,32,1280]{2,1,0:T(8,128)(2,1)S(1)} %collective-permute-done.1.direct), channel_id=1, source_target_pairs={{0,16},{16,0},{1,17},{17,1},{2,18},{18,2},{3,19},{19,3},{4,20},{20... | collective-permute-start | bytes 491528 | tf_op jit(solution)/shard_map/ppermute | solution.py:146
  16.2 6.6 %collective-permute-start.5 = (bf16[64,16,128]{2,1,0:T(8,128)(2,1)S(1)}, bf16[64,16,128]{2,1,0:T(8,128)(2,1)S(1)}, u32[]{:S(2)}, u32[]{:S(2)}) collective-permute-start(bf16[64,16,128]{2,1,0:T(8,128)(2,1)S(1)} %collective-permute-done.4.film_direct), channel_id=1, source_target_pairs={{0,16},{16,0},{1,17},{17,1},{2,18},{18,2},{3,19},{19,3},{4,20},{20... | collective-permute-start | bytes 786440 | tf_op jit(solution)/shard_map/ppermute | solution.py:146
  23.3 7.6 %collective-permute-start.6 = (f32[112,128]{1,0:T(8,128)S(1)}, f32[112,128]{1,0:T(8,128)S(1)}, u32[]{:S(2)}, u32[]{:S(2)}) collective-permute-start(f32[112,128]{1,0:T(8,128)S(1)} %get-tuple-element.18.mine), channel_id=1, source_target_pairs={{2,5},{3,4},{4,3},{5,2},{6,9},{7,8},{8,7},{9,6},{10,13},{11,12},{1... | collective-permute-start | bytes 172040 | tf_op jit(solution)/shard_map/ppermute | solution.py:157
  26.0 6.1 %collective-permute-start.8 = (f32[112,128]{1,0:T(8,128)S(1)}, f32[112,128]{1,0:T(8,128)S(1)}, u32[]{:S(2)}, u32[]{:S(2)}) collective-permute-start(f32[112,128]{1,0:T(8,128)S(1)} %get-tuple-element.18.mine), channel_id=1, source_target_pairs={{0,1},{1,0},{2,3},{3,2},{4,5},{5,4},{6,7},{7,6},{8,9},{9,8},{10,11... | collective-permute-start | bytes 172040 | tf_op jit(solution)/shard_map/ppermute | solution.py:157
  26.4 5.7 %collective-permute-start.7 = (f32[64,128]{1,0:T(8,128)S(1)}, f32[64,128]{1,0:T(8,128)S(1)}, u32[]{:S(2)}, u32[]{:S(2)}) collective-permute-start(f32[64,128]{1,0:T(8,128)S(1)} %get-tuple-element.20), channel_id=1, source_target_pairs={{2,4},{3,5},{4,2},{5,3},{6,8},{7,9},{8,6},{9,7},{10,12},{11,13},{1... | collective-permute-start | bytes 98312 | tf_op jit(solution)/shard_map/ppermute | solution.py:157
  32.1 4.8 %copy-start.1 = (s32[1,1,32]{2,1,0:T(1,128)S(1)}, s32[1,1,32]{2,1,0:T(1,128)}, u32[]{:S(2)}) copy-start(s32[1,1,32]{2,1,0:T(1,128)} %param.11) | copy-start | bytes 388
  32.2 4.8 %collective-permute-start.9 = (f32[288,128]{1,0:T(8,128)S(1)}, f32[288,128]{1,0:T(8,128)S(1)}, u32[]{:S(2)}, u32[]{:S(2)}) collective-permute-start(f32[288,128]{1,0:T(8,128)S(1)} %constant_dynamic-update-slice_fusion.direct), channel_id=1, source_target_pairs={{0,16},{16,0},{1,17},{17,1},{2,18},{18,2},{3,19},{19,3},{4,20},{20... | collective-permute-start | bytes 442376 | tf_op jit(solution)/shard_map/ppermute | solution.py:146

commit v4 on v3

--- a/solution.py
+++ b/solution.py
@@ -130,12 +130,11 @@
     return result[None, None]
 
 
-OFFSETS = (
-    ((-1, -3, 3, 1), (3, 1, -1, -3)),
-    ((-2, -2, 2, 2), (-3, 3, -3, 3)),
-    ((1, -1, 1, -1), (2, 2, -2, -2)),
-)
 BESIDE = ((1, -1, 1, -1), (-1, 1, -1, 1))
+EDGES = ((1, -1, 1, -1), (2, 2, -2, -2))
+ACROSS = ((-1, -3, 3, 1), (3, 1, -1, -3))
+PLANES = ((4, -4, 4, -4), (4, 4, -4, -4))
+RELAYED = ((-3, 3, -3, 3), (-2, -2, 2, 2))
 
 
 def take_lanes(values, lanes):
@@ -151,7 +150,7 @@
     pairs = []
     for core, steps in enumerate(offsets):
         for i in range(count):
-            other = i + steps[i % 4]
+            other = i + steps[i % len(steps)]
             if 0 <= other < count:
                 pairs.append((core * count + i, core * count + other))
     return lax.ppermute(x, ("ty", "tx"), pairs)
@@ -159,18 +158,44 @@
 
 def partner(offsets):
     core = lax.axis_index("ty")
-    place = lax.axis_index("tx") & 3
     picked = []
     for steps in offsets:
-        step = jnp.int32(steps[3])
-        for i in range(3):
+        place = lax.axis_index("tx") & (len(steps) - 1)
+        step = jnp.int32(steps[-1])
+        for i in range(len(steps) - 1):
             step = jnp.where(place == i, steps[i], step)
         picked.append(step)
     return jnp.where(core == 0, picked[0], picked[1]), jnp.where(core == 0, picked[1], picked[0])
 
 
+def pack_kernel(
+    counts, footprints, traces, order, centres,
+    packed, ordering, patch_buf, trace_buf, order_buf, centre_buf, numbers, sems,
+):
+    pairs = (
+        (order, order_buf),
+        (centres, centre_buf),
+        (footprints, patch_buf),
+        (traces, trace_buf),
+    )
+    copies = [pltpu.make_async_copy(a, b, sems.at[i]) for i, (a, b) in enumerate(pairs)]
+    for copy in copies:
+        copy.start()
+    slots, width = patch_buf.shape
+    numbers[...] = jnp.zeros_like(numbers)
+    for copy in copies:
+        copy.wait()
+    numbers[0:1, 0:slots] = order_buf[...].astype(jnp.float32)
+    numbers[1:3, 0:slots] = centre_buf[...].astype(jnp.float32)
+    numbers[3:4, :] = jnp.full((1, LANES), counts[0, 0], jnp.int32).astype(jnp.float32)
+    ordering[...] = order_buf[...]
+    packed[:, :width] = patch_buf[...]
+    packed[:, width:width + LANES] = trace_buf[...]
+    packed[:, width + LANES:] = numbers[...].astype(jnp.bfloat16)
+
+
 def paint_kernel(
-    own, direct, other, mine, links, scale, begin, coupling,
+    own, direct, other, mine, links, scale, begin, coupling, beside,
     patches, canvas, start, numbers, table, sem,
 ):
     slots = own.shape[1]
@@ -293,6 +318,10 @@
     scale[...] = jnp.broadcast_to(diagonal, scale.shape)
     for q in range(BLOCKS):
         begin[q * group:(q + 1) * group, :] = start[q * source + group:q * source + 2 * group, :]
+    for i, q in enumerate((1, 2)):
+        for side in range(2):
+            at = q * source + 2 * side * group
+            beside[(2 * i + side) * group:(2 * i + side + 1) * group, :] = start[at:at + group, :]
     share = margins / diagonal
     for i, q in enumerate((1, 2, 3)):
         links[i * group:(i + 1) * group, :] = share[q * group:(q + 1) * group, :LANES]
@@ -301,7 +330,7 @@
 
 def drive_kernel(
     mine, links, scale, begin, coupling, film_own, film_pair, film_direct, film_other,
-    far, far_short, keep, film,
+    near, across, level, film,
 ):
     core = lax.axis_index("ty")
     side_direct, side_other = partner(BESIDE)
@@ -331,85 +360,125 @@
     for step in range(mine.shape[0]):
         pixels_here = film[step * 4:(step + 1) * 4].reshape(mine.shape[2], -1)
         drive += jnp.dot(mine[step], pixels_here, preferred_element_type=jnp.float32)
-    level = begin[...] + (drive - coupling[...]) / scale[...]
+    level[...] = begin[...] + (drive - coupling[...]) / scale[...]
 
     def rows_of(x, q):
-        return x[q * group:(q + 1) * group]
-
-    first = jnp.maximum(rows_of(level, 0), 0.0)
-    change = first - begin[0:group, :]
-    pieces = (
-        change,
-        rows_of(level, 1), begin[group:2 * group, :], links[0:group, :],
-        rows_of(level, 2), begin[2 * group:3 * group, :], links[group:2 * group, :],
-    )
-    for ref in (far, far_short):
-        for i in range(ref.shape[0] // group):
-            ref[i * group:(i + 1) * group, :] = pieces[i]
-    keep[0:group, :] = first
-    keep[group:2 * group, :] = rows_of(level, 3)
-    keep[2 * group:4 * group, :] = links[2 * group:4 * group, :]
-
-
-def sweep_kernel(mine, keep, direct, other, order, out, box, current):
+        return x[q * group:(q + 1) * group, :]
+
+    change = jnp.maximum(rows_of(level, 0), 0.0) - rows_of(begin, 0)
+    varied = jnp.where(core == 0, rows_of(level, 2), rows_of(begin, 1))
+    for ref, fourth in ((near, varied), (across, rows_of(level, 2))):
+        pieces = (change, rows_of(level, 1), rows_of(links, 0), fourth, rows_of(links, 1))
+        for i, piece in enumerate(pieces):
+            ref[i * group:(i + 1) * group, :] = piece
+
+
+def sweep_kernel(
+    level, begin, links, beside, near_direct, near_other, across_direct, across_other,
+    relay_direct, relay_other, order, out, box, current,
+):
     slots = out.shape[0]
     block = slots // BLOCKS
     group = 2 * block
     reach = BLOCKS - 1
-    box[reach] = mine[...]
-    at = 0
-    for offsets, size in zip(OFFSETS, (7 * group, 4 * group, 7 * group)):
-        step_direct, step_other = partner(offsets)
-        box[reach + step_direct, 0:size, :] = direct[at:at + size, :]
-        box[reach + step_other, 0:size, :] = other[at:at + size, :]
-        at += size
-
-    def exact(a, b):
-        return jnp.dot(a, b, precision=precise, preferred_element_type=jnp.float32)
-
-    def around(values, j):
-        return [values[j - 1], values[j], values[j + 1]]
+    refs = (near_direct, near_other, across_direct, across_other, relay_direct, relay_other)
+    steps = (*partner(EDGES), *partner(ACROSS), *partner(RELAYED))
+    for ref, step in zip(refs, steps):
+        box[reach + step] = ref[...]
+
+    def halves(x):
+        high = x.astype(jnp.bfloat16)
+        return high, (x - high.astype(jnp.float32)).astype(jnp.bfloat16)
+
+    def product(a, b):
+        (a1, a2), (b1, b2) = halves(a), halves(b)
+        return sum(
+            jnp.dot(x, y, preferred_element_type=jnp.float32)
+            for x, y in ((a1, b1), (a1, b2), (a2, b1))
+        )
+
+    def block_of(x, i):
+        return x[i * group:(i + 1) * group, :]
 
     def part(j, i):
         return box[j, i * group:(i + 1) * group, :]
 
-    change0 = {j: part(j, 0) for j in range(2 * reach + 1)}
-    renewed1, change1 = {}, {}
-    for j in range(1, 2 * reach):
-        near = jnp.concatenate(around(change0, j), axis=0)
-        renewed1[j] = jnp.maximum(part(j, 1) - exact(part(j, 3)[:, :3 * group], near), 0.0)
-        change1[j] = renewed1[j] - part(j, 2)
-    renewed2, change2 = {}, {}
-    for j in range(2, 2 * reach - 1):
-        near = jnp.concatenate(around(change0, j) + around(change1, j), axis=0)
-        renewed2[j] = jnp.maximum(part(j, 4) - exact(part(j, 6)[:, :6 * group], near), 0.0)
-        change2[j] = renewed2[j] - part(j, 5)
-    near = jnp.concatenate(
-        around(change0, reach) + around(change1, reach) + around(change2, reach), axis=0
-    )
-    share = jnp.concatenate(
-        [keep[2 * group:3 * group, :], keep[3 * group:4 * group, :9 * group - LANES]], axis=1
-    )
-    current[0:group, :] = keep[0:group, :]
-    current[group:2 * group, :] = renewed1[reach]
-    current[2 * group:3 * group, :] = renewed2[reach]
+    lane = lax.broadcasted_iota(jnp.int32, (group, LANES), 1)
+    near = 3 * group
+
+    def band(share, begins, target):
+        kept = jnp.where((lane >= begins) & (lane < begins + near), share, 0.0)
+        return pltpu.roll(kept, (target - begins) % LANES, 1)
+
+    width = 2 * reach + 1
+    spare = jnp.zeros((LANES - width * group, LANES), jnp.float32)
+    first = jnp.maximum(block_of(level, 0), 0.0)
+    change0 = [
+        first - block_of(begin, 0) if j == reach else part(j, 0) for j in range(width)
+    ]
+    change0 = jnp.concatenate(change0 + [spare], axis=0)
+
+    inner = range(1, width - 1)
+    levels = [block_of(level, 1) if j == reach else part(j, 1) for j in inner]
+    shares = [block_of(links, 0) if j == reach else part(j, 2) for j in inner]
+    begins = [
+        part(1, 3), block_of(beside, 0), block_of(begin, 1), block_of(beside, 1), part(5, 3)
+    ]
+    shares = [band(share, 0, (j - 1) * group) for j, share in zip(inner, shares)]
+    renewed1 = jnp.maximum(
+        jnp.concatenate(levels, axis=0) - product(jnp.concatenate(shares, axis=0), change0), 0.0
+    )
+    change1 = renewed1 - jnp.concatenate(begins, axis=0)
+    spare = jnp.zeros((LANES - change1.shape[0], LANES), jnp.float32)
+    changes = jnp.concatenate([change0, change1, spare], axis=0)
+
+    inner = range(2, width - 2)
+    levels = [block_of(level, 2) if j == reach else part(j, 3) for j in inner]
+    shares = [block_of(links, 1) if j == reach else part(j, 4) for j in inner]
+    begins = [block_of(beside, 2), block_of(begin, 2), block_of(beside, 3)]
+    shares = [
+        jnp.concatenate(
+            [band(share, 0, (j - 1) * group), band(share, near, (j - 2) * group)], axis=1
+        )
+        for j, share in zip(inner, shares)
+    ]
+    renewed2 = jnp.maximum(
+        jnp.concatenate(levels, axis=0) - product(jnp.concatenate(shares, axis=0), changes), 0.0
+    )
+    change2 = renewed2 - jnp.concatenate(begins, axis=0)
+
+    middle = (reach - 1) * group
+    changes = jnp.concatenate(
+        [change0[middle:middle + near], change1[middle - group:middle - group + near], change2],
+        axis=0,
+    )
+    share = jnp.concatenate([block_of(links, 2), block_of(links, 3)], axis=1)
+    share = share[:, :3 * near]
+    current[0:group, :] = first
+    current[group:2 * group, :] = renewed1[middle:middle + group]
+    current[2 * group:3 * group, :] = renewed2[group:2 * group]
     current[3 * group:4 * group, :] = jnp.maximum(
-        keep[group:2 * group, :] - exact(share, near), 0.0
+        block_of(level, 3) - product(share, changes), 0.0
     )
     row = pl.multiple_of(lax.axis_index("ty") * block, block)
     ordered = jnp.concatenate(
         [current[pl.ds(q * group + row, block), :] for q in range(BLOCKS)], axis=0
     )
     place = lax.broadcasted_iota(jnp.int32, (slots, slots), 0) == order[...]
-    out[...] = exact(place.astype(jnp.float32), ordered)
-
-
-def call(kernel, outs, scratch, megabytes, space=pltpu.VMEM, cost=None):
+    out[...] = jnp.dot(
+        place.astype(jnp.float32), ordered, precision=precise, preferred_element_type=jnp.float32
+    )
+
+
+def call(kernel, outs, scratch, megabytes, spaces=None, cost=None):
     def run(*operands):
         return pl.pallas_call(
             kernel,
             out_shape=[jax.ShapeDtypeStruct(*out) for out in outs],
-            in_specs=[pl.BlockSpec(memory_space=space)] * len(operands),
+            in_specs=[
+                pl.BlockSpec(memory_space=space)
+                for space in spaces or [pltpu.VMEM] * len(operands)
+            ],
             out_specs=[pl.BlockSpec(memory_space=pltpu.VMEM)] * len(outs),
             scratch_shapes=scratch,
             compiler_params=pltpu.CompilerParams(vmem_limit_bytes=megabytes << 20),
@@ -428,14 +497,21 @@
     total = 6 * slots
     bf16, f32 = jnp.bfloat16, jnp.float32
 
-    def spread(values, top):
-        below = slots - top - values.shape[0]
-        return jnp.pad(values, ((top, below), (0, LANES - values.shape[1])))
-
-    numbers = spread(order[0], 0) + spread(centres[0, 0].T, 1) + spread(counts, 3)
-    packed = jnp.concatenate(
-        [footprints[0, 0], traces[0, 0], numbers.astype(bf16)], axis=1
-    )
+    given = (footprints[0, 0], traces[0, 0], order[0], centres[0, 0].T)
+    packed, ordering = call(
+        pack_kernel,
+        [((slots, area + 2 * LANES), bf16), ((1, slots), jnp.int32)],
+        [
+            pltpu.VMEM((slots, area), bf16),
+            pltpu.VMEM((slots, frames), bf16),
+            pltpu.VMEM((1, slots), jnp.int32),
+            pltpu.VMEM((2, slots), jnp.int32),
+            pltpu.VMEM((slots, LANES), f32),
+            pltpu.SemaphoreType.DMA((len(given),)),
+        ],
+        4,
+        [pltpu.SMEM] + [pltpu.HBM] * len(given),
+    )(counts, *(pltpu.with_memory_space_constraint(x, pltpu.HBM) for x in given))
     film = movie
     own = jnp.stack([packed, swap(packed)])
     pair_film = swap(film)
@@ -457,6 +533,7 @@
             ((2 * slots, frames), f32),
             ((2 * slots, frames), f32),
             ((2 * slots, frames), f32),
+            ((4 * group, frames), f32),
         ],
         [
             pltpu.VMEM((total * area // LANES, LANES), f32),
@@ -469,26 +546,32 @@
         16,
         cost=pl.CostEstimate(flops=4_000_000_000, bytes_accessed=0, transcendentals=0),
     )(own, direct, other)
-    far, far_short, keep = call(
+    mine, links, scale, begin, coupling, beside = painted
+    near, across, level = call(
         drive_kernel,
-        [((7 * group, frames), f32), ((4 * group, frames), f32), ((4 * group, frames), f32)],
+        [((5 * group, frames), f32), ((5 * group, frames), f32), ((4 * group, frames), f32)],
         [pltpu.VMEM((2 * height, 2 * PATCH, frames), bf16)],
         8,
-    )(*painted, film, pair_film, film_direct, film_other)
-
-    far0 = pairwise(far, OFFSETS[0])
-    far1 = pairwise(far_short, OFFSETS[1])
-    far2 = pairwise(far, OFFSETS[2])
-    came = jnp.concatenate([far0, far1, far2], axis=0)
+    )(mine, links, scale, begin, coupling, film, pair_film, film_direct, film_other)
+
+    near_direct = pairwise(near, EDGES)
+    across_direct = pairwise(across, ACROSS)
+    relay_direct = pairwise(near_direct, PLANES)
+    near_other = swap(near_direct)
+    across_other = swap(across_direct)
+    relay_other = swap(relay_direct)
     (result,) = call(
         sweep_kernel,
         [((slots, frames), f32)],
         [
-            pltpu.VMEM((2 * BLOCKS - 1, 7 * group, frames), f32),
+            pltpu.VMEM((2 * BLOCKS - 1, 5 * group, frames), f32),
             pltpu.VMEM((4 * group, frames), f32),
         ],
         4,
-    )(far, keep, came, swap(came), order[0])
+    )(
+        level, begin, links, beside, near_direct, near_other, across_direct, across_other,
+        relay_direct, relay_other, ordering,
+    )
     return result[None, None]
 
 

time: 38.7 us -> 37 us (0.956)
  the two profiles are of different devices: /device:TPU:7 before, /device:TPU:0 now
where the time goes in v4:
time: 37 us; the launch traced here: 36.4 us
  starting transfers between devices  14.2 us (38%)
  waiting for transfers between devices  12.9 us (35%)
  Pallas kernels  7.52 us (20%)
  local copies, waits for them, and re-layouts  0.94 us (3%)
  between operations  0.78 us (2%)
    ppermute x5, starting transfers between devices, pairwise(): return lax.ppermute(x, ('ty', 'tx'), pairs)  13 us
    ppermute x5, waiting for transfers between devices, pairwise(): return lax.ppermute(x, ('ty', 'tx'), pairs)  11.7 us
    pallas_call x4, Pallas kernels, run(): pl.pallas_call(kernel, out_shape=[jax.ShapeDtypeStruct(*out) for out in o...  7.52 us
    ppermute x7, starting transfers between devices, swap(): return lax.ppermute(x, 'ty', [(0, 1), (1, 0)])  1.23 us
    ppermute x7, waiting for transfers between devices, swap(): return lax.ppermute(x, 'ty', [(0, 1), (1, 0)])  1.23 us
    dynamic_slice x2, local copies, waits for them, and re-layouts, strip_body(): lax.dynamic_slice_in_dim(x, edge, half, axis=1)  0.93 us
  transfers between devices with their start and end apart: 12, of which 5 were waited for; matrix products, arithmetic and copies ran while one was open for 3% of the time, Pallas kernels for 13%

profile of v4, /device:TPU:0, one launch (start us, length us, event | category | flops | bytes accessed | tf_op | source)
XLA Modules:
  0.0 36.4 jit_solution(10424495857817775768)
XLA Ops:
  0.7 0.9 %shard_map.64 = (bf16[32,1280]{1,0:T(8,128)(2,1)S(1)}, s32[1,32]{1,0:T(1,128)S(1)}) custom-call(s32[1,1]{1,0:T(1,128)S(6)} %copy.7.counts, bf16[32,1024]{1,0:T(8,128)(2,1)} %bitcast.11, bf16[32,128]{1,0:T(8,128)(2,1)} %bitcast.12, s32[1,32]{1,0:T(1,128)} %bitcast.14, s32[2,32]{1,0:T(2,128)} %bitcast.13), custom_call_target="tpu_custom_call" | custom-call | tf_op jit(solution)/shard_map/pallas_call | solution.py:475
  1.6 0.6 %collective-permute-start = (bf16[32,1280]{1,0:T(8,128)(2,1)S(1)}, bf16[32,1280]{1,0:T(8,128)(2,1)S(1)}, u32[]{:S(2)}, u32[]{:S(2)}) collective-permute-start(bf16[32,1280]{1,0:T(8,128)(2,1)S(1)} %get-tuple-element.16), channel_id=1, source_target_pairs={{0,16},{16,0},{1,17},{17,1},{2,18},{18,2},{3,19},{19,3},{4,20},{20... | collective-permute-start | bytes 245768 | tf_op jit(solution)/shard_map/ppermute | solution.py:145
  2.1 0.1 collective-permute-start.3
  2.2 0.9 %constant_dynamic-slice_fusion.1 = bf16[32,16,128]{2,1,0:T(8,128)(2,1)S(1)} fusion(bf16[32,32,128]{2,1,0:T(8,128)(2,1)} %film_own.1, s32[]{:T(128)S(6)} %select_n.36), kind=kLoop, calls=%fused_computation.3 | loop fusion | bytes 262148 | tf_op jit(solution)/shard_map/dynamic_slice | solution.py:521
  3.1 0.0 collective-permute-done
  3.2 4.8 %collective-permute-start.1 = (bf16[2,32,1280]{2,1,0:T(8,128)(2,1)S(1)}, bf16[2,32,1280]{2,1,0:T(8,128)(2,1)S(1)}, u32[]{:S(2)}, u32[]{:S(2)}) collective-permute-start(bf16[2,32,1280]{2,1,0:T(8,128)(2,1)S(1)} %pad_maximum_fusion.1.own), channel_id=1, source_target_pairs={{0,1},{1,0},{2,3},{3,2},{4,5},{5,4},{6,7},{7,6},{8,9},{9,8},{10,11... | collective-permute-start | bytes 491528 | tf_op jit(solution)/shard_map/ppermute | solution.py:156
  8.0 0.0 collective-permute-done.3.film_pair
  8.1 0.0 copy-start
  8.1 2.1 %collective-permute-start.4 = (bf16[64,16,128]{2,1,0:T(8,128)(2,1)S(1)}, bf16[64,16,128]{2,1,0:T(8,128)(2,1)S(1)}, u32[]{:S(2)}, u32[]{:S(2)}) collective-permute-start(bf16[64,16,128]{2,1,0:T(8,128)(2,1)S(1)} %pad_maximum_fusion), channel_id=1, source_target_pairs={{0,1},{1,0},{2,3},{3,2},{4,5},{5,4},{6,7},{7,6},{8,9},{9,8},{10,11... | collective-permute-start | bytes 786440 | tf_op jit(solution)/shard_map/ppermute | solution.py:156
  10.1 2.4 %collective-permute-done.1.direct = bf16[2,32,1280]{2,1,0:T(8,128)(2,1)S(1)} collective-permute-done((bf16[2,32,1280]{2,1,0:T(8,128)(2,1)S(1)}, bf16[2,32,1280]{2,1,0:T(8,128)(2,1)S(1)}, u32[]{:S(2)}, u32[]{:S(2)}) %collective-permute-start.1) | collective-permute-done | bytes 163872 | tf_op jit(solution)/shard_map/ppermute | solution.py:156
  12.6 0.0 collective-permute-start.2
  12.6 6.4 %collective-permute-done.4.film_direct = bf16[64,16,128]{2,1,0:T(8,128)(2,1)S(1)} collective-permute-done((bf16[64,16,128]{2,1,0:T(8,128)(2,1)S(1)}, bf16[64,16,128]{2,1,0:T(8,128)(2,1)S(1)}, u32[]{:S(2)}, u32[]{:S(2)}) %collective-permute-start.4) | collective-permute-done | bytes 262176 | tf_op jit(solution)/shard_map/ppermute | solution.py:156
  19.0 0.0 collective-permute-start.5
  19.0 0.0 collective-permute-done.2.other
  19.0 4.7 %shard_map.65 = (bf16[16,64,256]{2,1,0:T(8,128)(2,1)S(1)}, f32[64,128]{1,0:T(8,128)S(1)}, f32[64,128]{1,0:T(8,128)S(1)}, f32[64,128]{1,0:T(8,128)S(1)}, f32[64,128]{1,0:T(8,128)S(1)}, /*index=5*/f32[64,128]{1,0:T(8,128)S(1)}) custom-call(bf16[2,32,1280]{2,1,0:T(8,128)(2,1)S(1)} %pad_maximum_fusion.1.own, ...), custom_call_target="tpu_custom_call" | custom-call | flops 4000000000 | tf_op jit(solution)/shard_map/pallas_call | solution.py:475
  23.8 0.0 collective-permute-done.5.film_other
  23.8 0.0 copy-done
  23.8 0.5 %shard_map.66 = (f32[80,128]{1,0:T(8,128)S(1)}, f32[80,128]{1,0:T(8,128)S(1)}, f32[64,128]{1,0:T(8,128)S(1)}) custom-call(bf16[16,64,256]{2,1,0:T(8,128)(2,1)S(1)} %get-tuple-element.17.mine, f32[64,128]{1,0:T(8,128)S(1)} %get-tuple-element.18.links, f32[64,128]{1,0:T(8,128)S(1)} %get-tuple-element.19.scale, f32[64,128]{1,0:T(8,128)S(1)} %get-tuple-element.20.begin, ...), custom_call_target="tpu_custom_call" | custom-call | tf_op jit(solution)/shard_map/pallas_call | solution.py:475
  24.3 1.7 %collective-permute-start.6 = (f32[80,128]{1,0:T(8,128)S(1)}, f32[80,128]{1,0:T(8,128)S(1)}, u32[]{:S(2)}, u32[]{:S(2)}) collective-permute-start(f32[80,128]{1,0:T(8,128)S(1)} %get-tuple-element.24), channel_id=1, source_target_pairs={{0,1},{1,0},{2,3},{3,2},{4,5},{5,4},{6,7},{7,6},{8,9},{9,8},{10,11... | collective-permute-start | bytes 122888 | tf_op jit(solution)/shard_map/ppermute | solution.py:156
  26.0 0.7 %collective-permute-start.8 = (f32[80,128]{1,0:T(8,128)S(1)}, f32[80,128]{1,0:T(8,128)S(1)}, u32[]{:S(2)}, u32[]{:S(2)}) collective-permute-start(f32[80,128]{1,0:T(8,128)S(1)} %get-tuple-element.25), channel_id=1, source_target_pairs={{2,5},{3,4},{4,3},{5,2},{6,9},{7,8},{8,7},{9,6},{10,13},{11,12},{1... | collective-permute-start | bytes 122888 | tf_op jit(solution)/shard_map/ppermute | solution.py:156
  26.7 1.7 %collective-permute-done.6.near_direct = f32[80,128]{1,0:T(8,128)S(1)} collective-permute-done((f32[80,128]{1,0:T(8,128)S(1)}, f32[80,128]{1,0:T(8,128)S(1)}, u32[]{:S(2)}, u32[]{:S(2)}) %collective-permute-start.6) | collective-permute-done | bytes 40992 | tf_op jit(solution)/shard_map/ppermute | solution.py:156
  28.4 3.7 %collective-permute-start.10 = (f32[80,128]{1,0:T(8,128)S(1)}, f32[80,128]{1,0:T(8,128)S(1)}, u32[]{:S(2)}, u32[]{:S(2)}) collective-permute-start(f32[80,128]{1,0:T(8,128)S(1)} %collective-permute-done.6.near_direct), channel_id=1, source_target_pairs={{0,4},{2,6},{4,8},{5,1},{6,10},{7,3},{8,12},{9,5},{10,14},{11,7},{... | collective-permute-start | bytes 122888 | tf_op jit(solution)/shard_map/ppermute | solution.py:156
  32.1 0.5 %collective-permute-start.7 = (f32[80,128]{1,0:T(8,128)S(1)}, f32[80,128]{1,0:T(8,128)S(1)}, u32[]{:S(2)}, u32[]{:S(2)}) collective-permute-start(f32[80,128]{1,0:T(8,128)S(1)} %collective-permute-done.6.near_direct), channel_id=1, source_target_pairs={{0,16},{16,0},{1,17},{17,1},{2,18},{18,2},{3,19},{19,3},{4,20},{20... | collective-permute-start | bytes 122888 | tf_op jit(solution)/shard_map/ppermute | solution.py:145
  32.6 0.0 collective-permute-done.8.across_direct
  32.6 0.1 collective-permute-start.9
  32.7 1.1 %collective-permute-done.10.relay_direct = f32[80,128]{1,0:T(8,128)S(1)} collective-permute-done((f32[80,128]{1,0:T(8,128)S(1)}, f32[80,128]{1,0:T(8,128)S(1)}, u32[]{:S(2)}, u32[]{:S(2)}) %collective-permute-start.10) | collective-permute-done | bytes 40992 | tf_op jit(solution)/shard_map/ppermute | solution.py:156
  33.8 0.0 collective-permute-start.11
  33.8 0.0 collective-permute-done.7.near_other
  33.8 0.0 collective-permute-done.9.across_other
  33.8 1.2 %collective-permute-done.11.relay_other = f32[80,128]{1,0:T(8,128)S(1)} collective-permute-done((f32[80,128]{1,0:T(8,128)S(1)}, f32[80,128]{1,0:T(8,128)S(1)}, u32[]{:S(2)}, u32[]{:S(2)}) %collective-permute-start.11) | collective-permute-done | bytes 40992 | tf_op jit(solution)/shard_map/ppermute | solution.py:145
  35.0 1.4 %shard_map.67 = f32[32,128]{1,0:T(8,128)} custom-call(f32[64,128]{1,0:T(8,128)S(1)} %get-tuple-element.22.level, f32[64,128]{1,0:T(8,128)S(1)} %get-tuple-element.20.begin, f32[64,128]{1,0:T(8,128)S(1)} %get-tuple-element.18.links, f32[64,128]{1,0:T(8,128)S(1)} %get-tuple-element.23.beside, f32[80,128]{1,0:T(8,128)S(1)} %collective-permute-done.6.near_direct, ...), custom_call_target="tpu_custom_call" | custom-call | tf_op jit(solution)/shard_map/pallas_call | solution.py:475
  (3 shorter events, 0.1 us)
Async XLA Ops:
  1.6 1.6 %collective-permute-start = (bf16[32,1280]{1,0:T(8,128)(2,1)S(1)}, bf16[32,1280]{1,0:T(8,128)(2,1)S(1)}, u32[]{:S(2)}, u32[]{:S(2)}) collective-permute-start(bf16[32,1280]{1,0:T(8,128)(2,1)S(1)} %get-tuple-element.16), channel_id=1, source_target_pairs={{0,16},{16,0},{1,17},{17,1},{2,18},{18,2},{3,19},{19,3},{4,20},{20... | collective-permute-start | bytes 245768 | tf_op jit(solution)/shard_map/ppermute | solution.py:145
  2.1 5.9 %collective-permute-start.3 = (bf16[32,32,128]{2,1,0:T(8,128)(2,1)}, bf16[32,32,128]{2,1,0:T(8,128)(2,1)S(1)}, u32[]{:S(2)}, u32[]{:S(2)}) collective-permute-start(bf16[32,32,128]{2,1,0:T(8,128)(2,1)} %film_own.1), channel_id=1, source_target_pairs={{0,16},{16,0},{1,17},{17,1},{2,18},{18,2},{3,19},{19,3},{4,20},{20... | collective-permute-start | bytes 786440 | tf_op jit(solution)/shard_map/ppermute | solution.py:145
  3.2 9.4 %collective-permute-start.1 = (bf16[2,32,1280]{2,1,0:T(8,128)(2,1)S(1)}, bf16[2,32,1280]{2,1,0:T(8,128)(2,1)S(1)}, u32[]{:S(2)}, u32[]{:S(2)}) collective-permute-start(bf16[2,32,1280]{2,1,0:T(8,128)(2,1)S(1)} %pad_maximum_fusion.1.own), channel_id=1, source_target_pairs={{0,1},{1,0},{2,3},{3,2},{4,5},{5,4},{6,7},{7,6},{8,9},{9,8},{10,11... | collective-permute-start | bytes 491528 | tf_op jit(solution)/shard_map/ppermute | solution.py:156
  8.1 15.7 %copy-start = (bf16[32,32,128]{2,1,0:T(8,128)(2,1)S(1)}, bf16[32,32,128]{2,1,0:T(8,128)(2,1)}, u32[]{:S(2)}) copy-start(bf16[32,32,128]{2,1,0:T(8,128)(2,1)} %film_own.1) | copy-start | bytes 786436
  8.1 10.9 %collective-permute-start.4 = (bf16[64,16,128]{2,1,0:T(8,128)(2,1)S(1)}, bf16[64,16,128]{2,1,0:T(8,128)(2,1)S(1)}, u32[]{:S(2)}, u32[]{:S(2)}) collective-permute-start(bf16[64,16,128]{2,1,0:T(8,128)(2,1)S(1)} %pad_maximum_fusion), channel_id=1, source_target_pairs={{0,1},{1,0},{2,3},{3,2},{4,5},{5,4},{6,7},{7,6},{8,9},{9,8},{10,11... | collective-permute-start | bytes 786440 | tf_op jit(solution)/shard_map/ppermute | solution.py:156
  12.6 6.5 %collective-permute-start.2 = (bf16[2,32,1280]{2,1,0:T(8,128)(2,1)S(1)}, bf16[2,32,1280]{2,1,0:T(8,128)(2,1)S(1)}, u32[]{:S(2)}, u32[]{:S(2)}) collective-permute-start(bf16[2,32,1280]{2,1,0:T(8,128)(2,1)S(1)} %collective-permute-done.1.direct), channel_id=1, source_target_pairs={{0,16},{16,0},{1,17},{17,1},{2,18},{18,2},{3,19},{19,3},{4,20},{20... | collective-permute-start | bytes 491528 | tf_op jit(solution)/shard_map/ppermute | solution.py:145
  19.0 4.8 %collective-permute-start.5 = (bf16[64,16,128]{2,1,0:T(8,128)(2,1)S(1)}, bf16[64,16,128]{2,1,0:T(8,128)(2,1)S(1)}, u32[]{:S(2)}, u32[]{:S(2)}) collective-permute-start(bf16[64,16,128]{2,1,0:T(8,128)(2,1)S(1)} %collective-permute-done.4.film_direct), channel_id=1, source_target_pairs={{0,16},{16,0},{1,17},{17,1},{2,18},{18,2},{3,19},{19,3},{4,20},{20... | collective-permute-start | bytes 786440 | tf_op jit(solution)/shard_map/ppermute | solution.py:145
  24.3 4.1 %collective-permute-start.6 = (f32[80,128]{1,0:T(8,128)S(1)}, f32[80,128]{1,0:T(8,128)S(1)}, u32[]{:S(2)}, u32[]{:S(2)}) collective-permute-start(f32[80,128]{1,0:T(8,128)S(1)} %get-tuple-element.24), channel_id=1, source_target_pairs={{0,1},{1,0},{2,3},{3,2},{4,5},{5,4},{6,7},{7,6},{8,9},{9,8},{10,11... | collective-permute-start | bytes 122888 | tf_op jit(solution)/shard_map/ppermute | solution.py:156
  26.0 6.6 %collective-permute-start.8 = (f32[80,128]{1,0:T(8,128)S(1)}, f32[80,128]{1,0:T(8,128)S(1)}, u32[]{:S(2)}, u32[]{:S(2)}) collective-permute-start(f32[80,128]{1,0:T(8,128)S(1)} %get-tuple-element.25), channel_id=1, source_target_pairs={{2,5},{3,4},{4,3},{5,2},{6,9},{7,8},{8,7},{9,6},{10,13},{11,12},{1... | collective-permute-start | bytes 122888 | tf_op jit(solution)/shard_map/ppermute | solution.py:156
  28.4 5.4 %collective-permute-start.10 = (f32[80,128]{1,0:T(8,128)S(1)}, f32[80,128]{1,0:T(8,128)S(1)}, u32[]{:S(2)}, u32[]{:S(2)}) collective-permute-start(f32[80,128]{1,0:T(8,128)S(1)} %collective-permute-done.6.near_direct), channel_id=1, source_target_pairs={{0,4},{2,6},{4,8},{5,1},{6,10},{7,3},{8,12},{9,5},{10,14},{11,7},{... | collective-permute-start | bytes 122888 | tf_op jit(solution)/shard_map/ppermute | solution.py:156
  32.1 1.7 %collective-permute-start.7 = (f32[80,128]{1,0:T(8,128)S(1)}, f32[80,128]{1,0:T(8,128)S(1)}, u32[]{:S(2)}, u32[]{:S(2)}) collective-permute-start(f32[80,128]{1,0:T(8,128)S(1)} %collective-permute-done.6.near_direct), channel_id=1, source_target_pairs={{0,16},{16,0},{1,17},{17,1},{2,18},{18,2},{3,19},{19,3},{4,20},{20... | collective-permute-start | bytes 122888 | tf_op jit(solution)/shard_map/ppermute | solution.py:145
  32.6 1.2 %collective-permute-start.9 = (f32[80,128]{1,0:T(8,128)S(1)}, f32[80,128]{1,0:T(8,128)S(1)}, u32[]{:S(2)}, u32[]{:S(2)}) collective-permute-start(f32[80,128]{1,0:T(8,128)S(1)} %collective-permute-done.8.across_direct), channel_id=1, source_target_pairs={{0,16},{16,0},{1,17},{17,1},{2,18},{18,2},{3,19},{19,3},{4,20},{20... | collective-permute-start | bytes 122888 | tf_op jit(solution)/shard_map/ppermute | solution.py:145
  33.8 1.2 %collective-permute-start.11 = (f32[80,128]{1,0:T(8,128)S(1)}, f32[80,128]{1,0:T(8,128)S(1)}, u32[]{:S(2)}, u32[]{:S(2)}) collective-permute-start(f32[80,128]{1,0:T(8,128)S(1)} %collective-permute-done.10.relay_direct), channel_id=1, source_target_pairs={{0,16},{16,0},{1,17},{17,1},{2,18},{18,2},{3,19},{19,3},{4,20},{20... | collective-permute-start | bytes 122888 | tf_op jit(solution)/shard_map/ppermute | solution.py:145

commit v5 on v4

--- a/solution.py
+++ b/solution.py
@@ -130,7 +130,6 @@
     return result[None, None]
 
 
-BESIDE = ((1, -1, 1, -1), (-1, 1, -1, 1))
 EDGES = ((1, -1, 1, -1), (2, 2, -2, -2))
 ACROSS = ((-1, -3, 3, 1), (3, 1, -1, -3))
 PLANES = ((4, -4, 4, -4), (4, 4, -4, -4))
@@ -145,15 +144,30 @@
     return lax.ppermute(x, "ty", [(0, 1), (1, 0)])
 
 
+def beside(x):
+    count = lax.axis_size("tx")
+    ring = list(range(count)) + list(range(2 * count - 1, count - 1, -1))
+    return lax.ppermute(x, ("ty", "tx"), list(zip(ring, ring[1:] + ring[:1])))
+
+
 def pairwise(x, offsets):
     count = lax.axis_size("tx")
     pairs = []
     for core, steps in enumerate(offsets):
-        for i in range(count):
-            other = i + steps[i % len(steps)]
-            if 0 <= other < count:
-                pairs.append((core * count + i, core * count + other))
+        targets = [i + steps[i % len(steps)] for i in range(count)]
+        used = [i for i in range(count) if 0 <= targets[i] < count]
+        free = sorted(set(range(count)) - {targets[i] for i in used})
+        idle = [i for i in range(count) if i not in used]
+        if any(i == j for i, j in zip(idle, free)):
+            free = [free[k ^ 1] if k ^ 1 < len(free) else free[k] for k in range(len(free))]
+        for i, j in [(i, targets[i]) for i in used] + list(zip(idle, free)):
+            pairs.append((core * count + i, core * count + j))
     return lax.ppermute(x, ("ty", "tx"), pairs)
+
+
+def exists(step):
+    column = lax.axis_index("tx") + step
+    return (column >= 0) & (column < lax.axis_size("tx"))
 
 
 def partner(offsets):
@@ -169,21 +183,22 @@
 
 
 def pack_kernel(
-    counts, footprints, traces, order, centres,
-    packed, ordering, patch_buf, trace_buf, order_buf, centre_buf, numbers, sems,
+    counts, footprints, traces, order, centres, movie,
+    packed, ordering, film, patch_buf, trace_buf, order_buf, centre_buf, numbers, sems,
 ):
     pairs = (
         (order, order_buf),
         (centres, centre_buf),
         (footprints, patch_buf),
         (traces, trace_buf),
+        (movie, film),
     )
     copies = [pltpu.make_async_copy(a, b, sems.at[i]) for i, (a, b) in enumerate(pairs)]
     for copy in copies:
         copy.start()
     slots, width = patch_buf.shape
     numbers[...] = jnp.zeros_like(numbers)
-    for copy in copies:
+    for copy in copies[:4]:
         copy.wait()
     numbers[0:1, 0:slots] = order_buf[...].astype(jnp.float32)
     numbers[1:3, 0:slots] = centre_buf[...].astype(jnp.float32)
@@ -192,29 +207,22 @@
     packed[:, :width] = patch_buf[...]
     packed[:, width:width + LANES] = trace_buf[...]
     packed[:, width + LANES:] = numbers[...].astype(jnp.bfloat16)
-
-
-def paint_kernel(
-    own, direct, other, mine, links, scale, begin, coupling, beside,
-    patches, canvas, start, numbers, table, sem,
+    copies[4].wait()
+
+
+def paint_tiles(
+    sources, rows, columns, canvas, start, patches, numbers, table, sem, prepare=None
 ):
-    slots = own.shape[1]
-    tiles = 6
-    total = tiles * slots
+    slots = sources[0][0].shape[1]
+    total = start.shape[0]
     block = slots // BLOCKS
     group = 2 * block
     source = 3 * group
     pixels = PATCH * PATCH // LANES
     width = pixels * LANES
-    depth = canvas.shape[0] // total
-    sources = ((own, 0), (own, 1), (direct, 0), (direct, 1), (other, 0), (other, 1))
-    core = lax.axis_index("ty")
-    step_direct, step_other = partner(BESIDE)
-    tile_rows = (core, 1 - core, core, 1 - core, 1 - core, core)
-    tile_cols = (0, 0, step_direct, step_direct, step_other, step_other)
 
     heads = [ref[u, 0:16, width + LANES:].astype(jnp.float32) for ref, u in sources]
-    spare = [jnp.zeros((8 - tiles, LANES), jnp.float32)]
+    spare = [jnp.zeros((8 - len(sources), LANES), jnp.float32)]
     ordering, top, left, count = (
         jnp.concatenate([head[i:i + 1, :] for head in heads] + spare, axis=0).astype(jnp.int32)
         for i in range(4)
@@ -222,9 +230,10 @@
     row = lax.broadcasted_iota(jnp.int32, (8, LANES), 0)
     tile_row = jnp.zeros((8, LANES), jnp.int32)
     tile_col = jnp.zeros((8, LANES), jnp.int32)
-    for t in range(tiles):
-        tile_row = jnp.where(row == t, tile_rows[t], tile_row)
-        tile_col = jnp.where(row == t, tile_cols[t], tile_col)
+    for t in range(len(sources)):
+        tile_row = jnp.where(row == t, rows[t], tile_row)
+        tile_col = jnp.where(row == t, columns[t], tile_col)
+        count = jnp.where((row == t) & jnp.logical_not(exists(columns[t])), 0, count)
     slot_of = lax.broadcasted_iota(jnp.int32, (8, LANES), 1)
     live = (ordering < count[:, 0:1]).astype(jnp.int32)
     top = take_lanes(top, ordering) + tile_row * PATCH
@@ -245,7 +254,8 @@
     fetch = pltpu.make_async_copy(numbers, table, sem)
     fetch.start()
 
-    canvas[...] = jnp.zeros_like(canvas)
+    if prepare is not None:
+        prepare()
     for t, (ref, u) in enumerate(sources):
         for k in range(pixels):
             patches[pl.ds(t * slots * pixels + k, slots, stride=pixels), :] = ref[
@@ -260,7 +270,7 @@
             preferred_element_type=jnp.float32,
         )
         for q in range(BLOCKS):
-            at = q * source + (tile_cols[t] + 1) * group + tile_rows[t] * block
+            at = q * source + (columns[t] + 1) * group + rows[t] * block
             start[pl.ds(pl.multiple_of(at, block), block), :] = trail[q * block:(q + 1) * block]
     fetch.wait()
 
@@ -270,26 +280,56 @@
     low_first = low & (sub == 0)
     inner = lane & (LANES // 2 - 1)
 
-    def paint(t, s):
-        origin, at, begins, ends, odd_row, *turns = (
-            table[i * 8 + t, s] for i in range(len(fields))
-        )
-        value = patches[pl.ds(pl.multiple_of(origin, pixels), pixels), :]
-        turned = [pltpu.roll(value, turn, 1) for turn in turns]
-        down = pltpu.roll(turned[0], 1, 0)
-        is_odd = jnp.broadcast_to(odd_row, sub.shape) > 0
-        inside = (inner >= begins) & (inner < ends)
-        first = jnp.where(is_odd, jnp.where(sub == 0, 0.0, down), turned[0])
-        even_rows = jnp.where(low, first, turned[1])
-        odd_rows = jnp.where(low, turned[2], turned[3])
-        last = jnp.where(inside & low_first & is_odd, down, 0.0)
-        canvas[pl.ds(at, pixels, stride=2 * total), :] = jnp.where(inside, even_rows, 0.0)
-        canvas[pl.ds(at + total, pixels, stride=2 * total), :] = jnp.where(inside, odd_rows, 0.0)
-        canvas[pl.ds(at + 2 * pixels * total, 1), :] = last[0:1, :]
-
-    for t in range(tiles):
+    for t in range(len(sources)):
         for s in range(slots):
-            paint(t, s)
+            origin, at, begins, ends, odd_row, *turns = (
+                table[i * 8 + t, s] for i in range(len(fields))
+            )
+            value = patches[pl.ds(pl.multiple_of(origin, pixels), pixels), :]
+            turned = [pltpu.roll(value, turn, 1) for turn in turns]
+            down = pltpu.roll(turned[0], 1, 0)
+            is_odd = jnp.broadcast_to(odd_row, sub.shape) > 0
+            inside = (inner >= begins) & (inner < ends)
+            first = jnp.where(is_odd, jnp.where(sub == 0, 0.0, down), turned[0])
+            even_rows = jnp.where(inside, jnp.where(low, first, turned[1]), 0.0)
+            odd_rows = jnp.where(inside, jnp.where(low, turned[2], turned[3]), 0.0)
+            last = jnp.where(inside & low_first & is_odd, down, 0.0)
+            canvas[pl.ds(at, pixels, stride=2 * total), :] = even_rows
+            canvas[pl.ds(at + total, pixels, stride=2 * total), :] = odd_rows
+            canvas[pl.ds(at + 2 * pixels * total, 1), :] = last[0:1, :]
+
+
+def own_kernel(own, canvas, start, patches, numbers, table, sem):
+    core = lax.axis_index("ty")
+
+    def clear():
+        canvas[...] = jnp.zeros_like(canvas)
+
+    paint_tiles(
+        ((own, 0), (own, 1)), (core, 1 - core), (0, 0),
+        canvas, start, patches, numbers, table, sem, clear,
+    )
+
+
+def near_kernel(
+    canvas_own, start_own, direct, other,
+    canvas, start, mine, links, scale, begin, coupling, begin_near,
+    patches, numbers, table, sem,
+):
+    slots = direct.shape[1]
+    total = start.shape[0]
+    group = 2 * slots // BLOCKS
+    source = 3 * group
+    depth = canvas.shape[0] // total
+    core = lax.axis_index("ty")
+    step_direct = 2 * core - 1
+    step_other = -step_direct
+    paint_tiles(
+        ((direct, 0), (direct, 1), (other, 0), (other, 1)),
+        (core, 1 - core, 1 - core, core),
+        (step_direct, step_direct, step_other, step_other),
+        canvas, start, patches, numbers, table, sem,
+    )
 
     margins = jnp.zeros((2 * slots, total), jnp.float32)
     edge = PATCH // 8
@@ -321,7 +361,8 @@
     for i, q in enumerate((1, 2)):
         for side in range(2):
             at = q * source + 2 * side * group
-            beside[(2 * i + side) * group:(2 * i + side + 1) * group, :] = start[at:at + group, :]
+            row = (2 * i + side) * group
+            begin_near[row:row + group, :] = start[at:at + group, :]
     share = margins / diagonal
     for i, q in enumerate((1, 2, 3)):
         links[i * group:(i + 1) * group, :] = share[q * group:(q + 1) * group, :LANES]
@@ -333,7 +374,8 @@
     near, across, level, film,
 ):
     core = lax.axis_index("ty")
-    side_direct, side_other = partner(BESIDE)
+    side_direct = 2 * core - 1
+    side_other = -side_direct
     height = film_own.shape[0]
     half = PATCH // 2
     group = links.shape[0] // 4
@@ -347,6 +389,7 @@
         for u in range(2):
             row = row_of(nearest if u == 0 else 1 - nearest)
             part = ref[u * height:(u + 1) * height]
+            part = jnp.where(exists(side), part, jnp.zeros_like(part))
 
             @pl.when(side < 0)
             def _():
@@ -374,7 +417,7 @@
 
 
 def sweep_kernel(
-    level, begin, links, beside, near_direct, near_other, across_direct, across_other,
+    level, begin, links, begin_near, near_direct, near_other, across_direct, across_other,
     relay_direct, relay_other, order, out, box, current,
 ):
     slots = out.shape[0]
@@ -384,7 +427,7 @@
     refs = (near_direct, near_other, across_direct, across_other, relay_direct, relay_other)
     steps = (*partner(EDGES), *partner(ACROSS), *partner(RELAYED))
     for ref, step in zip(refs, steps):
-        box[reach + step] = ref[...]
+        box[reach + step] = jnp.where(exists(step), ref[...], 0.0)
 
     def halves(x):
         high = x.astype(jnp.bfloat16)
@@ -422,7 +465,7 @@
     levels = [block_of(level, 1) if j == reach else part(j, 1) for j in inner]
     shares = [block_of(links, 0) if j == reach else part(j, 2) for j in inner]
     begins = [
-        part(1, 3), block_of(beside, 0), block_of(begin, 1), block_of(beside, 1), part(5, 3)
+        part(1, 3), block_of(begin_near, 0), block_of(begin, 1), block_of(begin_near, 1), part(5, 3)
     ]
     shares = [band(share, 0, (j - 1) * group) for j, share in zip(inner, shares)]
     renewed1 = jnp.maximum(
@@ -435,7 +478,7 @@
     inner = range(2, width - 2)
     levels = [block_of(level, 2) if j == reach else part(j, 3) for j in inner]
     shares = [block_of(links, 1) if j == reach else part(j, 4) for j in inner]
-    begins = [block_of(beside, 2), block_of(begin, 2), block_of(beside, 3)]
+    begins = [block_of(begin_near, 2), block_of(begin, 2), block_of(begin_near, 3)]
     shares = [
         jnp.concatenate(
             [band(share, 0, (j - 1) * group), band(share, near, (j - 2) * group)], axis=1
@@ -470,7 +513,7 @@
     )
 
 
-def call(kernel, outs, scratch, megabytes, spaces=None, cost=None):
+def call(kernel, outs, scratch, megabytes, spaces=None, cost=None, aliases={}):
     def run(*operands):
         return pl.pallas_call(
             kernel,
@@ -483,6 +526,7 @@
             scratch_shapes=scratch,
             compiler_params=pltpu.CompilerParams(vmem_limit_bytes=megabytes << 20),
             cost_estimate=cost,
+            input_output_aliases=aliases,
         )(*operands)
 
     return run
@@ -497,10 +541,10 @@
     total = 6 * slots
     bf16, f32 = jnp.bfloat16, jnp.float32
 
-    given = (footprints[0, 0], traces[0, 0], order[0], centres[0, 0].T)
-    packed, ordering = call(
+    given = (footprints[0, 0], traces[0, 0], order[0], centres[0, 0].T, movie)
+    packed, ordering, film = call(
         pack_kernel,
-        [((slots, area + 2 * LANES), bf16), ((1, slots), jnp.int32)],
+        [((slots, area + 2 * LANES), bf16), ((1, slots), jnp.int32), (movie.shape, bf16)],
         [
             pltpu.VMEM((slots, area), bf16),
             pltpu.VMEM((slots, frames), bf16),
@@ -512,22 +556,39 @@
         4,
         [pltpu.SMEM] + [pltpu.HBM] * len(given),
     )(counts, *(pltpu.with_memory_space_constraint(x, pltpu.HBM) for x in given))
-    film = movie
     own = jnp.stack([packed, swap(packed)])
     pair_film = swap(film)
-    direct = pairwise(own, BESIDE)
-    edge = jnp.where(partner(BESIDE)[0] > 0, half, 0)
+    direct = beside(own)
+    edge = jnp.where(lax.axis_index("ty") == 0, half, 0)
     edges = jnp.concatenate(
         [lax.dynamic_slice_in_dim(x, edge, half, axis=1) for x in (film, pair_film)], axis=0
     )
-    film_direct = pairwise(edges, BESIDE)
+    film_direct = beside(edges)
     other = swap(direct)
     film_other = swap(film_direct)
 
-    canvas_rows = (2 * height + PATCH) // 2
-    painted = call(
-        paint_kernel,
+    canvas = ((2 * height + PATCH) // 2 * total, LANES)
+
+    def painting(tiles):
+        return [
+            pltpu.VMEM((tiles * slots * area // LANES, LANES), f32),
+            pltpu.VMEM((72, LANES), jnp.int32),
+            pltpu.SMEM((72, LANES), jnp.int32),
+            pltpu.SemaphoreType.DMA,
+        ]
+
+    own_canvas, own_start = call(
+        own_kernel,
+        [(canvas, f32), ((total, frames), f32)],
+        painting(2),
+        4,
+        cost=pl.CostEstimate(flops=1_500_000_000, bytes_accessed=0, transcendentals=0),
+    )(own)
+    *_, mine, links, scale, begin, coupling, begin_near = call(
+        near_kernel,
         [
+            (canvas, f32),
+            ((total, frames), f32),
             ((height // 2, 2 * slots, 2 * LANES), bf16),
             ((4 * group, LANES), f32),
             ((2 * slots, frames), f32),
@@ -535,18 +596,11 @@
             ((2 * slots, frames), f32),
             ((4 * group, frames), f32),
         ],
-        [
-            pltpu.VMEM((total * area // LANES, LANES), f32),
-            pltpu.VMEM((canvas_rows * total, LANES), f32),
-            pltpu.VMEM((total, frames), f32),
-            pltpu.VMEM((72, LANES), jnp.int32),
-            pltpu.SMEM((72, LANES), jnp.int32),
-            pltpu.SemaphoreType.DMA,
-        ],
-        16,
-        cost=pl.CostEstimate(flops=4_000_000_000, bytes_accessed=0, transcendentals=0),
-    )(own, direct, other)
-    mine, links, scale, begin, coupling, beside = painted
+        painting(4),
+        8,
+        cost=pl.CostEstimate(flops=3_000_000_000, bytes_accessed=0, transcendentals=0),
+        aliases={0: 0, 1: 1},
+    )(own_canvas, own_start, direct, other)
     near, across, level = call(
         drive_kernel,
         [((5 * group, frames), f32), ((5 * group, frames), f32), ((4 * group, frames), f32)],
@@ -569,7 +623,7 @@
         ],
         4,
     )(
-        level, begin, links, beside, near_direct, near_other, across_direct, across_other,
+        level, begin, links, begin_near, near_direct, near_other, across_direct, across_other,
         relay_direct, relay_other, ordering,
     )
     return result[None, None]

time: 37 us -> 32 us (0.86); the launches traced: 36.4 us -> 31.9 us
  starting transfers between devices: 14.2 us -> 9.54 us
  Pallas kernels: 7.52 us -> 8.85 us
  local copies, waits for them, and re-layouts: 0.94 us -> 0.02 us
    ppermute x5 -> x3, starting transfers between devices: 13 us -> 4.19 us  [pairwise(): return lax.ppermute(x, ('ty', 'tx'), pairs)]
    ppermute x5 -> x3, waiting for transfers between devices: 11.7 us -> 4.24 us  [pairwise(): return lax.ppermute(x, ('ty', 'tx'), pairs)]
    ppermute x0 -> x2, waiting for transfers between devices: none -> 6.4 us  [beside(): return lax.ppermute(x, ('ty', 'tx'), list(zip(ring, ring[1:] + ring[:1])))]
    ppermute x0 -> x2, starting transfers between devices: none -> 4.43 us  [beside(): return lax.ppermute(x, ('ty', 'tx'), list(zip(ring, ring[1:] + ring[:1])))]
    pallas_call x4 -> x5, Pallas kernels: 7.52 us -> 8.85 us  [run(): pl.pallas_call(kernel, out_shape=[jax.ShapeDtypeStruct(*out) for out in o...]
    dynamic_slice x2, local copies, waits for them, and re-layouts: 0.93 us -> 0.02 us  [strip_body(): lax.dynamic_slice_in_dim(x, edge, half, axis=1)]
    ppermute x7, waiting for transfers between devices: 1.23 us -> 2.05 us  [swap(): return lax.ppermute(x, 'ty', [(0, 1), (1, 0)])]
  transfers between devices with their start and end apart: 12 -> 12, of which waited for: 5 -> 7; matrix products, arithmetic and copies ran while one was open for 3% -> 0% of each run, Pallas kernels for 13% -> 18%
where the time goes in v5:
time: 32 us; the launch traced here: 31.9 us
  waiting for transfers between devices  12.7 us (40%)
  starting transfers between devices  9.54 us (30%)
  Pallas kernels  8.85 us (28%)
  between operations  0.72 us (2%)
    pallas_call x5, Pallas kernels, run(): pl.pallas_call(kernel, out_shape=[jax.ShapeDtypeStruct(*out) for out in o...  8.85 us
    ppermute x2, waiting for transfers between devices, beside(): return lax.ppermute(x, ('ty', 'tx'), list(zip(ring, ring[1:] + ring[:1])))  6.4 us
    ppermute x2, starting transfers between devices, beside(): return lax.ppermute(x, ('ty', 'tx'), list(zip(ring, ring[1:] + ring[:1])))  4.43 us
    ppermute x3, waiting for transfers between devices, pairwise(): return lax.ppermute(x, ('ty', 'tx'), pairs)  4.24 us
    ppermute x3, starting transfers between devices, pairwise(): return lax.ppermute(x, ('ty', 'tx'), pairs)  4.19 us
    ppermute x7, waiting for transfers between devices, swap(): return lax.ppermute(x, 'ty', [(0, 1), (1, 0)])  2.05 us
    ppermute x7, starting transfers between devices, swap(): return lax.ppermute(x, 'ty', [(0, 1), (1, 0)])  0.92 us
  transfers between devices with their start and end apart: 12, of which 7 were waited for; matrix products, arithmetic and copies ran while one was open for 0% of the time, Pallas kernels for 18%

profile of v5, /device:TPU:0, one launch (start us, length us, event | category | flops | bytes accessed | tf_op | source)
XLA Modules:
  0.0 31.9 jit_solution(3688917141124326458)
XLA Ops:
  0.7 1.1 %shard_map.64 = (bf16[32,1280]{1,0:T(8,128)(2,1)S(1)}, s32[1,32]{1,0:T(1,128)S(1)}, bf16[32,32,128]{2,1,0:T(8,128)(2,1)S(1)}) custom-call(s32[1,1]{1,0:T(1,128)S(6)} %copy.11.counts, bf16[32,1024]{1,0:T(8,128)(2,1)} %bitcast.11, bf16[32,128]{1,0:T(8,128)(2,1)} %bitcast.12, s32[1,32]{1,0:T(1,128)} %bitcast.14, s32[2,32]{1,0:T(2,128)} %bitcast.13, ...), custom_call_target="tpu_custom_call" | custom-call | tf_op jit(solution)/shard_map/pallas_call | solution.py:518
  1.7 0.6 %collective-permute-start = (bf16[32,1280]{1,0:T(8,128)(2,1)S(1)}, bf16[32,1280]{1,0:T(8,128)(2,1)S(1)}, u32[]{:S(2)}, u32[]{:S(2)}) collective-permute-start(bf16[32,1280]{1,0:T(8,128)(2,1)S(1)} %get-tuple-element.19), channel_id=1, source_target_pairs={{0,16},{16,0},{1,17},{17,1},{2,18},{18,2},{3,19},{19,3},{4,20},{20... | collective-permute-start | bytes 245768 | tf_op jit(solution)/shard_map/ppermute | solution.py:144
  2.3 0.1 collective-permute-start.3
  2.4 0.8 %collective-permute-done = bf16[32,1280]{1,0:T(8,128)(2,1)S(1)} collective-permute-done((bf16[32,1280]{1,0:T(8,128)(2,1)S(1)}, bf16[32,1280]{1,0:T(8,128)(2,1)S(1)}, u32[]{:S(2)}, u32[]{:S(2)}) %collective-permute-start) | collective-permute-done | bytes 81952 | tf_op jit(solution)/shard_map/ppermute | solution.py:144
  3.2 2.9 %collective-permute-start.1 = (bf16[2,32,1280]{2,1,0:T(8,128)(2,1)S(1)}, bf16[2,32,1280]{2,1,0:T(8,128)(2,1)S(1)}, u32[]{:S(2)}, u32[]{:S(2)}) collective-permute-start(bf16[2,32,1280]{2,1,0:T(8,128)(2,1)S(1)} %pad_maximum_fusion.1.own), channel_id=1, source_target_pairs={{0,1},{1,2},{2,3},{3,4},{4,5},{5,6},{6,7},{7,8},{8,9},{9,10},{10,1... | collective-permute-start | bytes 491528 | tf_op jit(solution)/shard_map/ppermute | solution.py:150
  6.1 0.0 collective-permute-done.3.film_pair
  6.2 1.5 %collective-permute-start.4 = (bf16[64,16,128]{2,1,0:T(8,128)(2,1)S(1)}, bf16[64,16,128]{2,1,0:T(8,128)(2,1)S(1)}, u32[]{:S(2)}, u32[]{:S(2)}) collective-permute-start(bf16[64,16,128]{2,1,0:T(8,128)(2,1)S(1)} %pad_maximum_fusion), channel_id=1, source_target_pairs={{0,1},{1,2},{2,3},{3,4},{4,5},{5,6},{6,7},{7,8},{8,9},{9,10},{10,1... | collective-permute-start | bytes 786440 | tf_op jit(solution)/shard_map/ppermute | solution.py:150
  7.7 5.8 %collective-permute-done.1.direct = bf16[2,32,1280]{2,1,0:T(8,128)(2,1)S(1)} collective-permute-done((bf16[2,32,1280]{2,1,0:T(8,128)(2,1)S(1)}, bf16[2,32,1280]{2,1,0:T(8,128)(2,1)S(1)}, u32[]{:S(2)}, u32[]{:S(2)}) %collective-permute-start.1) | collective-permute-done | bytes 163872 | tf_op jit(solution)/shard_map/ppermute | solution.py:150
  13.6 0.0 collective-permute-start.2
  13.6 2.2 %shard_map.65 = (f32[9216,128]{1,0:T(8,128)S(1)}, f32[192,128]{1,0:T(8,128)S(1)}) custom-call(bf16[2,32,1280]{2,1,0:T(8,128)(2,1)S(1)} %pad_maximum_fusion.1.own), custom_call_target="tpu_custom_call" | custom-call | flops 1500000000 | tf_op jit(solution)/shard_map/pallas_call | solution.py:518
  15.8 0.6 %collective-permute-done.4.film_direct = bf16[64,16,128]{2,1,0:T(8,128)(2,1)S(1)} collective-permute-done((bf16[64,16,128]{2,1,0:T(8,128)(2,1)S(1)}, bf16[64,16,128]{2,1,0:T(8,128)(2,1)S(1)}, u32[]{:S(2)}, u32[]{:S(2)}) %collective-permute-start.4) | collective-permute-done | bytes 262176 | tf_op jit(solution)/shard_map/ppermute | solution.py:150
  16.3 0.0 collective-permute-start.5
  16.4 0.0 collective-permute-done.2.other
  16.4 3.7 %shard_map.66 = (f32[9216,128]{1,0:T(8,128)S(1)}, f32[192,128]{1,0:T(8,128)S(1)}, bf16[16,64,256]{2,1,0:T(8,128)(2,1)S(1)}, f32[64,128]{1,0:T(8,128)S(1)}, f32[6...) custom-call(f32[9216,128]{1,0:T(8,128)S(1)} %get-tuple-element.20.ca, ...), custom_call_target="tpu_custom_call", output_to_operand_aliasing={{0}: (0, {}), {1}: (1, {})} | custom-call | flops 3000000000 | tf_op jit(solution)/shard_map/pallas_call | solution.py:518
  20.1 0.0 collective-permute-done.5.film_other
  20.1 0.5 %shard_map.67 = (f32[80,128]{1,0:T(8,128)S(1)}, f32[80,128]{1,0:T(8,128)S(1)}, f32[64,128]{1,0:T(8,128)S(1)}) custom-call(bf16[16,64,256]{2,1,0:T(8,128)(2,1)S(1)} %get-tuple-element.22.mine, f32[64,128]{1,0:T(8,128)S(1)} %get-tuple-element.23.links, f32[64,128]{1,0:T(8,128)S(1)} %get-tuple-element.24.scale, f32[64,128]{1,0:T(8,128)S(1)} %get-tuple-element.25.begin, ...), custom_call_target="tpu_custom_call" | custom-call | tf_op jit(solution)/shard_map/pallas_call | solution.py:518
  20.6 2.5 %collective-permute-start.6 = (f32[80,128]{1,0:T(8,128)S(1)}, f32[80,128]{1,0:T(8,128)S(1)}, u32[]{:S(2)}, u32[]{:S(2)}) collective-permute-start(f32[80,128]{1,0:T(8,128)S(1)} %get-tuple-element.30), channel_id=1, source_target_pairs={{0,1},{1,0},{2,3},{3,2},{4,5},{5,4},{6,7},{7,6},{8,9},{9,8},{10,11... | collective-permute-start | bytes 122888 | tf_op jit(solution)/shard_map/ppermute | solution.py:165
  23.1 0.1 collective-permute-start.8
  23.2 2.1 %collective-permute-done.6.near_direct = f32[80,128]{1,0:T(8,128)S(1)} collective-permute-done((f32[80,128]{1,0:T(8,128)S(1)}, f32[80,128]{1,0:T(8,128)S(1)}, u32[]{:S(2)}, u32[]{:S(2)}) %collective-permute-start.6) | collective-permute-done | bytes 40992 | tf_op jit(solution)/shard_map/ppermute | solution.py:165
  25.3 1.6 %collective-permute-start.10 = (f32[80,128]{1,0:T(8,128)S(1)}, f32[80,128]{1,0:T(8,128)S(1)}, u32[]{:S(2)}, u32[]{:S(2)}) collective-permute-start(f32[80,128]{1,0:T(8,128)S(1)} %collective-permute-done.6.near_direct), channel_id=1, source_target_pairs={{0,4},{2,6},{4,8},{5,1},{6,10},{7,3},{8,12},{9,5},{10,14},{11,7},{... | collective-permute-start | bytes 122888 | tf_op jit(solution)/shard_map/ppermute | solution.py:165
  26.9 0.0 collective-permute-start.7
  26.9 0.3 collective-permute-done.8.across_direct
  27.1 0.3 collective-permute-start.9
  27.4 1.9 %collective-permute-done.10.relay_direct = f32[80,128]{1,0:T(8,128)S(1)} collective-permute-done((f32[80,128]{1,0:T(8,128)S(1)}, f32[80,128]{1,0:T(8,128)S(1)}, u32[]{:S(2)}, u32[]{:S(2)}) %collective-permute-start.10) | collective-permute-done | bytes 40992 | tf_op jit(solution)/shard_map/ppermute | solution.py:165
  29.3 0.0 collective-permute-start.11
  29.3 0.0 collective-permute-done.7.near_other
  29.3 0.0 collective-permute-done.9.across_other
  29.3 1.2 %collective-permute-done.11.relay_other = f32[80,128]{1,0:T(8,128)S(1)} collective-permute-done((f32[80,128]{1,0:T(8,128)S(1)}, f32[80,128]{1,0:T(8,128)S(1)}, u32[]{:S(2)}, u32[]{:S(2)}) %collective-permute-start.11) | collective-permute-done | bytes 40992 | tf_op jit(solution)/shard_map/ppermute | solution.py:144
  30.5 1.4 %shard_map.68 = f32[32,128]{1,0:T(8,128)} custom-call(f32[64,128]{1,0:T(8,128)S(1)} %get-tuple-element.28.level, f32[64,128]{1,0:T(8,128)S(1)} %get-tuple-element.25.begin, f32[64,128]{1,0:T(8,128)S(1)} %get-tuple-element.23.links, f32[64,128]{1,0:T(8,128)S(1)} %get-tuple-element.29.begin_near, f32[80,128]{1,0:T(8,128)S(1)} %collective-permute-done.6.near_direct, ...), custom_call_target="tpu_custom_call" | custom-call | tf_op jit(solution)/shard_map/pallas_call | solution.py:518
  (4 shorter events, 0.1 us)
Async XLA Ops:
  1.7 1.5 %collective-permute-start = (bf16[32,1280]{1,0:T(8,128)(2,1)S(1)}, bf16[32,1280]{1,0:T(8,128)(2,1)S(1)}, u32[]{:S(2)}, u32[]{:S(2)}) collective-permute-start(bf16[32,1280]{1,0:T(8,128)(2,1)S(1)} %get-tuple-element.19), channel_id=1, source_target_pairs={{0,16},{16,0},{1,17},{17,1},{2,18},{18,2},{3,19},{19,3},{4,20},{20... | collective-permute-start | bytes 245768 | tf_op jit(solution)/shard_map/ppermute | solution.py:144
  2.3 3.8 %collective-permute-start.3 = (bf16[32,32,128]{2,1,0:T(8,128)(2,1)S(1)}, bf16[32,32,128]{2,1,0:T(8,128)(2,1)S(1)}, u32[]{:S(2)}, u32[]{:S(2)}) collective-permute-start(bf16[32,32,128]{2,1,0:T(8,128)(2,1)S(1)} %get-tuple-element.27.film_own), channel_id=1, source_target_pairs={{0,16},{16,0},{1,17},{17,1},{2,18},{18,2},{3,19},{19,3},{4,20},{20... | collective-permute-start | bytes 786440 | tf_op jit(solution)/shard_map/ppermute | solution.py:144
  3.2 10.3 %collective-permute-start.1 = (bf16[2,32,1280]{2,1,0:T(8,128)(2,1)S(1)}, bf16[2,32,1280]{2,1,0:T(8,128)(2,1)S(1)}, u32[]{:S(2)}, u32[]{:S(2)}) collective-permute-start(bf16[2,32,1280]{2,1,0:T(8,128)(2,1)S(1)} %pad_maximum_fusion.1.own), channel_id=1, source_target_pairs={{0,1},{1,2},{2,3},{3,4},{4,5},{5,6},{6,7},{7,8},{8,9},{9,10},{10,1... | collective-permute-start | bytes 491528 | tf_op jit(solution)/shard_map/ppermute | solution.py:150
  6.2 10.2 %collective-permute-start.4 = (bf16[64,16,128]{2,1,0:T(8,128)(2,1)S(1)}, bf16[64,16,128]{2,1,0:T(8,128)(2,1)S(1)}, u32[]{:S(2)}, u32[]{:S(2)}) collective-permute-start(bf16[64,16,128]{2,1,0:T(8,128)(2,1)S(1)} %pad_maximum_fusion), channel_id=1, source_target_pairs={{0,1},{1,2},{2,3},{3,4},{4,5},{5,6},{6,7},{7,8},{8,9},{9,10},{10,1... | collective-permute-start | bytes 786440 | tf_op jit(solution)/shard_map/ppermute | solution.py:150
  13.6 2.8 %collective-permute-start.2 = (bf16[2,32,1280]{2,1,0:T(8,128)(2,1)S(1)}, bf16[2,32,1280]{2,1,0:T(8,128)(2,1)S(1)}, u32[]{:S(2)}, u32[]{:S(2)}) collective-permute-start(bf16[2,32,1280]{2,1,0:T(8,128)(2,1)S(1)} %collective-permute-done.1.direct), channel_id=1, source_target_pairs={{0,16},{16,0},{1,17},{17,1},{2,18},{18,2},{3,19},{19,3},{4,20},{20... | collective-permute-start | bytes 491528 | tf_op jit(solution)/shard_map/ppermute | solution.py:144
  16.3 3.7 %collective-permute-start.5 = (bf16[64,16,128]{2,1,0:T(8,128)(2,1)S(1)}, bf16[64,16,128]{2,1,0:T(8,128)(2,1)S(1)}, u32[]{:S(2)}, u32[]{:S(2)}) collective-permute-start(bf16[64,16,128]{2,1,0:T(8,128)(2,1)S(1)} %collective-permute-done.4.film_direct), channel_id=1, source_target_pairs={{0,16},{16,0},{1,17},{17,1},{2,18},{18,2},{3,19},{19,3},{4,20},{20... | collective-permute-start | bytes 786440 | tf_op jit(solution)/shard_map/ppermute | solution.py:144
  20.6 4.7 %collective-permute-start.6 = (f32[80,128]{1,0:T(8,128)S(1)}, f32[80,128]{1,0:T(8,128)S(1)}, u32[]{:S(2)}, u32[]{:S(2)}) collective-permute-start(f32[80,128]{1,0:T(8,128)S(1)} %get-tuple-element.30), channel_id=1, source_target_pairs={{0,1},{1,0},{2,3},{3,2},{4,5},{5,4},{6,7},{7,6},{8,9},{9,8},{10,11... | collective-permute-start | bytes 122888 | tf_op jit(solution)/shard_map/ppermute | solution.py:165
  23.1 4.0 %collective-permute-start.8 = (f32[80,128]{1,0:T(8,128)S(1)}, f32[80,128]{1,0:T(8,128)S(1)}, u32[]{:S(2)}, u32[]{:S(2)}) collective-permute-start(f32[80,128]{1,0:T(8,128)S(1)} %get-tuple-element.31), channel_id=1, source_target_pairs={{2,5},{3,4},{4,3},{5,2},{6,9},{7,8},{8,7},{9,6},{10,13},{11,12},{1... | collective-permute-start | bytes 122888 | tf_op jit(solution)/shard_map/ppermute | solution.py:165
  25.3 4.0 %collective-permute-start.10 = (f32[80,128]{1,0:T(8,128)S(1)}, f32[80,128]{1,0:T(8,128)S(1)}, u32[]{:S(2)}, u32[]{:S(2)}) collective-permute-start(f32[80,128]{1,0:T(8,128)S(1)} %collective-permute-done.6.near_direct), channel_id=1, source_target_pairs={{0,4},{2,6},{4,8},{5,1},{6,10},{7,3},{8,12},{9,5},{10,14},{11,7},{... | collective-permute-start | bytes 122888 | tf_op jit(solution)/shard_map/ppermute | solution.py:165
  26.9 2.4 %collective-permute-start.7 = (f32[80,128]{1,0:T(8,128)S(1)}, f32[80,128]{1,0:T(8,128)S(1)}, u32[]{:S(2)}, u32[]{:S(2)}) collective-permute-start(f32[80,128]{1,0:T(8,128)S(1)} %collective-permute-done.6.near_direct), channel_id=1, source_target_pairs={{0,16},{16,0},{1,17},{17,1},{2,18},{18,2},{3,19},{19,3},{4,20},{20... | collective-permute-start | bytes 122888 | tf_op jit(solution)/shard_map/ppermute | solution.py:144
  27.1 2.2 %collective-permute-start.9 = (f32[80,128]{1,0:T(8,128)S(1)}, f32[80,128]{1,0:T(8,128)S(1)}, u32[]{:S(2)}, u32[]{:S(2)}) collective-permute-start(f32[80,128]{1,0:T(8,128)S(1)} %collective-permute-done.8.across_direct), channel_id=1, source_target_pairs={{0,16},{16,0},{1,17},{17,1},{2,18},{18,2},{3,19},{19,3},{4,20},{20... | collective-permute-start | bytes 122888 | tf_op jit(solution)/shard_map/ppermute | solution.py:144
  29.3 1.2 %collective-permute-start.11 = (f32[80,128]{1,0:T(8,128)S(1)}, f32[80,128]{1,0:T(8,128)S(1)}, u32[]{:S(2)}, u32[]{:S(2)}) collective-permute-start(f32[80,128]{1,0:T(8,128)S(1)} %collective-permute-done.10.relay_direct), channel_id=1, source_target_pairs={{0,16},{16,0},{1,17},{17,1},{2,18},{18,2},{3,19},{19,3},{4,20},{20... | collective-permute-start | bytes 122888 | tf_op jit(solution)/shard_map/ppermute | solution.py:144

commit v6 on v5

--- a/solution.py
+++ b/solution.py
@@ -132,8 +132,7 @@
 
 EDGES = ((1, -1, 1, -1), (2, 2, -2, -2))
 ACROSS = ((-1, -3, 3, 1), (3, 1, -1, -3))
-PLANES = ((4, -4, 4, -4), (4, 4, -4, -4))
-RELAYED = ((-3, 3, -3, 3), (-2, -2, 2, 2))
+CROSS = ((-2, -2, 2, 2), (-3, 3, -3, 3))
 
 
 def take_lanes(values, lanes):
@@ -144,9 +143,10 @@
     return lax.ppermute(x, "ty", [(0, 1), (1, 0)])
 
 
-def beside(x):
+def beside(x, turn=1):
     count = lax.axis_size("tx")
     ring = list(range(count)) + list(range(2 * count - 1, count - 1, -1))
+    ring = ring[::turn]
     return lax.ppermute(x, ("ty", "tx"), list(zip(ring, ring[1:] + ring[:1])))
 
 
@@ -213,7 +213,7 @@
 def paint_tiles(
     sources, rows, columns, canvas, start, patches, numbers, table, sem, prepare=None
 ):
-    slots = sources[0][0].shape[1]
+    slots = sources[0].shape[0]
     total = start.shape[0]
     block = slots // BLOCKS
     group = 2 * block
@@ -221,7 +221,7 @@
     pixels = PATCH * PATCH // LANES
     width = pixels * LANES
 
-    heads = [ref[u, 0:16, width + LANES:].astype(jnp.float32) for ref, u in sources]
+    heads = [ref[0:16, width + LANES:].astype(jnp.float32) for ref in sources]
     spare = [jnp.zeros((8 - len(sources), LANES), jnp.float32)]
     ordering, top, left, count = (
         jnp.concatenate([head[i:i + 1, :] for head in heads] + spare, axis=0).astype(jnp.int32)
@@ -256,16 +256,16 @@
 
     if prepare is not None:
         prepare()
-    for t, (ref, u) in enumerate(sources):
+    for t, ref in enumerate(sources):
         for k in range(pixels):
             patches[pl.ds(t * slots * pixels + k, slots, stride=pixels), :] = ref[
-                u, :, k * LANES:(k + 1) * LANES
+                :, k * LANES:(k + 1) * LANES
             ].astype(jnp.float32)
         which = lax.broadcasted_iota(jnp.int32, (slots, slots), 0)
         chosen = (which == ordering[t:t + 1, :slots]) & (which < count[t:t + 1, 0:1])
         trail = lax.dot_general(
             chosen.astype(jnp.bfloat16),
-            ref[u, :, width:width + LANES],
+            ref[:, width:width + LANES],
             (((0,), (0,)), ((), ())),
             preferred_element_type=jnp.float32,
         )
@@ -299,35 +299,34 @@
             canvas[pl.ds(at + 2 * pixels * total, 1), :] = last[0:1, :]
 
 
-def own_kernel(own, canvas, start, patches, numbers, table, sem):
+def own_kernel(own, pair, canvas, start, patches, numbers, table, sem):
     core = lax.axis_index("ty")
 
     def clear():
         canvas[...] = jnp.zeros_like(canvas)
 
     paint_tiles(
-        ((own, 0), (own, 1)), (core, 1 - core), (0, 0),
+        (own, pair), (core, 1 - core), (0, 0),
         canvas, start, patches, numbers, table, sem, clear,
     )
 
 
 def near_kernel(
-    canvas_own, start_own, direct, other,
+    canvas_own, start_own, first, second, first_other, second_other,
     canvas, start, mine, links, scale, begin, coupling, begin_near,
     patches, numbers, table, sem,
 ):
-    slots = direct.shape[1]
+    slots = first.shape[0]
     total = start.shape[0]
     group = 2 * slots // BLOCKS
     source = 3 * group
     depth = canvas.shape[0] // total
     core = lax.axis_index("ty")
-    step_direct = 2 * core - 1
-    step_other = -step_direct
+    step = 2 * core - 1
     paint_tiles(
-        ((direct, 0), (direct, 1), (other, 0), (other, 1)),
-        (core, 1 - core, 1 - core, core),
-        (step_direct, step_direct, step_other, step_other),
+        (first, second, first_other, second_other),
+        (core, core, 1 - core, 1 - core),
+        (step, -step, -step, step),
         canvas, start, patches, numbers, table, sem,
     )
 
@@ -371,7 +370,7 @@
 
 def drive_kernel(
     mine, links, scale, begin, coupling, film_own, film_pair, film_direct, film_other,
-    near, across, level, film,
+    near, across, cross, level, film,
 ):
     core = lax.axis_index("ty")
     side_direct = 2 * core - 1
@@ -410,24 +409,28 @@
 
     change = jnp.maximum(rows_of(level, 0), 0.0) - rows_of(begin, 0)
     varied = jnp.where(core == 0, rows_of(level, 2), rows_of(begin, 1))
-    for ref, fourth in ((near, varied), (across, rows_of(level, 2))):
-        pieces = (change, rows_of(level, 1), rows_of(links, 0), fourth, rows_of(links, 1))
-        for i, piece in enumerate(pieces):
+    common = (change, rows_of(level, 1), rows_of(links, 0))
+    for ref, rest in (
+        (near, (varied, rows_of(links, 1))),
+        (across, (rows_of(level, 2), rows_of(links, 1))),
+        (cross, (rows_of(begin, 1),)),
+    ):
+        for i, piece in enumerate(common + rest):
             ref[i * group:(i + 1) * group, :] = piece
 
 
 def sweep_kernel(
     level, begin, links, begin_near, near_direct, near_other, across_direct, across_other,
-    relay_direct, relay_other, order, out, box, current,
+    cross_direct, cross_other, order, out, box, current,
 ):
     slots = out.shape[0]
     block = slots // BLOCKS
     group = 2 * block
     reach = BLOCKS - 1
-    refs = (near_direct, near_other, across_direct, across_other, relay_direct, relay_other)
-    steps = (*partner(EDGES), *partner(ACROSS), *partner(RELAYED))
+    refs = (near_direct, near_other, across_direct, across_other, cross_direct, cross_other)
+    steps = (*partner(EDGES), *partner(ACROSS), *partner(CROSS))
     for ref, step in zip(refs, steps):
-        box[reach + step] = jnp.where(exists(step), ref[...], 0.0)
+        box[reach + step, 0:ref.shape[0], :] = jnp.where(exists(step), ref[...], 0.0)
 
     def halves(x):
         high = x.astype(jnp.bfloat16)
@@ -556,15 +559,17 @@
         4,
         [pltpu.SMEM] + [pltpu.HBM] * len(given),
     )(counts, *(pltpu.with_memory_space_constraint(x, pltpu.HBM) for x in given))
-    own = jnp.stack([packed, swap(packed)])
-    pair_film = swap(film)
-    direct = beside(own)
+    pair_film = swap(movie)
+    first = beside(packed)
+    second = beside(packed, -1)
+    pair = swap(packed)
     edge = jnp.where(lax.axis_index("ty") == 0, half, 0)
     edges = jnp.concatenate(
         [lax.dynamic_slice_in_dim(x, edge, half, axis=1) for x in (film, pair_film)], axis=0
     )
     film_direct = beside(edges)
-    other = swap(direct)
+    first_other = swap(first)
+    second_other = swap(second)
     film_other = swap(film_direct)
 
     canvas = ((2 * height + PATCH) // 2 * total, LANES)
@@ -583,7 +588,7 @@
         painting(2),
         4,
         cost=pl.CostEstimate(flops=1_500_000_000, bytes_accessed=0, transcendentals=0),
-    )(own)
+    )(packed, pair)
     *_, mine, links, scale, begin, coupling, begin_near = call(
         near_kernel,
         [
@@ -600,20 +605,20 @@
         8,
         cost=pl.CostEstimate(flops=3_000_000_000, bytes_accessed=0, transcendentals=0),
         aliases={0: 0, 1: 1},
-    )(own_canvas, own_start, direct, other)
-    near, across, level = call(
+    )(own_canvas, own_start, first, second, first_other, second_other)
+    near, across, cross, level = call(
         drive_kernel,
-        [((5 * group, frames), f32), ((5 * group, frames), f32), ((4 * group, frames), f32)],
+        [((rows * group, frames), f32) for rows in (5, 5, 4, 4)],
         [pltpu.VMEM((2 * height, 2 * PATCH, frames), bf16)],
         8,
     )(mine, links, scale, begin, coupling, film, pair_film, film_direct, film_other)
 
+    across_direct = pairwise(across, ACROSS)
+    cross_direct = pairwise(cross, CROSS)
     near_direct = pairwise(near, EDGES)
-    across_direct = pairwise(across, ACROSS)
-    relay_direct = pairwise(near_direct, PLANES)
+    across_other = swap(across_direct)
+    cross_other = swap(cross_direct)
     near_other = swap(near_direct)
-    across_other = swap(across_direct)
-    relay_other = swap(relay_direct)
     (result,) = call(
         sweep_kernel,
         [((slots, frames), f32)],
@@ -624,7 +629,7 @@
         4,
     )(
         level, begin, links, begin_near, near_direct, near_other, across_direct, across_other,
-        relay_direct, relay_other, ordering,
+        cross_direct, cross_other, ordering,
     )
     return result[None, None]
 

time: 32 us -> 33 us (1.031)
  the two profiles are of different devices: /device:TPU:0 before, /device:TPU:7 now
where the time goes in v6:
time: 33 us; the launch traced here: 32.8 us
  starting transfers between devices  17.3 us (52%)
  Pallas kernels  8.86 us (27%)
  waiting for transfers between devices  5.91 us (18%)
  between operations  0.75 us (2%)
    ppermute x8, starting transfers between devices, swap(): return lax.ppermute(x, 'ty', [(0, 1), (1, 0)])  9.46 us
    pallas_call x5, Pallas kernels, run(): pl.pallas_call(kernel, out_shape=[jax.ShapeDtypeStruct(*out) for out in o...  8.86 us
    ppermute x3, waiting for transfers between devices, beside(): return lax.ppermute(x, ('ty', 'tx'), list(zip(ring, ring[1:] + ring[:1])))  5.03 us
    ppermute x3, starting transfers between devices, pairwise(): return lax.ppermute(x, ('ty', 'tx'), pairs)  4.23 us
    ppermute x3, starting transfers between devices, beside(): return lax.ppermute(x, ('ty', 'tx'), list(zip(ring, ring[1:] + ring[:1])))  3.57 us
    ppermute x8, waiting for transfers between devices, swap(): return lax.ppermute(x, 'ty', [(0, 1), (1, 0)])  0.88 us
  transfers between devices with their start and end apart: 14, of which 2 were waited for; matrix products, arithmetic and copies ran while one was open for 0% of the time, Pallas kernels for 21%

profile of v6, /device:TPU:7, one launch (start us, length us, event | category | flops | bytes accessed | tf_op | source)
XLA Modules:
  0.0 32.8 jit_solution(15208377085930010061)
XLA Ops:
  0.0 0.7 %collective-permute-start.5 = (bf16[32,32,128]{2,1,0:T(8,128)(2,1)}, bf16[32,32,128]{2,1,0:T(8,128)(2,1)S(1)}, u32[]{:S(2)}, u32[]{:S(2)}) collective-permute-start(bf16[32,32,128]{2,1,0:T(8,128)(2,1)} %movie.1), channel_id=1, source_target_pairs={{0,16},{16,0},{1,17},{17,1},{2,18},{18,2},{3,19},{19,3},{4,20},{20... | collective-permute-start | bytes 786440 | tf_op jit(solution)/shard_map/ppermute | solution.py:143
  1.3 1.1 %shard_map.64 = (bf16[32,1280]{1,0:T(8,128)(2,1)S(1)}, s32[1,32]{1,0:T(1,128)S(1)}, bf16[32,32,128]{2,1,0:T(8,128)(2,1)S(1)}) custom-call(s32[1,1]{1,0:T(1,128)S(6)} %copy.11.counts, bf16[32,1024]{1,0:T(8,128)(2,1)} %bitcast.7, bf16[32,128]{1,0:T(8,128)(2,1)} %bitcast.8, s32[1,32]{1,0:T(1,128)} %bitcast.10, s32[2,32]{1,0:T(2,128)} %bitcast.9, ...), custom_call_target="tpu_custom_call" | custom-call | tf_op jit(solution)/shard_map/pallas_call | solution.py:521
  2.4 0.0 collective-permute-done.5.film_pair
  2.5 0.3 collective-permute-start.6
  2.8 1.2 %collective-permute-start.1 = (bf16[32,1280]{1,0:T(8,128)(2,1)S(1)}, bf16[32,1280]{1,0:T(8,128)(2,1)S(1)}, u32[]{:S(2)}, u32[]{:S(2)}) collective-permute-start(bf16[32,1280]{1,0:T(8,128)(2,1)S(1)} %get-tuple-element.20.own), channel_id=1, source_target_pairs={{0,1},{1,2},{2,3},{3,4},{4,5},{5,6},{6,7},{7,8},{8,9},{9,10},{10,1... | collective-permute-start | bytes 245768 | tf_op jit(solution)/shard_map/ppermute | solution.py:150
  4.0 2.1 %collective-permute-start.2 = (bf16[32,1280]{1,0:T(8,128)(2,1)S(1)}, bf16[32,1280]{1,0:T(8,128)(2,1)S(1)}, u32[]{:S(2)}, u32[]{:S(2)}) collective-permute-start(bf16[32,1280]{1,0:T(8,128)(2,1)S(1)} %get-tuple-element.20.own), channel_id=1, source_target_pairs={{16,17},{17,18},{18,19},{19,20},{20,21},{21,22},{22,23},{23,24},{2... | collective-permute-start | bytes 245768 | tf_op jit(solution)/shard_map/ppermute | solution.py:150
  6.1 0.0 collective-permute-start
  6.1 5.0 %collective-permute-done.1.first = bf16[32,1280]{1,0:T(8,128)(2,1)S(1)} collective-permute-done((bf16[32,1280]{1,0:T(8,128)(2,1)S(1)}, bf16[32,1280]{1,0:T(8,128)(2,1)S(1)}, u32[]{:S(2)}, u32[]{:S(2)}) %collective-permute-start.1) | collective-permute-done | bytes 81952 | tf_op jit(solution)/shard_map/ppermute | solution.py:150
  11.1 2.4 %collective-permute-start.3 = (bf16[32,1280]{1,0:T(8,128)(2,1)S(1)}, bf16[32,1280]{1,0:T(8,128)(2,1)S(1)}, u32[]{:S(2)}, u32[]{:S(2)}) collective-permute-start(bf16[32,1280]{1,0:T(8,128)(2,1)S(1)} %collective-permute-done.1.first), channel_id=1, source_target_pairs={{0,16},{16,0},{1,17},{17,1},{2,18},{18,2},{3,19},{19,3},{4,20},{20... | collective-permute-start | bytes 245768 | tf_op jit(solution)/shard_map/ppermute | solution.py:143
  13.5 0.0 collective-permute-done.2.second
  13.5 0.0 collective-permute-start.4
  13.5 0.0 collective-permute-done.pair
  13.5 2.2 %shard_map.65 = (f32[9216,128]{1,0:T(8,128)S(1)}, f32[192,128]{1,0:T(8,128)S(1)}) custom-call(bf16[32,1280]{1,0:T(8,128)(2,1)S(1)} %get-tuple-element.20.own, bf16[32,1280]{1,0:T(8,128)(2,1)S(1)} %collective-permute-done.pair), custom_call_target="tpu_custom_call" | custom-call | flops 1500000000 | tf_op jit(solution)/shard_map/pallas_call | solution.py:521
  15.8 0.0 collective-permute-done.6.film_direct
  15.8 0.6 %collective-permute-start.7 = (bf16[64,16,128]{2,1,0:T(8,128)(2,1)S(1)}, bf16[64,16,128]{2,1,0:T(8,128)(2,1)S(1)}, u32[]{:S(2)}, u32[]{:S(2)}) collective-permute-start(bf16[64,16,128]{2,1,0:T(8,128)(2,1)S(1)} %collective-permute-done.6.film_direct), channel_id=1, source_target_pairs={{0,16},{16,0},{1,17},{17,1},{2,18},{18,2},{3,19},{19,3},{4,20},{20... | collective-permute-start | bytes 786440 | tf_op jit(solution)/shard_map/ppermute | solution.py:143
  16.3 0.0 collective-permute-done.3.first_other
  16.3 0.0 collective-permute-done.4.second_other
  16.3 3.7 %shard_map.66 = (f32[9216,128]{1,0:T(8,128)S(1)}, f32[192,128]{1,0:T(8,128)S(1)}, bf16[16,64,256]{2,1,0:T(8,128)(2,1)S(1)}, f32[64,128]{1,0:T(8,128)S(1)}, f32[6...) custom-call(f32[9216,128]{1,0:T(8,128)S(1)} %get-tuple-element.21.ca, ...), custom_call_target="tpu_custom_call", output_to_operand_aliasing={{0}: (0, {}), {1}: (1, {})} | custom-call | flops 3000000000 | tf_op jit(solution)/shard_map/pallas_call | solution.py:521
  20.1 0.0 collective-permute-done.7.film_other
  20.1 0.5 %shard_map.67 = (f32[80,128]{1,0:T(8,128)S(1)}, f32[80,128]{1,0:T(8,128)S(1)}, f32[64,128]{1,0:T(8,128)S(1)}, f32[64,128]{1,0:T(8,128)S(1)}) custom-call(bf16[16,64,256]{2,1,0:T(8,128)(2,1)S(1)} %get-tuple-element.23.mine, f32[64,128]{1,0:T(8,128)S(1)} %get-tuple-element.24.links, f32[64,128]{1,0:T(8,128)S(1)} %get-tuple-element.25.scale, ...), custom_call_target="tpu_custom_call" | custom-call | tf_op jit(solution)/shard_map/pallas_call | solution.py:521
  20.6 0.8 %collective-permute-start.10 = (f32[80,128]{1,0:T(8,128)S(1)}, f32[80,128]{1,0:T(8,128)S(1)}, u32[]{:S(2)}, u32[]{:S(2)}) collective-permute-start(f32[80,128]{1,0:T(8,128)S(1)} %get-tuple-element.32), channel_id=1, source_target_pairs={{2,5},{3,4},{4,3},{5,2},{6,9},{7,8},{8,7},{9,6},{10,13},{11,12},{1... | collective-permute-start | bytes 122888 | tf_op jit(solution)/shard_map/ppermute | solution.py:165
  21.4 1.2 %collective-permute-start.8 = (f32[80,128]{1,0:T(8,128)S(1)}, f32[80,128]{1,0:T(8,128)S(1)}, u32[]{:S(2)}, u32[]{:S(2)}) collective-permute-start(f32[80,128]{1,0:T(8,128)S(1)} %get-tuple-element.31), channel_id=1, source_target_pairs={{0,1},{1,0},{2,3},{3,2},{4,5},{5,4},{6,7},{7,6},{8,9},{9,8},{10,11... | collective-permute-start | bytes 122888 | tf_op jit(solution)/shard_map/ppermute | solution.py:165
  22.6 2.2 %collective-permute-start.12 = (f32[64,128]{1,0:T(8,128)S(1)}, f32[64,128]{1,0:T(8,128)S(1)}, u32[]{:S(2)}, u32[]{:S(2)}) collective-permute-start(f32[64,128]{1,0:T(8,128)S(1)} %get-tuple-element.33), channel_id=1, source_target_pairs={{2,4},{3,5},{4,2},{5,3},{6,8},{7,9},{8,6},{9,7},{10,12},{11,13},{1... | collective-permute-start | bytes 98312 | tf_op jit(solution)/shard_map/ppermute | solution.py:165
  24.8 0.0 collective-permute-done.10.across_direct
  24.8 1.7 %collective-permute-start.11 = (f32[80,128]{1,0:T(8,128)S(1)}, f32[80,128]{1,0:T(8,128)S(1)}, u32[]{:S(2)}, u32[]{:S(2)}) collective-permute-start(f32[80,128]{1,0:T(8,128)S(1)} %collective-permute-done.10.across_direct), channel_id=1, source_target_pairs={{0,16},{16,0},{1,17},{17,1},{2,18},{18,2},{3,19},{19,3},{4,20},{20... | collective-permute-start | bytes 122888 | tf_op jit(solution)/shard_map/ppermute | solution.py:143
  26.5 0.0 collective-permute-done.8.near_direct
  26.5 1.3 %collective-permute-start.9 = (f32[80,128]{1,0:T(8,128)S(1)}, f32[80,128]{1,0:T(8,128)S(1)}, u32[]{:S(2)}, u32[]{:S(2)}) collective-permute-start(f32[80,128]{1,0:T(8,128)S(1)} %collective-permute-done.8.near_direct), channel_id=1, source_target_pairs={{0,16},{16,0},{1,17},{17,1},{2,18},{18,2},{3,19},{19,3},{4,20},{20... | collective-permute-start | bytes 122888 | tf_op jit(solution)/shard_map/ppermute | solution.py:143
  27.8 0.0 collective-permute-done.12.cross_direct
  27.8 2.8 %collective-permute-start.13 = (f32[64,128]{1,0:T(8,128)S(1)}, f32[64,128]{1,0:T(8,128)S(1)}, u32[]{:S(2)}, u32[]{:S(2)}) collective-permute-start(f32[64,128]{1,0:T(8,128)S(1)} %collective-permute-done.12.cross_direct), channel_id=1, source_target_pairs={{0,16},{16,0},{1,17},{17,1},{2,18},{18,2},{3,19},{19,3},{4,20},{20... | collective-permute-start | bytes 98312 | tf_op jit(solution)/shard_map/ppermute | solution.py:143
  30.6 0.9 %collective-permute-done.13.cross_other = f32[64,128]{1,0:T(8,128)S(1)} collective-permute-done((f32[64,128]{1,0:T(8,128)S(1)}, f32[64,128]{1,0:T(8,128)S(1)}, u32[]{:S(2)}, u32[]{:S(2)}) %collective-permute-start.13) | collective-permute-done | bytes 32800 | tf_op jit(solution)/shard_map/ppermute | solution.py:143
  31.5 0.0 collective-permute-done.11.across_other
  31.5 0.0 collective-permute-done.9.near_other
  31.5 1.4 %shard_map.68 = f32[32,128]{1,0:T(8,128)} custom-call(f32[64,128]{1,0:T(8,128)S(1)} %get-tuple-element.29.level, f32[64,128]{1,0:T(8,128)S(1)} %get-tuple-element.26.begin, f32[64,128]{1,0:T(8,128)S(1)} %get-tuple-element.24.links, f32[64,128]{1,0:T(8,128)S(1)} %get-tuple-element.30.begin_near, f32[80,128]{1,0:T(8,128)S(1)} %collective-permute-done.8.near_direct, ...), custom_call_target="tpu_custom_call" | custom-call | tf_op jit(solution)/shard_map/pallas_call | solution.py:521
  (3 shorter events, 0.1 us)
Async XLA Ops:
  0.0 2.5 %collective-permute-start.5 = (bf16[32,32,128]{2,1,0:T(8,128)(2,1)}, bf16[32,32,128]{2,1,0:T(8,128)(2,1)S(1)}, u32[]{:S(2)}, u32[]{:S(2)}) collective-permute-start(bf16[32,32,128]{2,1,0:T(8,128)(2,1)} %movie.1), channel_id=1, source_target_pairs={{0,16},{16,0},{1,17},{17,1},{2,18},{18,2},{3,19},{19,3},{4,20},{20... | collective-permute-start | bytes 786440 | tf_op jit(solution)/shard_map/ppermute | solution.py:143
  2.5 13.2 %collective-permute-start.6 = (bf16[64,16,128]{2,1,0:T(8,128)(2,1)S(1)}, bf16[64,16,128]{2,1,0:T(8,128)(2,1)S(1)}, u32[]{:S(2)}, u32[]{:S(2)}) collective-permute-start(bf16[64,16,128]{2,1,0:T(8,128)(2,1)S(1)} %pad_maximum_fusion), channel_id=1, source_target_pairs={{0,1},{1,2},{2,3},{3,4},{4,5},{5,6},{6,7},{7,8},{8,9},{9,10},{10,1... | collective-permute-start | bytes 786440 | tf_op jit(solution)/shard_map/ppermute | solution.py:150
  2.8 8.3 %collective-permute-start.1 = (bf16[32,1280]{1,0:T(8,128)(2,1)S(1)}, bf16[32,1280]{1,0:T(8,128)(2,1)S(1)}, u32[]{:S(2)}, u32[]{:S(2)}) collective-permute-start(bf16[32,1280]{1,0:T(8,128)(2,1)S(1)} %get-tuple-element.20.own), channel_id=1, source_target_pairs={{0,1},{1,2},{2,3},{3,4},{4,5},{5,6},{6,7},{7,8},{8,9},{9,10},{10,1... | collective-permute-start | bytes 245768 | tf_op jit(solution)/shard_map/ppermute | solution.py:150
  4.0 9.6 %collective-permute-start.2 = (bf16[32,1280]{1,0:T(8,128)(2,1)S(1)}, bf16[32,1280]{1,0:T(8,128)(2,1)S(1)}, u32[]{:S(2)}, u32[]{:S(2)}) collective-permute-start(bf16[32,1280]{1,0:T(8,128)(2,1)S(1)} %get-tuple-element.20.own), channel_id=1, source_target_pairs={{16,17},{17,18},{18,19},{19,20},{20,21},{21,22},{22,23},{23,24},{2... | collective-permute-start | bytes 245768 | tf_op jit(solution)/shard_map/ppermute | solution.py:150
  6.1 7.5 %collective-permute-start = (bf16[32,1280]{1,0:T(8,128)(2,1)S(1)}, bf16[32,1280]{1,0:T(8,128)(2,1)S(1)}, u32[]{:S(2)}, u32[]{:S(2)}) collective-permute-start(bf16[32,1280]{1,0:T(8,128)(2,1)S(1)} %get-tuple-element.20.own), channel_id=1, source_target_pairs={{0,16},{16,0},{1,17},{17,1},{2,18},{18,2},{3,19},{19,3},{4,20},{20... | collective-permute-start | bytes 245768 | tf_op jit(solution)/shard_map/ppermute | solution.py:143
  11.1 5.2 %collective-permute-start.3 = (bf16[32,1280]{1,0:T(8,128)(2,1)S(1)}, bf16[32,1280]{1,0:T(8,128)(2,1)S(1)}, u32[]{:S(2)}, u32[]{:S(2)}) collective-permute-start(bf16[32,1280]{1,0:T(8,128)(2,1)S(1)} %collective-permute-done.1.first), channel_id=1, source_target_pairs={{0,16},{16,0},{1,17},{17,1},{2,18},{18,2},{3,19},{19,3},{4,20},{20... | collective-permute-start | bytes 245768 | tf_op jit(solution)/shard_map/ppermute | solution.py:143
  13.5 2.8 %collective-permute-start.4 = (bf16[32,1280]{1,0:T(8,128)(2,1)S(1)}, bf16[32,1280]{1,0:T(8,128)(2,1)S(1)}, u32[]{:S(2)}, u32[]{:S(2)}) collective-permute-start(bf16[32,1280]{1,0:T(8,128)(2,1)S(1)} %collective-permute-done.2.second), channel_id=1, source_target_pairs={{0,16},{16,0},{1,17},{17,1},{2,18},{18,2},{3,19},{19,3},{4,20},{20... | collective-permute-start | bytes 245768 | tf_op jit(solution)/shard_map/ppermute | solution.py:143
  15.8 4.3 %collective-permute-start.7 = (bf16[64,16,128]{2,1,0:T(8,128)(2,1)S(1)}, bf16[64,16,128]{2,1,0:T(8,128)(2,1)S(1)}, u32[]{:S(2)}, u32[]{:S(2)}) collective-permute-start(bf16[64,16,128]{2,1,0:T(8,128)(2,1)S(1)} %collective-permute-done.6.film_direct), channel_id=1, source_target_pairs={{0,16},{16,0},{1,17},{17,1},{2,18},{18,2},{3,19},{19,3},{4,20},{20... | collective-permute-start | bytes 786440 | tf_op jit(solution)/shard_map/ppermute | solution.py:143
  20.6 4.2 %collective-permute-start.10 = (f32[80,128]{1,0:T(8,128)S(1)}, f32[80,128]{1,0:T(8,128)S(1)}, u32[]{:S(2)}, u32[]{:S(2)}) collective-permute-start(f32[80,128]{1,0:T(8,128)S(1)} %get-tuple-element.32), channel_id=1, source_target_pairs={{2,5},{3,4},{4,3},{5,2},{6,9},{7,8},{8,7},{9,6},{10,13},{11,12},{1... | collective-permute-start | bytes 122888 | tf_op jit(solution)/shard_map/ppermute | solution.py:165
  21.4 5.1 %collective-permute-start.8 = (f32[80,128]{1,0:T(8,128)S(1)}, f32[80,128]{1,0:T(8,128)S(1)}, u32[]{:S(2)}, u32[]{:S(2)}) collective-permute-start(f32[80,128]{1,0:T(8,128)S(1)} %get-tuple-element.31), channel_id=1, source_target_pairs={{0,1},{1,0},{2,3},{3,2},{4,5},{5,4},{6,7},{7,6},{8,9},{9,8},{10,11... | collective-permute-start | bytes 122888 | tf_op jit(solution)/shard_map/ppermute | solution.py:165
  22.6 5.1 %collective-permute-start.12 = (f32[64,128]{1,0:T(8,128)S(1)}, f32[64,128]{1,0:T(8,128)S(1)}, u32[]{:S(2)}, u32[]{:S(2)}) collective-permute-start(f32[64,128]{1,0:T(8,128)S(1)} %get-tuple-element.33), channel_id=1, source_target_pairs={{2,4},{3,5},{4,2},{5,3},{6,8},{7,9},{8,6},{9,7},{10,12},{11,13},{1... | collective-permute-start | bytes 98312 | tf_op jit(solution)/shard_map/ppermute | solution.py:165
  24.8 6.7 %collective-permute-start.11 = (f32[80,128]{1,0:T(8,128)S(1)}, f32[80,128]{1,0:T(8,128)S(1)}, u32[]{:S(2)}, u32[]{:S(2)}) collective-permute-start(f32[80,128]{1,0:T(8,128)S(1)} %collective-permute-done.10.across_direct), channel_id=1, source_target_pairs={{0,16},{16,0},{1,17},{17,1},{2,18},{18,2},{3,19},{19,3},{4,20},{20... | collective-permute-start | bytes 122888 | tf_op jit(solution)/shard_map/ppermute | solution.py:143
  26.5 5.0 %collective-permute-start.9 = (f32[80,128]{1,0:T(8,128)S(1)}, f32[80,128]{1,0:T(8,128)S(1)}, u32[]{:S(2)}, u32[]{:S(2)}) collective-permute-start(f32[80,128]{1,0:T(8,128)S(1)} %collective-permute-done.8.near_direct), channel_id=1, source_target_pairs={{0,16},{16,0},{1,17},{17,1},{2,18},{18,2},{3,19},{19,3},{4,20},{20... | collective-permute-start | bytes 122888 | tf_op jit(solution)/shard_map/ppermute | solution.py:143
  27.8 3.7 %collective-permute-start.13 = (f32[64,128]{1,0:T(8,128)S(1)}, f32[64,128]{1,0:T(8,128)S(1)}, u32[]{:S(2)}, u32[]{:S(2)}) collective-permute-start(f32[64,128]{1,0:T(8,128)S(1)} %collective-permute-done.12.cross_direct), channel_id=1, source_target_pairs={{0,16},{16,0},{1,17},{17,1},{2,18},{18,2},{3,19},{19,3},{4,20},{20... | collective-permute-start | bytes 98312 | tf_op jit(solution)/shard_map/ppermute | solution.py:143

commit v7 on v6

--- a/solution.py
+++ b/solution.py
@@ -139,6 +139,14 @@
     return jnp.take_along_axis(values, lanes, axis=1, mode="promise_in_bounds")
 
 
+def thirds(x):
+    parts = []
+    for _ in range(3):
+        parts.append(x.astype(jnp.bfloat16))
+        x = x - parts[-1].astype(jnp.float32)
+    return parts
+
+
 def swap(x):
     return lax.ppermute(x, "ty", [(0, 1), (1, 0)])
 
@@ -313,14 +321,8 @@
 
 def near_kernel(
     canvas_own, start_own, first, second, first_other, second_other,
-    canvas, start, mine, links, scale, begin, coupling, begin_near,
-    patches, numbers, table, sem,
+    canvas, start, patches, numbers, table, sem,
 ):
-    slots = first.shape[0]
-    total = start.shape[0]
-    group = 2 * slots // BLOCKS
-    source = 3 * group
-    depth = canvas.shape[0] // total
     core = lax.axis_index("ty")
     step = 2 * core - 1
     paint_tiles(
@@ -330,6 +332,13 @@
         canvas, start, patches, numbers, table, sem,
     )
 
+
+def margins_kernel(canvas, start, mine, links, scale, begin, coupling, begin_near):
+    total = start.shape[0]
+    slots = total // 6
+    group = 2 * slots // BLOCKS
+    source = 3 * group
+    depth = canvas.shape[0] // total
     margins = jnp.zeros((2 * slots, total), jnp.float32)
     edge = PATCH // 8
     for step in range(depth // 2):
@@ -346,8 +355,9 @@
         if edge <= step < depth // 2 - edge:
             mine[step - edge] = targets
 
-    coupling[...] = jnp.dot(
-        margins, start[...], precision=precise, preferred_element_type=jnp.float32
+    begins = start[...].astype(jnp.bfloat16)
+    coupling[...] = sum(
+        jnp.dot(x, begins, preferred_element_type=jnp.float32) for x in thirds(margins)
     )
     line = lax.broadcasted_iota(jnp.int32, margins.shape, 0)
     column = lax.broadcasted_iota(jnp.int32, margins.shape, 1)
@@ -511,8 +521,9 @@
         [current[pl.ds(q * group + row, block), :] for q in range(BLOCKS)], axis=0
     )
     place = lax.broadcasted_iota(jnp.int32, (slots, slots), 0) == order[...]
-    out[...] = jnp.dot(
-        place.astype(jnp.float32), ordered, precision=precise, preferred_element_type=jnp.float32
+    place = place.astype(jnp.bfloat16)
+    out[...] = sum(
+        jnp.dot(place, x, preferred_element_type=jnp.float32) for x in thirds(ordered)
     )
 
 
@@ -589,11 +600,17 @@
         4,
         cost=pl.CostEstimate(flops=1_500_000_000, bytes_accessed=0, transcendentals=0),
     )(packed, pair)
-    *_, mine, links, scale, begin, coupling, begin_near = call(
+    painted, start = call(
         near_kernel,
+        [(canvas, f32), ((total, frames), f32)],
+        painting(4),
+        4,
+        cost=pl.CostEstimate(flops=2_000_000_000, bytes_accessed=0, transcendentals=0),
+        aliases={0: 0, 1: 1},
+    )(own_canvas, own_start, first, second, first_other, second_other)
+    mine, links, scale, begin, coupling, begin_near = call(
+        margins_kernel,
         [
-            (canvas, f32),
-            ((total, frames), f32),
             ((height // 2, 2 * slots, 2 * LANES), bf16),
             ((4 * group, LANES), f32),
             ((2 * slots, frames), f32),
@@ -601,11 +618,10 @@
             ((2 * slots, frames), f32),
             ((4 * group, frames), f32),
         ],
-        painting(4),
-        8,
-        cost=pl.CostEstimate(flops=3_000_000_000, bytes_accessed=0, transcendentals=0),
-        aliases={0: 0, 1: 1},
-    )(own_canvas, own_start, first, second, first_other, second_other)
+        [],
+        4,
+        cost=pl.CostEstimate(flops=1_500_000_000, bytes_accessed=0, transcendentals=0),
+    )(painted, start)
     near, across, cross, level = call(
         drive_kernel,
         [((rows * group, frames), f32) for rows in (5, 5, 4, 4)],

time: 33 us -> 32.9 us (level)
    pallas_call x5 -> x6, Pallas kernels: 8.86 us -> 8.73 us  [run(): pl.pallas_call(kernel, out_shape=[jax.ShapeDtypeStruct(*out) for out in o...]
where the time goes in v7:
time: 32.9 us; the launch traced here: 32.7 us
  starting transfers between devices  17.3 us (53%)
  Pallas kernels  8.73 us (27%)
  waiting for transfers between devices  5.91 us (18%)
  between operations  0.75 us (2%)
    ppermute x8, starting transfers between devices, swap(): return lax.ppermute(x, 'ty', [(0, 1), (1, 0)])  9.46 us
    pallas_call x6, Pallas kernels, run(): pl.pallas_call(kernel, out_shape=[jax.ShapeDtypeStruct(*out) for out in o...  8.73 us
    ppermute x3, waiting for transfers between devices, beside(): return lax.ppermute(x, ('ty', 'tx'), list(zip(ring, ring[1:] + ring[:1])))  5.03 us
    ppermute x3, starting transfers between devices, pairwise(): return lax.ppermute(x, ('ty', 'tx'), pairs)  4.23 us
    ppermute x3, starting transfers between devices, beside(): return lax.ppermute(x, ('ty', 'tx'), list(zip(ring, ring[1:] + ring[:1])))  3.57 us
    ppermute x8, waiting for transfers between devices, swap(): return lax.ppermute(x, 'ty', [(0, 1), (1, 0)])  0.88 us
  transfers between devices with their start and end apart: 14, of which 2 were waited for; matrix products, arithmetic and copies ran while one was open for 0% of the time, Pallas kernels for 21%

profile of v7, /device:TPU:7, one launch (start us, length us, event | category | flops | bytes accessed | tf_op | source)
XLA Modules:
  0.0 32.7 jit_solution(2634567699418586626)
XLA Ops:
  0.0 0.7 %collective-permute-start.5 = (bf16[32,32,128]{2,1,0:T(8,128)(2,1)}, bf16[32,32,128]{2,1,0:T(8,128)(2,1)S(1)}, u32[]{:S(2)}, u32[]{:S(2)}) collective-permute-start(bf16[32,32,128]{2,1,0:T(8,128)(2,1)} %movie.1), channel_id=1, source_target_pairs={{0,16},{16,0},{1,17},{17,1},{2,18},{18,2},{3,19},{19,3},{4,20},{20... | collective-permute-start | bytes 786440 | tf_op jit(solution)/shard_map/ppermute | solution.py:151
  1.3 1.1 %shard_map.64 = (bf16[32,1280]{1,0:T(8,128)(2,1)S(1)}, s32[1,32]{1,0:T(1,128)S(1)}, bf16[32,32,128]{2,1,0:T(8,128)(2,1)S(1)}) custom-call(s32[1,1]{1,0:T(1,128)S(6)} %copy.11.counts, bf16[32,1024]{1,0:T(8,128)(2,1)} %bitcast.7, bf16[32,128]{1,0:T(8,128)(2,1)} %bitcast.8, s32[1,32]{1,0:T(1,128)} %bitcast.10, s32[2,32]{1,0:T(2,128)} %bitcast.9, ...), custom_call_target="tpu_custom_call" | custom-call | tf_op jit(solution)/shard_map/pallas_call | solution.py:532
  2.4 0.0 collective-permute-done.5.film_pair
  2.5 0.3 collective-permute-start.6
  2.8 1.2 %collective-permute-start.1 = (bf16[32,1280]{1,0:T(8,128)(2,1)S(1)}, bf16[32,1280]{1,0:T(8,128)(2,1)S(1)}, u32[]{:S(2)}, u32[]{:S(2)}) collective-permute-start(bf16[32,1280]{1,0:T(8,128)(2,1)S(1)} %get-tuple-element.22.own), channel_id=1, source_target_pairs={{0,1},{1,2},{2,3},{3,4},{4,5},{5,6},{6,7},{7,8},{8,9},{9,10},{10,1... | collective-permute-start | bytes 245768 | tf_op jit(solution)/shard_map/ppermute | solution.py:158
  4.0 2.1 %collective-permute-start.2 = (bf16[32,1280]{1,0:T(8,128)(2,1)S(1)}, bf16[32,1280]{1,0:T(8,128)(2,1)S(1)}, u32[]{:S(2)}, u32[]{:S(2)}) collective-permute-start(bf16[32,1280]{1,0:T(8,128)(2,1)S(1)} %get-tuple-element.22.own), channel_id=1, source_target_pairs={{16,17},{17,18},{18,19},{19,20},{20,21},{21,22},{22,23},{23,24},{2... | collective-permute-start | bytes 245768 | tf_op jit(solution)/shard_map/ppermute | solution.py:158
  6.1 0.0 collective-permute-start
  6.1 5.0 %collective-permute-done.1.first = bf16[32,1280]{1,0:T(8,128)(2,1)S(1)} collective-permute-done((bf16[32,1280]{1,0:T(8,128)(2,1)S(1)}, bf16[32,1280]{1,0:T(8,128)(2,1)S(1)}, u32[]{:S(2)}, u32[]{:S(2)}) %collective-permute-start.1) | collective-permute-done | bytes 81952 | tf_op jit(solution)/shard_map/ppermute | solution.py:158
  11.1 2.4 %collective-permute-start.3 = (bf16[32,1280]{1,0:T(8,128)(2,1)S(1)}, bf16[32,1280]{1,0:T(8,128)(2,1)S(1)}, u32[]{:S(2)}, u32[]{:S(2)}) collective-permute-start(bf16[32,1280]{1,0:T(8,128)(2,1)S(1)} %collective-permute-done.1.first), channel_id=1, source_target_pairs={{0,16},{16,0},{1,17},{17,1},{2,18},{18,2},{3,19},{19,3},{4,20},{20... | collective-permute-start | bytes 245768 | tf_op jit(solution)/shard_map/ppermute | solution.py:151
  13.5 0.0 collective-permute-done.2.second
  13.5 0.0 collective-permute-start.4
  13.5 0.0 collective-permute-done.pair
  13.5 2.2 %shard_map.65 = (f32[9216,128]{1,0:T(8,128)S(1)}, f32[192,128]{1,0:T(8,128)S(1)}) custom-call(bf16[32,1280]{1,0:T(8,128)(2,1)S(1)} %get-tuple-element.22.own, bf16[32,1280]{1,0:T(8,128)(2,1)S(1)} %collective-permute-done.pair), custom_call_target="tpu_custom_call" | custom-call | flops 1500000000 | tf_op jit(solution)/shard_map/pallas_call | solution.py:532
  15.8 0.0 collective-permute-done.6.film_direct
  15.8 0.6 %collective-permute-start.7 = (bf16[64,16,128]{2,1,0:T(8,128)(2,1)S(1)}, bf16[64,16,128]{2,1,0:T(8,128)(2,1)S(1)}, u32[]{:S(2)}, u32[]{:S(2)}) collective-permute-start(bf16[64,16,128]{2,1,0:T(8,128)(2,1)S(1)} %collective-permute-done.6.film_direct), channel_id=1, source_target_pairs={{0,16},{16,0},{1,17},{17,1},{2,18},{18,2},{3,19},{19,3},{4,20},{20... | collective-permute-start | bytes 786440 | tf_op jit(solution)/shard_map/ppermute | solution.py:151
  16.3 0.0 collective-permute-done.3.first_other
  16.3 0.0 collective-permute-done.4.second_other
  16.3 2.5 %shard_map.66 = (f32[9216,128]{1,0:T(8,128)S(1)}, f32[192,128]{1,0:T(8,128)S(1)}) custom-call(f32[9216,128]{1,0:T(8,128)S(1)} %get-tuple-element.23.canvas_own, f32[192,128]{1,0:T(8,128)S(1)} %get-tuple-element.24.start_own, bf16[32,1280]{1,0:T(8,128)(2,1)S(1)} %collective-permute-done.1.first, ...), custom_call_target="tpu_custom_call", output_to_operand_aliasing={{0}: (0, {}), {1}: (1, {})} | custom-call | flops 2000000000 | tf_op jit(solution)/shard_map/pallas_call | solution.py:532
  18.8 1.1 %shard_map.67 = (bf16[16,64,256]{2,1,0:T(8,128)(2,1)S(1)}, f32[64,128]{1,0:T(8,128)S(1)}, f32[64,128]{1,0:T(8,128)S(1)}, f32[64,128]{1,0:T(8,128)S(1)}, f32[64,128]{1,0:T(8,128)S(1)}, /*index=5*/f32[64,128]{1,0:T(8,128)S(1)}) custom-call(f32[9216,128]{1,0:T(8,128)S(1)} %get-tuple-element.25.canvas, f32[192,128]{1,0:T(8,128)S(1)} %get-tuple-element.26.start), custom_call_target="tpu_custom_call" | custom-call | flops 1500000000 | tf_op jit(solution)/shard_map/pallas_call | solution.py:532
  19.9 0.0 collective-permute-done.7.film_other
  19.9 0.5 %shard_map.68 = (f32[80,128]{1,0:T(8,128)S(1)}, f32[80,128]{1,0:T(8,128)S(1)}, f32[64,128]{1,0:T(8,128)S(1)}, f32[64,128]{1,0:T(8,128)S(1)}) custom-call(bf16[16,64,256]{2,1,0:T(8,128)(2,1)S(1)} %get-tuple-element.27.mine, f32[64,128]{1,0:T(8,128)S(1)} %get-tuple-element.28.links, f32[64,128]{1,0:T(8,128)S(1)} %get-tuple-element.29.scale, ...), custom_call_target="tpu_custom_call" | custom-call | tf_op jit(solution)/shard_map/pallas_call | solution.py:532
  20.5 0.8 %collective-permute-start.10 = (f32[80,128]{1,0:T(8,128)S(1)}, f32[80,128]{1,0:T(8,128)S(1)}, u32[]{:S(2)}, u32[]{:S(2)}) collective-permute-start(f32[80,128]{1,0:T(8,128)S(1)} %get-tuple-element.36), channel_id=1, source_target_pairs={{2,5},{3,4},{4,3},{5,2},{6,9},{7,8},{8,7},{9,6},{10,13},{11,12},{1... | collective-permute-start | bytes 122888 | tf_op jit(solution)/shard_map/ppermute | solution.py:173
  21.3 1.2 %collective-permute-start.8 = (f32[80,128]{1,0:T(8,128)S(1)}, f32[80,128]{1,0:T(8,128)S(1)}, u32[]{:S(2)}, u32[]{:S(2)}) collective-permute-start(f32[80,128]{1,0:T(8,128)S(1)} %get-tuple-element.35), channel_id=1, source_target_pairs={{0,1},{1,0},{2,3},{3,2},{4,5},{5,4},{6,7},{7,6},{8,9},{9,8},{10,11... | collective-permute-start | bytes 122888 | tf_op jit(solution)/shard_map/ppermute | solution.py:173
  22.5 2.2 %collective-permute-start.12 = (f32[64,128]{1,0:T(8,128)S(1)}, f32[64,128]{1,0:T(8,128)S(1)}, u32[]{:S(2)}, u32[]{:S(2)}) collective-permute-start(f32[64,128]{1,0:T(8,128)S(1)} %get-tuple-element.37), channel_id=1, source_target_pairs={{2,4},{3,5},{4,2},{5,3},{6,8},{7,9},{8,6},{9,7},{10,12},{11,13},{1... | collective-permute-start | bytes 98312 | tf_op jit(solution)/shard_map/ppermute | solution.py:173
  24.7 0.0 collective-permute-done.10.across_direct
  24.7 1.7 %collective-permute-start.11 = (f32[80,128]{1,0:T(8,128)S(1)}, f32[80,128]{1,0:T(8,128)S(1)}, u32[]{:S(2)}, u32[]{:S(2)}) collective-permute-start(f32[80,128]{1,0:T(8,128)S(1)} %collective-permute-done.10.across_direct), channel_id=1, source_target_pairs={{0,16},{16,0},{1,17},{17,1},{2,18},{18,2},{3,19},{19,3},{4,20},{20... | collective-permute-start | bytes 122888 | tf_op jit(solution)/shard_map/ppermute | solution.py:151
  26.4 0.0 collective-permute-done.8.near_direct
  26.4 1.3 %collective-permute-start.9 = (f32[80,128]{1,0:T(8,128)S(1)}, f32[80,128]{1,0:T(8,128)S(1)}, u32[]{:S(2)}, u32[]{:S(2)}) collective-permute-start(f32[80,128]{1,0:T(8,128)S(1)} %collective-permute-done.8.near_direct), channel_id=1, source_target_pairs={{0,16},{16,0},{1,17},{17,1},{2,18},{18,2},{3,19},{19,3},{4,20},{20... | collective-permute-start | bytes 122888 | tf_op jit(solution)/shard_map/ppermute | solution.py:151
  27.7 0.0 collective-permute-done.12.cross_direct
  27.7 2.8 %collective-permute-start.13 = (f32[64,128]{1,0:T(8,128)S(1)}, f32[64,128]{1,0:T(8,128)S(1)}, u32[]{:S(2)}, u32[]{:S(2)}) collective-permute-start(f32[64,128]{1,0:T(8,128)S(1)} %collective-permute-done.12.cross_direct), channel_id=1, source_target_pairs={{0,16},{16,0},{1,17},{17,1},{2,18},{18,2},{3,19},{19,3},{4,20},{20... | collective-permute-start | bytes 98312 | tf_op jit(solution)/shard_map/ppermute | solution.py:151
  30.5 0.9 %collective-permute-done.13.cross_other = f32[64,128]{1,0:T(8,128)S(1)} collective-permute-done((f32[64,128]{1,0:T(8,128)S(1)}, f32[64,128]{1,0:T(8,128)S(1)}, u32[]{:S(2)}, u32[]{:S(2)}) %collective-permute-start.13) | collective-permute-done | bytes 32800 | tf_op jit(solution)/shard_map/ppermute | solution.py:151
  31.3 0.0 collective-permute-done.11.across_other
  31.4 0.0 collective-permute-done.9.near_other
  31.4 1.4 %shard_map.69 = f32[32,128]{1,0:T(8,128)} custom-call(f32[64,128]{1,0:T(8,128)S(1)} %get-tuple-element.33.level, f32[64,128]{1,0:T(8,128)S(1)} %get-tuple-element.30.begin, f32[64,128]{1,0:T(8,128)S(1)} %get-tuple-element.28.links, f32[64,128]{1,0:T(8,128)S(1)} %get-tuple-element.34.begin_near, f32[80,128]{1,0:T(8,128)S(1)} %collective-permute-done.8.near_direct, ...), custom_call_target="tpu_custom_call" | custom-call | tf_op jit(solution)/shard_map/pallas_call | solution.py:532
  (3 shorter events, 0.1 us)
Async XLA Ops:
  0.0 2.5 %collective-permute-start.5 = (bf16[32,32,128]{2,1,0:T(8,128)(2,1)}, bf16[32,32,128]{2,1,0:T(8,128)(2,1)S(1)}, u32[]{:S(2)}, u32[]{:S(2)}) collective-permute-start(bf16[32,32,128]{2,1,0:T(8,128)(2,1)} %movie.1), channel_id=1, source_target_pairs={{0,16},{16,0},{1,17},{17,1},{2,18},{18,2},{3,19},{19,3},{4,20},{20... | collective-permute-start | bytes 786440 | tf_op jit(solution)/shard_map/ppermute | solution.py:151
  2.5 13.2 %collective-permute-start.6 = (bf16[64,16,128]{2,1,0:T(8,128)(2,1)S(1)}, bf16[64,16,128]{2,1,0:T(8,128)(2,1)S(1)}, u32[]{:S(2)}, u32[]{:S(2)}) collective-permute-start(bf16[64,16,128]{2,1,0:T(8,128)(2,1)S(1)} %pad_maximum_fusion), channel_id=1, source_target_pairs={{0,1},{1,2},{2,3},{3,4},{4,5},{5,6},{6,7},{7,8},{8,9},{9,10},{10,1... | collective-permute-start | bytes 786440 | tf_op jit(solution)/shard_map/ppermute | solution.py:158
  2.8 8.3 %collective-permute-start.1 = (bf16[32,1280]{1,0:T(8,128)(2,1)S(1)}, bf16[32,1280]{1,0:T(8,128)(2,1)S(1)}, u32[]{:S(2)}, u32[]{:S(2)}) collective-permute-start(bf16[32,1280]{1,0:T(8,128)(2,1)S(1)} %get-tuple-element.22.own), channel_id=1, source_target_pairs={{0,1},{1,2},{2,3},{3,4},{4,5},{5,6},{6,7},{7,8},{8,9},{9,10},{10,1... | collective-permute-start | bytes 245768 | tf_op jit(solution)/shard_map/ppermute | solution.py:158
  4.0 9.6 %collective-permute-start.2 = (bf16[32,1280]{1,0:T(8,128)(2,1)S(1)}, bf16[32,1280]{1,0:T(8,128)(2,1)S(1)}, u32[]{:S(2)}, u32[]{:S(2)}) collective-permute-start(bf16[32,1280]{1,0:T(8,128)(2,1)S(1)} %get-tuple-element.22.own), channel_id=1, source_target_pairs={{16,17},{17,18},{18,19},{19,20},{20,21},{21,22},{22,23},{23,24},{2... | collective-permute-start | bytes 245768 | tf_op jit(solution)/shard_map/ppermute | solution.py:158
  6.1 7.5 %collective-permute-start = (bf16[32,1280]{1,0:T(8,128)(2,1)S(1)}, bf16[32,1280]{1,0:T(8,128)(2,1)S(1)}, u32[]{:S(2)}, u32[]{:S(2)}) collective-permute-start(bf16[32,1280]{1,0:T(8,128)(2,1)S(1)} %get-tuple-element.22.own), channel_id=1, source_target_pairs={{0,16},{16,0},{1,17},{17,1},{2,18},{18,2},{3,19},{19,3},{4,20},{20... | collective-permute-start | bytes 245768 | tf_op jit(solution)/shard_map/ppermute | solution.py:151
  11.1 5.2 %collective-permute-start.3 = (bf16[32,1280]{1,0:T(8,128)(2,1)S(1)}, bf16[32,1280]{1,0:T(8,128)(2,1)S(1)}, u32[]{:S(2)}, u32[]{:S(2)}) collective-permute-start(bf16[32,1280]{1,0:T(8,128)(2,1)S(1)} %collective-permute-done.1.first), channel_id=1, source_target_pairs={{0,16},{16,0},{1,17},{17,1},{2,18},{18,2},{3,19},{19,3},{4,20},{20... | collective-permute-start | bytes 245768 | tf_op jit(solution)/shard_map/ppermute | solution.py:151
  13.5 2.8 %collective-permute-start.4 = (bf16[32,1280]{1,0:T(8,128)(2,1)S(1)}, bf16[32,1280]{1,0:T(8,128)(2,1)S(1)}, u32[]{:S(2)}, u32[]{:S(2)}) collective-permute-start(bf16[32,1280]{1,0:T(8,128)(2,1)S(1)} %collective-permute-done.2.second), channel_id=1, source_target_pairs={{0,16},{16,0},{1,17},{17,1},{2,18},{18,2},{3,19},{19,3},{4,20},{20... | collective-permute-start | bytes 245768 | tf_op jit(solution)/shard_map/ppermute | solution.py:151
  15.8 4.2 %collective-permute-start.7 = (bf16[64,16,128]{2,1,0:T(8,128)(2,1)S(1)}, bf16[64,16,128]{2,1,0:T(8,128)(2,1)S(1)}, u32[]{:S(2)}, u32[]{:S(2)}) collective-permute-start(bf16[64,16,128]{2,1,0:T(8,128)(2,1)S(1)} %collective-permute-done.6.film_direct), channel_id=1, source_target_pairs={{0,16},{16,0},{1,17},{17,1},{2,18},{18,2},{3,19},{19,3},{4,20},{20... | collective-permute-start | bytes 786440 | tf_op jit(solution)/shard_map/ppermute | solution.py:151
  20.5 4.2 %collective-permute-start.10 = (f32[80,128]{1,0:T(8,128)S(1)}, f32[80,128]{1,0:T(8,128)S(1)}, u32[]{:S(2)}, u32[]{:S(2)}) collective-permute-start(f32[80,128]{1,0:T(8,128)S(1)} %get-tuple-element.36), channel_id=1, source_target_pairs={{2,5},{3,4},{4,3},{5,2},{6,9},{7,8},{8,7},{9,6},{10,13},{11,12},{1... | collective-permute-start | bytes 122888 | tf_op jit(solution)/shard_map/ppermute | solution.py:173
  21.3 5.1 %collective-permute-start.8 = (f32[80,128]{1,0:T(8,128)S(1)}, f32[80,128]{1,0:T(8,128)S(1)}, u32[]{:S(2)}, u32[]{:S(2)}) collective-permute-start(f32[80,128]{1,0:T(8,128)S(1)} %get-tuple-element.35), channel_id=1, source_target_pairs={{0,1},{1,0},{2,3},{3,2},{4,5},{5,4},{6,7},{7,6},{8,9},{9,8},{10,11... | collective-permute-start | bytes 122888 | tf_op jit(solution)/shard_map/ppermute | solution.py:173
  22.5 5.1 %collective-permute-start.12 = (f32[64,128]{1,0:T(8,128)S(1)}, f32[64,128]{1,0:T(8,128)S(1)}, u32[]{:S(2)}, u32[]{:S(2)}) collective-permute-start(f32[64,128]{1,0:T(8,128)S(1)} %get-tuple-element.37), channel_id=1, source_target_pairs={{2,4},{3,5},{4,2},{5,3},{6,8},{7,9},{8,6},{9,7},{10,12},{11,13},{1... | collective-permute-start | bytes 98312 | tf_op jit(solution)/shard_map/ppermute | solution.py:173
  24.7 6.7 %collective-permute-start.11 = (f32[80,128]{1,0:T(8,128)S(1)}, f32[80,128]{1,0:T(8,128)S(1)}, u32[]{:S(2)}, u32[]{:S(2)}) collective-permute-start(f32[80,128]{1,0:T(8,128)S(1)} %collective-permute-done.10.across_direct), channel_id=1, source_target_pairs={{0,16},{16,0},{1,17},{17,1},{2,18},{18,2},{3,19},{19,3},{4,20},{20... | collective-permute-start | bytes 122888 | tf_op jit(solution)/shard_map/ppermute | solution.py:151
  26.4 5.0 %collective-permute-start.9 = (f32[80,128]{1,0:T(8,128)S(1)}, f32[80,128]{1,0:T(8,128)S(1)}, u32[]{:S(2)}, u32[]{:S(2)}) collective-permute-start(f32[80,128]{1,0:T(8,128)S(1)} %collective-permute-done.8.near_direct), channel_id=1, source_target_pairs={{0,16},{16,0},{1,17},{17,1},{2,18},{18,2},{3,19},{19,3},{4,20},{20... | collective-permute-start | bytes 122888 | tf_op jit(solution)/shard_map/ppermute | solution.py:151
  27.7 3.7 %collective-permute-start.13 = (f32[64,128]{1,0:T(8,128)S(1)}, f32[64,128]{1,0:T(8,128)S(1)}, u32[]{:S(2)}, u32[]{:S(2)}) collective-permute-start(f32[64,128]{1,0:T(8,128)S(1)} %collective-permute-done.12.cross_direct), channel_id=1, source_target_pairs={{0,16},{16,0},{1,17},{17,1},{2,18},{18,2},{3,19},{19,3},{4,20},{20... | collective-permute-start | bytes 98312 | tf_op jit(solution)/shard_map/ppermute | solution.py:151
